TPU v7x, 32 devices: a whole 2x2x4 slice. The times are simulated.
32 devices in a mesh: mic: 2 (over x), tile: 16 (over z, y, core).
Axes of the slice: x: 2, y: 2, z: 4, core: 2. Of those that a mesh axis runs over, the one named last changes fastest.
Arguments:
- micrograph: bfloat16 [32, 384, 384], P(('mic', 'tile')), parts along dimension 0, may hold values from -6 to 6
- templates: bfloat16 [16, 128, 128], P('tile'), may hold values from -0.046875 to 0.046875
- orient_list: int32 [32, 4], P('mic'), parts along dimension 0, may hold values from 0 to 15
- lengths: int32 [32], P('mic'), parts along dimension 0, may hold values from 1 to 4, 32 in all
- defocus: float32 [32], P('mic'), parts along dimension 0, may hold values from 8000 to 25000
Outputs:
- snr_map: float32 [32, 384, 384], P(('mic', 'tile')), parts along dimension 0
- mean_map: float32 [32, 384, 384], P(('mic', 'tile')), parts along dimension 0
- var_map: float32 [32, 384, 384], P(('mic', 'tile')), parts along dimension 0
There are 2 independent parts, one for each index of `mic`. A program takes and returns all parts, laid end to end along the dimension named above; an argument that names none is the same for every part. Nothing has to cross between parts.
Inputs may be any that keep to these rules, and one draw needn't show every extreme that they name: `orient_list`: orientation numbers; a tile's list may name one orientation more than once. The lengths of all tiles of a micrograph sum to 32.
All inputs are finite; a program needn't handle non-finite values.
Results may differ from a plain program's by a relative error of at most 0.0098.
Values may be sent and summed in bfloat16 or wider, within the bound.
No kernel may reach another device: no remote copies, remote signals or barrier semaphores. Data moves between devices by JAX's collectives and lax.ppermute only.
A program may use at most 64 MiB of HBM per device.

v0:
```python
import functools
import math

import jax
import jax.numpy as jnp
import numpy as np
from jax import lax
from jax.experimental import pallas as pl
from jax.experimental.pallas import tpu as pltpu
from jax.sharding import PartitionSpec as P


GRID = 8
LMAX = 4

wave_length = 0.0197
spherical = 27000000.0
contrast = 0.07
var_floor = 0.1


def wave_tables(index, position, extent):
    product = index[:, None] * position[None, :] % extent
    angle = product * (2.0 * math.pi / extent)
    nyquist = 1.0 - 2.0 * (position[None, :] % 2)
    return np.cos(angle), np.where(index[:, None] == 0, nyquist, np.sin(angle))


def make_tables(extent, box):
    half = extent // 2
    position = np.arange(half)
    even, odd = position[::2], position[1::2]
    tables = []
    for index in (even, odd):
        cosine, sine = wave_tables(index, position, extent)
        tables.append(np.concatenate([cosine, sine], axis=0).T)
    tables += [table.T for table in tables]
    for index in (even, odd):
        cosine, sine = wave_tables(index, position, extent)
        tables.append(np.concatenate([cosine, np.where(index[:, None] == 0, sine, -sine)], axis=0))
    order = np.concatenate([even, odd])
    centred = np.arange(box) - box // 2
    cosine, sine = wave_tables(order, centred, extent)
    tables.append(np.concatenate([cosine, sine], axis=0).T)
    first = order[:, None] == 0
    plain = np.where(first, 0.0, sine)
    nyquist, zero = sine[:1] + 0 * sine, 0 * sine
    tables.append(
        np.concatenate(
            [
                np.concatenate([cosine, -plain], axis=1),
                np.concatenate([-plain, -cosine], axis=1),
                np.where(first, np.concatenate([nyquist, zero], axis=1), np.concatenate([cosine, plain], axis=1)),
                np.where(first, np.concatenate([zero, -nyquist], axis=1), np.concatenate([plain, -cosine], axis=1)),
            ],
            axis=0,
        )
    )
    return [jnp.asarray(table, jnp.bfloat16) for table in tables]


def sine_of_turns(turns):
    part = turns - jnp.round(turns)
    folded = jnp.where(jnp.abs(part) > 0.25, jnp.where(part > 0, 0.5, -0.5) - part, part)
    angle = folded * (2.0 * math.pi)
    square = angle * angle
    series = -1.0 / 39916800.0
    for factor in (362880.0, -5040.0, 120.0, -6.0, 1.0):
        series = series * square + 1.0 / factor
    return angle * series


def transfer(row, column, focus_value, extent):
    radius = (row * row + column * column) * (1.0 / (extent * extent))
    turns = (0.5 * wave_length) * focus_value * radius - (
        0.25 * spherical * wave_length**3
    ) * radius * radius
    return -sine_of_turns(turns + math.asin(contrast) / (2.0 * math.pi))


def flips(tile_count):
    if tile_count == 2 * GRID:
        return [GRID, 2, 4, 1]
    return [1 << k for k in reversed(range(tile_count.bit_length() - 1))]


def dot(left, right):
    return jnp.dot(left, right, preferred_element_type=jnp.float32)


def swap_halves(block, lanes):
    return pltpu.roll(block, lanes, 1)


def early_kernel(defocus, centre_ref, weight_ref, mate_ref, peer_ref):
    me = lax.axis_index("tile")
    focus_value = defocus[me]
    lane = weight_ref.shape[1] // 2
    extent = 4 * lane
    edge = float(2 * lane)
    scale = 2.0 / (extent * extent)
    i = lax.broadcasted_iota(jnp.int32, (lane, lane), 0)
    j = lax.broadcasted_iota(jnp.int32, (lane, lane), 1)
    for row_odd in range(2):
        for col_odd in range(2):
            row = (2 * i + row_odd).astype(jnp.float32)
            col = (2 * j + col_odd).astype(jnp.float32)
            rows = slice(row_odd * lane, (row_odd + 1) * lane)
            cols = slice(col_odd * lane, (col_odd + 1) * lane)
            if row_odd and col_odd:
                value = scale * transfer(row, col, focus_value, extent)
                parts = (value,) * 4
            elif row_odd or col_odd:
                value = scale * transfer(row, col, focus_value, extent)
                if row_odd:
                    other = transfer(row, jnp.where(j == 0, edge, col), focus_value, extent)
                else:
                    other = transfer(jnp.where(i == 0, edge, row), col, focus_value, extent)
                other = scale * other
                parts = (value, value, other, other)
            else:
                col_first = j == 0
                corner = col_first & (i == 0)
                row_first = (i == 0) & (j != 0)
                row_minus = jnp.where(row_first, edge, row)
                col_minus = jnp.where(col_first, edge, col)
                at_corner = jnp.where(corner, 0.5 * scale, scale)
                parts = (
                    at_corner * transfer(row, col, focus_value, extent),
                    at_corner * transfer(jnp.where(corner, edge, row), col, focus_value, extent),
                    at_corner * transfer(row_minus, col_minus, focus_value, extent),
                    at_corner * transfer(jnp.where(corner, edge, row_minus), col_minus, focus_value, extent),
                )
            for k in range(4):
                weight_ref[k, rows, cols] = parts[k]
    centre = centre_ref.shape[0]
    half = centre // 2
    first = centre_ref[:, :lane].astype(jnp.float32)
    last = centre_ref[:, centre - lane :].astype(jnp.float32)
    low = lax.broadcasted_iota(jnp.int32, (half, lane), 1) < lane // 2
    first = jnp.where(low, first[:half], swap_halves(first[half:], lane // 2))
    last = jnp.where(low, swap_halves(last[:half], lane // 2), last[half:])
    odd = lax.rem(me, 2) == 1
    mate_ref[...] = jnp.where(odd, first, last).astype(jnp.bfloat16)
    peer_ref[...] = jnp.where(odd, last, first).astype(jnp.bfloat16)


def packed_sides(mate, peer, lane, start, stop, left_open, right_open):
    odd = lax.rem(lax.axis_index("tile"), 2) == 1
    mate = mate[start:stop].astype(jnp.float32)
    peer = peer[start:stop].astype(jnp.float32)
    right = jnp.where(right_open, jnp.where(odd, peer, mate), 0.0)
    left = jnp.where(left_open, jnp.where(odd, mate, peer), 0.0)
    low = lax.broadcasted_iota(jnp.int32, right.shape, 1) < lane // 2
    upper = jnp.where(low, right, swap_halves(left, lane // 2))
    lower = jnp.where(low, swap_halves(right, lane // 2), left)
    return jnp.concatenate([upper, lower], axis=0)


def tile_kernel(paired, *refs):
    if paired:
        centre_ref, mate_ref, peer_ref, ends_ref, weight_ref = refs[:5]
        refs = refs[5:]
    else:
        centre_ref, cols_ref, rows_ref, weight_ref = refs[:4]
        refs = refs[4:]
    fwd_e, fwd_o, fwd_et, fwd_ot, filt, uv = refs
    centre, extent = centre_ref.shape[0], uv.shape[0]
    half, lane = extent // 2, extent // 4
    if paired:
        place = lax.rem(lax.axis_index("tile") + GRID // 2, 2 * GRID)
        column, upper_row = lax.rem(place, GRID), place < GRID
        opens = (column != 0, column != GRID - 1)
        side = packed_sides(mate_ref, peer_ref, lane, 0, centre // 2, *opens)
        corners = packed_sides(mate_ref, peer_ref, lane, centre // 2, mate_ref.shape[0], *opens)
        ends = jnp.concatenate([ends_ref[...].astype(jnp.float32), corners], axis=1)
        rim = jnp.concatenate([jnp.where(upper_row, ends, 0.0), jnp.where(upper_row, 0.0, ends)], axis=0)
    else:
        side = cols_ref[...].astype(jnp.float32)
        rim = rows_ref[...].astype(jnp.float32)
    own = centre_ref[...].astype(jnp.float32)
    far = jnp.concatenate([own[:, half:], side], axis=1)
    near = own[:, :half]
    uv[:centre, :half] = dot((near + far).astype(jnp.bfloat16), fwd_e[...])
    uv[:centre, half:] = dot((near - far).astype(jnp.bfloat16), fwd_o[...])
    near, far = rim[:, :half], rim[:, half:]
    uv[centre:, :half] = dot((near + far).astype(jnp.bfloat16), fwd_e[...])
    uv[centre:, half:] = dot((near - far).astype(jnp.bfloat16), fwd_o[...])
    near, far = uv[:half, :], uv[half:, :]
    spectra = (
        dot(fwd_et[...], (near + far).astype(jnp.bfloat16)),
        dot(fwd_ot[...], (near - far).astype(jnp.bfloat16)),
    )
    i = lax.broadcasted_iota(jnp.int32, (lane, lane), 0)
    j = lax.broadcasted_iota(jnp.int32, (lane, lane), 1)
    for row_odd in range(2):
        for col_odd in range(2):
            block = spectra[row_odd]
            left, right = block[:lane], block[lane:]
            u, v = 2 * col_odd * lane, (2 * col_odd + 1) * lane
            uc, vc, us, vs = left[:, u : u + lane], left[:, v : v + lane], right[:, u : u + lane], right[:, v : v + lane]
            parts = [uc - vs, -(us + vc), uc + vs, us - vc]
            if not row_odd:
                row_first = i == 0
                parts = [jnp.where(row_first, a, b) for a, b in zip((uc, -vc, us, -vs), parts)]
            if not col_odd:
                col_first = j == 0
                parts = [jnp.where(col_first, a, b) for a, b in zip((uc, -us, vc, vs), parts)]
            rows = slice(row_odd * lane, (row_odd + 1) * lane)
            cols = slice(col_odd * lane, (col_odd + 1) * lane)
            for k in range(4):
                filt[k, rows, cols] = weight_ref[k, rows, cols] * parts[k]


def match_kernel(
    orients, lengths, filt, near_ref, far_ref,
    fwd_e, fwd_o, inv_e, inv_o, temp_rows, temp_cols,
    snr_ref, mean_ref, var_ref,
    proj, mixed, combo_e, combo_o, out_buf, out_sem,
):
    me = lax.axis_index("tile")
    half = filt.shape[1]
    lane, extent = half // 2, 2 * half
    centre = out_buf.shape[1]
    tile_count = lax.axis_size("tile")
    distances = flips(tile_count)
    held = near_ref.shape[0] // (tile_count // 2)

    def chosen(slot):
        orient = jnp.clip(orients[slot, me], 0, 2 * near_ref.shape[0] - 1)
        apart = lax.div(orient, held) ^ me
        at = lax.rem(orient, held)
        for k, distance in enumerate(distances[:-1]):
            at = at + (lax.div(apart, distance) & 1) * (held << k)
        return jnp.where(apart & 1 == 1, far_ref[at], near_ref[at])

    step = 16
    lane_col = lax.broadcasted_iota(jnp.int32, (step, lane), 1) == 0
    first_row = lax.broadcasted_iota(jnp.int32, (step, lane), 0) == 0
    corner = lane_col & first_row
    box = near_ref.shape[1]
    sign = 1.0 - 2.0 * (lax.broadcasted_iota(jnp.int32, (box, lane), 0) % 2).astype(jnp.float32)
    box_col = lax.broadcasted_iota(jnp.int32, (box, lane), 1) == 0
    for slot in range(LMAX):
        waves = dot(chosen(slot), temp_rows[...])
        first_u, first_v = waves[:, :lane], waves[:, half : half + lane]
        row_edge = -jnp.sum(first_u * sign, axis=0, keepdims=True)
        col_edge = jnp.sum(first_v, axis=0, keepdims=True)
        v_part = jnp.concatenate([jnp.where(box_col, 0.0, first_v), waves[:, half + lane :]], axis=1)
        u_minus = jnp.concatenate([jnp.where(box_col, first_v, first_u), waves[:, lane:half]], axis=1)
        plus = jnp.concatenate([waves[:, :half], v_part], axis=0).astype(jnp.bfloat16)
        minus = jnp.concatenate([u_minus, v_part], axis=0).astype(jnp.bfloat16)
        proj[: 2 * half] = dot(temp_cols[: 2 * half], plus)
        proj[2 * half :] = dot(temp_cols[2 * half :], minus)
        base = slot * extent
        for start in range(0, half, step):
            row_odd, at = start // lane, start % lane
            for col_odd in range(2):
                cols = slice(col_odd * lane, (col_odd + 1) * lane)
                fpr, fpi, fmr, fmi = (filt[k, start : start + step, cols] for k in range(4))
                ppr, ppi, pmr, pmi = (proj[k * half + start : k * half + start + step, cols] for k in range(4))
                if start == 0 and col_odd == 0:
                    ppi = jnp.where(corner, row_edge, ppi)
                    pmi = jnp.where(corner, pmr, pmi)
                    pmr = jnp.where(corner, col_edge, pmr)
                plus_r, plus_i = fpr * ppr + fpi * ppi, fpi * ppr - fpr * ppi
                minus_r, minus_i = fmr * pmr + fmi * pmi, fmi * pmr - fmr * pmi
                cos_r, sin_r = plus_r + minus_r, minus_i - plus_i
                cos_i, sin_i = plus_i + minus_i, plus_r - minus_r
                if start == 0:
                    cos_r = jnp.where(first_row, plus_r, cos_r)
                    sin_r = jnp.where(first_row, minus_r, sin_r)
                    cos_i = jnp.where(first_row, plus_i, cos_i)
                    sin_i = jnp.where(first_row, minus_i, sin_i)
                if col_odd == 0:
                    cos_r = jnp.where(lane_col, plus_r, cos_r)
                    sin_r = jnp.where(lane_col, -plus_i, sin_r)
                    cos_i = jnp.where(lane_col, minus_r, cos_i)
                    sin_i = jnp.where(lane_col, minus_i, sin_i)
                    if start == 0:
                        cos_r = jnp.where(corner, fpr * ppr, cos_r)
                        sin_r = jnp.where(corner, fpi * ppi, sin_r)
                        cos_i = jnp.where(corner, fmr * pmr, cos_i)
                        sin_i = jnp.where(corner, fmi * pmi, sin_i)
                at_r = slice(base + col_odd * lane, base + (col_odd + 1) * lane)
                at_i = slice(base + half + col_odd * lane, base + half + (col_odd + 1) * lane)
                mixed[row_odd, at : at + step, at_r] = cos_r.astype(jnp.bfloat16)
                mixed[row_odd, lane + at : lane + at + step, at_r] = sin_r.astype(jnp.bfloat16)
                mixed[row_odd, at : at + step, at_i] = cos_i.astype(jnp.bfloat16)
                mixed[row_odd, lane + at : lane + at + step, at_i] = sin_i.astype(jnp.bfloat16)
        even = dot(fwd_e[...], mixed[0, :, base : base + extent])
        odd = dot(fwd_o[...], mixed[1, :, base : base + extent])
        total = even + odd
        for part in range(centre // lane):
            if part * lane < half:
                value = total[part * lane : (part + 1) * lane]
            else:
                near = slice(part * lane - half, (part + 1) * lane - half)
                value = even[near] - odd[near]
            value = value.astype(jnp.bfloat16)
            here = slice(slot * lane, (slot + 1) * lane)
            combo_e[part, here, :lane] = value[:, :lane]
            combo_e[part, here, lane:] = value[:, half : half + lane]
            combo_o[part, here, :lane] = value[:, lane:half]
            combo_o[part, here, lane:] = value[:, half + lane :]

    count = lengths[me]
    inverse_count = 1.0 / jnp.full((1, 1), count, jnp.int32).astype(jnp.float32)
    out_copies = []
    for part in range(centre // lane):
        even = dot(combo_e[part], inv_e[...])
        odd = dot(combo_o[part], inv_o[...])
        best = total = squares = None
        for slot in range(LMAX):
            here = slice(slot * lane, (slot + 1) * lane)
            score = jnp.concatenate(
                [even[here] + odd[here], even[here, : centre - half] - odd[here, : centre - half]], axis=1
            )
            if slot == 0:
                best, total, squares = score, score, score * score
            else:
                taken = slot < count
                kept = jnp.where(taken, score, 0.0)
                best = jnp.maximum(best, jnp.where(taken, score, -jnp.inf))
                total = total + kept
                squares = squares + kept * kept
        mean = total * inverse_count
        variance = squares * inverse_count - mean * mean
        snr = (best - mean) * lax.rsqrt(jnp.maximum(variance, var_floor))
        rows = slice(part * lane, (part + 1) * lane)
        for k, (value, out) in enumerate(((snr, snr_ref), (mean, mean_ref), (variance, var_ref))):
            out_buf[k, rows] = value
            copy = pltpu.make_async_copy(out_buf.at[k, rows], out.at[0, rows], out_sem.at[k, part])
            copy.start()
            out_copies.append(copy)
    for copy in out_copies:
        copy.wait()


def vmem_call(kernel, inputs, outs, scratch, scalars, limit, out_spec=pltpu.VMEM, cost=None):
    smem = pl.BlockSpec(memory_space=pltpu.SMEM)
    vmem = pl.BlockSpec(memory_space=pltpu.VMEM)
    return pl.pallas_call(
        kernel,
        out_shape=tuple(jax.ShapeDtypeStruct(shape, dtype) for shape, dtype in outs),
        in_specs=[smem] * scalars + [vmem] * (len(inputs) - scalars),
        out_specs=tuple(pl.BlockSpec(memory_space=out_spec) for _ in outs),
        scratch_shapes=scratch,
        compiler_params=pltpu.CompilerParams(vmem_limit_bytes=limit << 20),
        cost_estimate=cost,
    )(*inputs)


def early(defocus, centre_block, extent):
    centre, half, lane = centre_block.shape[0], extent // 2, extent // 4
    strip = ((centre // 2, lane), jnp.bfloat16)
    return vmem_call(early_kernel, (defocus, centre_block), (((4, half, half), jnp.float32), strip, strip), [], 1, 8)


def tile_spectrum(paired, pieces, weights, tables, extent):
    half = extent // 2
    (filt,) = vmem_call(
        functools.partial(tile_kernel, paired), (*pieces, weights, *tables[:4]),
        (((4, half, half), jnp.float32),), [pltpu.VMEM((extent, extent), jnp.float32)], 0, 16,
    )
    return filt


def match(orient_list, lengths, filt, near, far, tables, centre):
    half = filt.shape[1]
    lane, extent = half // 2, 2 * half
    parts = centre // lane
    out = ((1, centre, centre), jnp.float32)
    return vmem_call(
        match_kernel, (orient_list, lengths, filt, near, far, *tables[:2], *tables[4:]), (out, out, out),
        [
            pltpu.VMEM((2 * extent, half), jnp.float32),
            pltpu.VMEM((2, half, LMAX * extent), jnp.bfloat16),
            pltpu.VMEM((parts, LMAX * lane, half), jnp.bfloat16),
            pltpu.VMEM((parts, LMAX * lane, half), jnp.bfloat16),
            pltpu.VMEM((3, centre, centre), jnp.float32),
            pltpu.SemaphoreType.DMA((3, parts)),
        ],
        2, 24, pl.ANY,
    )


def shards(micrograph, templates, orient_list, lengths, defocus):
    position = lax.axis_index("tile")
    tile_count = lax.axis_size("tile")
    centre_block = micrograph[0]
    centre = centre_block.shape[0]
    box = templates.shape[1]
    margin = box // 2
    extent = centre + box
    tile_rows = tile_count // GRID
    grid_place = (position + GRID // 2) % tile_count
    column, tile_row = grid_place % GRID, grid_place // GRID
    tables = make_tables(extent, box)

    def send(block, target):
        return lax.ppermute(block, "tile", [(i, target(i)) for i in range(tile_count)])

    paired = tile_rows == 2
    if paired:
        odd = position % 2 == 1
        lower_row = tile_row == tile_rows - 1
        distances = flips(tile_count)
        pair = send(templates, lambda i: i ^ distances[0])
        start = jnp.where(lower_row, 0, centre - margin)
        ends = send(lax.dynamic_slice_in_dim(centre_block, start, margin, 0), lambda i: i ^ GRID)
        weights, to_mate, to_peer = early(defocus, centre_block, extent)

        def strip(own, use_first):
            edge = jnp.where(use_first, ends[:, :margin], ends[:, centre - margin :])
            edge = jnp.concatenate([edge[: margin // 2], edge[margin // 2 :]], axis=1)
            return jnp.concatenate([own, edge], axis=0)

        two = jnp.concatenate([templates, pair], axis=0)
        group = [two]
        for apart in (distances[2] | distances[1], distances[1], distances[2]):
            group.append(send(two, lambda i, apart=apart: i ^ apart))
        from_peer = send(strip(to_peer, ~odd), lambda i: (i + 1 if i % 2 else i - 1) % tile_count)
        from_mate = send(strip(to_mate, odd), lambda i: i ^ 1)
        near = jnp.concatenate([group[0], group[2], group[3], group[1]], axis=0)
        far = send(near, lambda i: i ^ 1)
        filt = tile_spectrum(True, (centre_block, from_mate, from_peer, ends), weights, tables, extent)
    else:

        def arrive(block, distance):
            return lax.ppermute(
                block, "tile", [((i + distance) % tile_count, i) for i in range(tile_count)]
            )

        weights, _, _ = early(defocus, centre_block, extent)
        right = arrive(centre_block[:, :margin], 1)
        left = arrive(centre_block[:, centre - margin :], -1)
        right = jnp.where(column == GRID - 1, jnp.zeros_like(right), right)
        left = jnp.where(column == 0, jnp.zeros_like(left), left)
        cols = jnp.concatenate([right, left], axis=1)
        wide = jnp.concatenate([centre_block, cols], axis=1)
        below = arrive(wide[:margin], GRID)
        above = arrive(wide[centre - margin :], -GRID)
        below = jnp.where(tile_row == tile_rows - 1, jnp.zeros_like(below), below)
        above = jnp.where(tile_row == 0, jnp.zeros_like(above), above)
        rows = jnp.concatenate([below, above], axis=0)
        near = templates
        for distance in flips(tile_count)[:-1]:
            near = jnp.concatenate([near, send(near, lambda i, d=distance: i ^ d)], axis=0)
        far = send(near, lambda i: i ^ 1)
        filt = tile_spectrum(False, (centre_block, cols, rows), weights, tables, extent)
    return match(orient_list.T, lengths, filt, near, far, tables, centre)


def solution(mesh):
    return jax.shard_map(
        shards,
        mesh=mesh,
        in_specs=(
            P(("mic", "tile"), None, None),
            P("tile", None, None),
            P("mic", None),
            P("mic"),
            P("mic"),
        ),
        out_specs=(
            P(("mic", "tile"), None, None),
            P(("mic", "tile"), None, None),
            P(("mic", "tile"), None, None),
        ),
        check_vma=False,
    )
```

profile of v0, /device:TPU:0, one launch (start us, length us, event | category | flops | bytes accessed | tf_op | source)
XLA Modules:
  0.0 29.4 jit_solution(312221930798211694)
XLA Ops:
  0.6 4.1 %collective-permute-start.3 = (bf16[1,128,128]{2,1,0:T(8,128)(2,1)}, bf16[1,128,128]{2,1,0:T(8,128)(2,1)S(1)}, u32[]{:S(2)}, u32[]{:S(2)}) collective-permute-start(bf16[1,128,128]{2,1,0:T(8,128)(2,1)} %param.14), channel_id=1, source_target_pairs={{0,8},{1,9},{2,10},{3,11},{4,12},{5,13},{6,14},{7,15},{8,0},{9,1},... | collective-permute-start | bytes 98312 | tf_op jit(solution)/shard_map/ppermute | solution.py:402
  4.8 0.8 %dynamic-slice_bitcast_fusion = bf16[64,384]{1,0:T(8,128)(2,1)S(1)} fusion(bf16[1,384,384]{2,1,0:T(8,128)(2,1)} %param.13, s32[]{:T(128)S(6)} %select_n.38), kind=kLoop, calls=%fused_computation.2 | loop fusion | bytes 98308 | tf_op jit(solution)/shard_map/dynamic_slice | solution.py:411
  5.6 0.1 collective-permute-start
  5.7 0.6 %copy-done.11 = f32[16]{0:T(128)S(1)} copy-done((f32[16]{0:T(128)S(1)}, f32[16]{0:T(128)}, u32[]{:S(2)}) %copy-start.11) | copy-done | bytes 88
  6.3 1.0 %copy-done = bf16[1,384,384]{2,1,0:T(8,128)(2,1)S(1)} copy-done((bf16[1,384,384]{2,1,0:T(8,128)(2,1)S(1)}, bf16[1,384,384]{2,1,0:T(8,128)(2,1)}, u32[]{:S(2)}) %copy-start) | copy-done | bytes 294936
  7.3 1.1 %shard_map.148 = (f32[4,256,256]{2,1,0:T(8,128)S(1)}, bf16[192,128]{1,0:T(8,128)(2,1)S(1)}, bf16[192,128]{1,0:T(8,128)(2,1)S(1)}) custom-call(f32[16]{0:T(128)S(1)} %copy-done.11, bf16[384,384]{1,0:T(8,128)(2,1)S(1)} %bitcast.4), custom_call_target="tpu_custom_call" | custom-call | tf_op jit(solution)/shard_map/pallas_call | solution.py:343
  8.4 2.9 %collective-permute-start.6 = (bf16[2,128,128]{2,1,0:T(8,128)(2,1)S(1)}, bf16[2,128,128]{2,1,0:T(8,128)(2,1)S(1)}, u32[]{:S(2)}, u32[]{:S(2)}) collective-permute-start(bf16[2,128,128]{2,1,0:T(8,128)(2,1)S(1)} %get-tuple-element.11), channel_id=1, source_target_pairs={{0,6},{1,7},{2,4},{3,5},{4,2},{5,3},{6,0},{7,1},{8,14},{9,15},{10,... | collective-permute-start | bytes 196616 | tf_op jit(solution)/shard_map/ppermute | solution.py:402
  11.3 0.4 %collective-permute-start.5 = (bf16[2,128,128]{2,1,0:T(8,128)(2,1)S(1)}, bf16[2,128,128]{2,1,0:T(8,128)(2,1)S(1)}, u32[]{:S(2)}, u32[]{:S(2)}) collective-permute-start(bf16[2,128,128]{2,1,0:T(8,128)(2,1)S(1)} %get-tuple-element.11), channel_id=1, source_target_pairs={{0,4},{1,5},{2,6},{3,7},{4,0},{5,1},{6,2},{7,3},{8,12},{9,13},{10,... | collective-permute-start | bytes 196616 | tf_op jit(solution)/shard_map/ppermute | solution.py:402
  11.7 0.2 collective-permute-start.4
  11.9 0.1 broadcast_select_fusion
  12.0 3.9 %collective-permute-done.4 = bf16[2,128,128]{2,1,0:T(8,128)(2,1)S(1)} collective-permute-done((bf16[2,128,128]{2,1,0:T(8,128)(2,1)S(1)}, bf16[2,128,128]{2,1,0:T(8,128)(2,1)S(1)}, u32[]{:S(2)}, u32[]{:S(2)}) %collective-permute-start.4) | collective-permute-done | bytes 65568 | tf_op jit(solution)/shard_map/ppermute | solution.py:402
  16.1 0.1 collective-permute-start.7
  16.2 0.1 maximum_maximum_fusion.1
  16.2 3.6 %collective-permute-start.2 = (bf16[224,128]{1,0:T(8,128)(2,1)S(1)}, bf16[224,128]{1,0:T(8,128)(2,1)S(1)}, u32[]{:S(2)}, u32[]{:S(2)}) collective-permute-start(bf16[224,128]{1,0:T(8,128)(2,1)S(1)} %maximum_maximum_fusion.1), channel_id=1, source_target_pairs={{0,15},{1,2},{2,1},{3,4},{4,3},{5,6},{6,5},{7,8},{8,7},{9,10},{10,... | collective-permute-start | bytes 172040 | tf_op jit(solution)/shard_map/ppermute | solution.py:402
  19.9 0.1 maximum_maximum_fusion
  20.0 0.0 collective-permute-start.1
  20.0 2.6 %collective-permute-done.2.refs_2_ = bf16[224,128]{1,0:T(8,128)(2,1)S(1)} collective-permute-done((bf16[224,128]{1,0:T(8,128)(2,1)S(1)}, bf16[224,128]{1,0:T(8,128)(2,1)S(1)}, u32[]{:S(2)}, u32[]{:S(2)}) %collective-permute-start.2) | collective-permute-done | bytes 57376 | tf_op jit(solution)/shard_map/ppermute | solution.py:402
  22.6 0.7 %shard_map.149.filt = f32[4,256,256]{2,1,0:T(8,128)S(1)} custom-call(bf16[384,384]{1,0:T(8,128)(2,1)S(1)} %bitcast.5, bf16[224,128]{1,0:T(8,128)(2,1)S(1)} %collective-permute-done.1.refs_1_, bf16[224,128]{1,0:T(8,128)(2,1)S(1)} %collective-permute-done.2.refs_2_, bf16[64,384]{1,0:T(8,128)(2,1)S(1)} %collective-permute-done.refs_3_, ...), custom_call_target="tpu_custom_call" | custom-call | tf_op jit(solution)/shard_map/pallas_call | solution.py:343
  23.3 0.3 copy-done.2
  23.6 0.0 copy-done.7
  23.6 0.0 copy-done.8
  23.7 0.0 copy-done.9
  23.7 0.3 %copy-done.12 = s32[16]{0:T(128)S(1)} copy-done((s32[16]{0:T(128)S(1)}, s32[16]{0:T(128)}, u32[]{:S(2)}) %copy-start.12) | copy-done | bytes 88
  24.1 5.3 %shard_map.150 = (f32[1,384,384]{2,1,0:T(8,128)}, f32[1,384,384]{2,1,0:T(8,128)}, f32[1,384,384]{2,1,0:T(8,128)}) custom-call(s32[4,16]{1,0:T(4,128)S(1)} %bitcast.6, s32[16]{0:T(128)S(1)} %copy-done.12, f32[4,256,256]{2,1,0:T(8,128)S(1)} %shard_map.149.filt, bf16[8,128,128]{2,1,0:T(8,128)(2,1)S(1)} %constant_dynamic-update-slice_fusion.2.near_ref, ...), custom_call_target="tpu_custom_call" | custom-call | tf_op jit(solution)/shard_map/pallas_call | solution.py:343
  (33 shorter events, 0.2 us)
Async XLA Ops:
  0.6 7.7 %collective-permute-start.3 = (bf16[1,128,128]{2,1,0:T(8,128)(2,1)}, bf16[1,128,128]{2,1,0:T(8,128)(2,1)S(1)}, u32[]{:S(2)}, u32[]{:S(2)}) collective-permute-start(bf16[1,128,128]{2,1,0:T(8,128)(2,1)} %param.14), channel_id=1, source_target_pairs={{0,8},{1,9},{2,10},{3,11},{4,12},{5,13},{6,14},{7,15},{8,0},{9,1},... | collective-permute-start | bytes 98312 | tf_op jit(solution)/shard_map/ppermute | solution.py:402
  4.8 0.9 %copy-start.13 = (bf16[1,128,128]{2,1,0:T(8,128)(2,1)S(1)}, bf16[1,128,128]{2,1,0:T(8,128)(2,1)}, u32[]{:S(2)}) copy-start(bf16[1,128,128]{2,1,0:T(8,128)(2,1)} %param.14) | copy-start | bytes 98308
  5.6 6.4 %collective-permute-start = (bf16[64,384]{1,0:T(8,128)(2,1)S(1)}, bf16[64,384]{1,0:T(8,128)(2,1)S(1)}, u32[]{:S(2)}, u32[]{:S(2)}) collective-permute-start(bf16[64,384]{1,0:T(8,128)(2,1)S(1)} %dynamic-slice_bitcast_fusion), channel_id=1, source_target_pairs={{0,8},{1,9},{2,10},{3,11},{4,12},{5,13},{6,14},{7,15},{8,0},{9,1},... | collective-permute-start | bytes 147464 | tf_op jit(solution)/shard_map/ppermute | solution.py:402
  5.7 0.7 %copy-start.11 = (f32[16]{0:T(128)S(1)}, f32[16]{0:T(128)}, u32[]{:S(2)}) copy-start(f32[16]{0:T(128)} %defocus.1) | copy-start | bytes 196
  6.3 1.0 %copy-start = (bf16[1,384,384]{2,1,0:T(8,128)(2,1)S(1)}, bf16[1,384,384]{2,1,0:T(8,128)(2,1)}, u32[]{:S(2)}) copy-start(bf16[1,384,384]{2,1,0:T(8,128)(2,1)} %param.13) | copy-start | bytes 884740
  8.3 14.2 %copy-start.6 = (bf16[256,256]{1,0:T(8,128)(2,1)S(1)}, bf16[256,256]{1,0:T(8,128)(2,1)}, u32[]{:S(2)}) copy-start(bf16[256,256]{1,0:T(8,128)(2,1)} %constant.68.clone.refs_7_) | copy-start | bytes 393220
  8.4 7.6 %collective-permute-start.6 = (bf16[2,128,128]{2,1,0:T(8,128)(2,1)S(1)}, bf16[2,128,128]{2,1,0:T(8,128)(2,1)S(1)}, u32[]{:S(2)}, u32[]{:S(2)}) collective-permute-start(bf16[2,128,128]{2,1,0:T(8,128)(2,1)S(1)} %get-tuple-element.11), channel_id=1, source_target_pairs={{0,6},{1,7},{2,4},{3,5},{4,2},{5,3},{6,0},{7,1},{8,14},{9,15},{10,... | collective-permute-start | bytes 196616 | tf_op jit(solution)/shard_map/ppermute | solution.py:402
  11.3 4.7 %collective-permute-start.5 = (bf16[2,128,128]{2,1,0:T(8,128)(2,1)S(1)}, bf16[2,128,128]{2,1,0:T(8,128)(2,1)S(1)}, u32[]{:S(2)}, u32[]{:S(2)}) collective-permute-start(bf16[2,128,128]{2,1,0:T(8,128)(2,1)S(1)} %get-tuple-element.11), channel_id=1, source_target_pairs={{0,4},{1,5},{2,6},{3,7},{4,0},{5,1},{6,2},{7,3},{8,12},{9,13},{10,... | collective-permute-start | bytes 196616 | tf_op jit(solution)/shard_map/ppermute | solution.py:402
  11.7 4.3 %collective-permute-start.4 = (bf16[2,128,128]{2,1,0:T(8,128)(2,1)S(1)}, bf16[2,128,128]{2,1,0:T(8,128)(2,1)S(1)}, u32[]{:S(2)}, u32[]{:S(2)}) collective-permute-start(bf16[2,128,128]{2,1,0:T(8,128)(2,1)S(1)} %get-tuple-element.11), channel_id=1, source_target_pairs={{0,2},{1,3},{2,0},{3,1},{4,6},{5,7},{6,4},{7,5},{8,10},{9,11},{10,... | collective-permute-start | bytes 196616 | tf_op jit(solution)/shard_map/ppermute | solution.py:402
  12.0 10.5 %copy-start.5 = (bf16[256,256]{1,0:T(8,128)(2,1)S(1)}, bf16[256,256]{1,0:T(8,128)(2,1)}, u32[]{:S(2)}) copy-start(bf16[256,256]{1,0:T(8,128)(2,1)} %constant.69.clone.refs_8_) | copy-start | bytes 393220
  16.0 6.6 %copy-start.1 = (bf16[1,384,384]{2,1,0:T(8,128)(2,1)S(1)}, bf16[1,384,384]{2,1,0:T(8,128)(2,1)}, u32[]{:S(2)}) copy-start(bf16[1,384,384]{2,1,0:T(8,128)(2,1)} %param.13) | copy-start | bytes 884740
  16.0 6.5 %copy-start.4 = (bf16[256,256]{1,0:T(8,128)(2,1)S(1)}, bf16[256,256]{1,0:T(8,128)(2,1)}, u32[]{:S(2)}) copy-start(bf16[256,256]{1,0:T(8,128)(2,1)} %constant.66.clone.refs_5_.fwd_e) | copy-start | bytes 393220
  16.1 6.5 %copy-start.3 = (bf16[256,256]{1,0:T(8,128)(2,1)S(1)}, bf16[256,256]{1,0:T(8,128)(2,1)}, u32[]{:S(2)}) copy-start(bf16[256,256]{1,0:T(8,128)(2,1)} %constant.67.clone.refs_6_.fwd_o) | copy-start | bytes 393220
  16.1 7.3 %collective-permute-start.7 = (bf16[8,128,128]{2,1,0:T(8,128)(2,1)S(1)}, bf16[8,128,128]{2,1,0:T(8,128)(2,1)S(1)}, u32[]{:S(2)}, u32[]{:S(2)}) collective-permute-start(bf16[8,128,128]{2,1,0:T(8,128)(2,1)S(1)} %constant_dynamic-update-slice_fusion.2.near_ref), channel_id=1, source_target_pairs={{0,1},{1,0},{2,3},{3,2},{4,5},{5,4},{6,7},{7,6},{8,9},{9,8},{10,11... | collective-permute-start | bytes 786440 | tf_op jit(solution)/shard_map/ppermute | solution.py:402
  16.2 6.3 %collective-permute-start.2 = (bf16[224,128]{1,0:T(8,128)(2,1)S(1)}, bf16[224,128]{1,0:T(8,128)(2,1)S(1)}, u32[]{:S(2)}, u32[]{:S(2)}) collective-permute-start(bf16[224,128]{1,0:T(8,128)(2,1)S(1)} %maximum_maximum_fusion.1), channel_id=1, source_target_pairs={{0,15},{1,2},{2,1},{3,4},{4,3},{5,6},{6,5},{7,8},{8,7},{9,10},{10,... | collective-permute-start | bytes 172040 | tf_op jit(solution)/shard_map/ppermute | solution.py:402
  20.0 2.6 %collective-permute-start.1 = (bf16[224,128]{1,0:T(8,128)(2,1)S(1)}, bf16[224,128]{1,0:T(8,128)(2,1)S(1)}, u32[]{:S(2)}, u32[]{:S(2)}) collective-permute-start(bf16[224,128]{1,0:T(8,128)(2,1)S(1)} %maximum_maximum_fusion), channel_id=1, source_target_pairs={{0,1},{1,0},{2,3},{3,2},{4,5},{5,4},{6,7},{7,6},{8,9},{9,8},{10,11... | collective-permute-start | bytes 172040 | tf_op jit(solution)/shard_map/ppermute | solution.py:402
  22.6 1.0 %copy-start.2 = (bf16[1024,256]{1,0:T(8,128)(2,1)S(1)}, bf16[1024,256]{1,0:T(8,128)(2,1)}, u32[]{:S(2)}) copy-start(bf16[1024,256]{1,0:T(8,128)(2,1)} %constant.73.clone.temp_cols) | copy-start | bytes 1572868
  22.6 1.1 %copy-start.7 = (bf16[128,512]{1,0:T(8,128)(2,1)S(1)}, bf16[128,512]{1,0:T(8,128)(2,1)}, u32[]{:S(2)}) copy-start(bf16[128,512]{1,0:T(8,128)(2,1)} %constant.72.clone.temp_rows) | copy-start | bytes 393220
  22.6 1.1 %copy-start.8 = (bf16[256,256]{1,0:T(8,128)(2,1)S(1)}, bf16[256,256]{1,0:T(8,128)(2,1)}, u32[]{:S(2)}) copy-start(bf16[256,256]{1,0:T(8,128)(2,1)} %constant.71.clone.inv_o) | copy-start | bytes 393220
  22.6 1.1 %copy-start.9 = (bf16[256,256]{1,0:T(8,128)(2,1)S(1)}, bf16[256,256]{1,0:T(8,128)(2,1)}, u32[]{:S(2)}) copy-start(bf16[256,256]{1,0:T(8,128)(2,1)} %constant.70.clone.inv_e) | copy-start | bytes 393220
  22.6 1.1 %copy-start.10 = (s32[16,4]{0,1:T(4,128)S(1)}, s32[16,4]{0,1:T(4,128)}, u32[]{:S(2)}) copy-start(s32[16,4]{0,1:T(4,128)} %param.15) | copy-start | bytes 772
  23.3 0.7 %copy-start.12 = (s32[16]{0:T(128)S(1)}, s32[16]{0:T(128)}, u32[]{:S(2)}) copy-start(s32[16]{0:T(128)} %lengths.1) | copy-start | bytes 196
where the time goes:
time: 29.6 us; the launch traced here: 29.4 us
  starting transfers between devices  11.5 us (39%)
  Pallas kernels  7.06 us (24%)
  waiting for transfers between devices  6.53 us (22%)
  local copies, waits for them, and re-layouts  3.25 us (11%)
  between operations  0.84 us (3%)
    ppermute x8, starting transfers between devices, send(): lax.ppermute(block, 'tile', [(i, target(i)) for i in range(tile_count)])  11.5 us
    pallas_call x3, Pallas kernels, vmem_call(): pl.pallas_call(kernel, out_shape=tuple((jax.ShapeDtypeStruct(shape, dtype...  7.06 us
    ppermute x8, waiting for transfers between devices, send(): lax.ppermute(block, 'tile', [(i, target(i)) for i in range(tile_count)])  6.53 us
    unnamed x31, local copies, waits for them, and re-layouts  2.41 us
    dynamic_slice x1, local copies, waits for them, and re-layouts, shards(): lax.dynamic_slice_in_dim(centre_block, start, margin, 0)  0.81 us
  transfers between devices with their start and end apart: 8, of which 2 were waited for; matrix products, arithmetic and copies ran while one was open for 4% of the time, Pallas kernels for 6%

commit v1 on v0

--- a/solution.py
+++ b/solution.py
@@ -37,7 +37,9 @@
     tables += [table.T for table in tables]
     for index in (even, odd):
         cosine, sine = wave_tables(index, position, extent)
-        tables.append(np.concatenate([cosine, np.where(index[:, None] == 0, sine, -sine)], axis=0))
+        first = index[:, None] == 0
+        cosine = np.where(first, 0.5 + 0.5 * sine, cosine)
+        tables.append(np.concatenate([cosine, np.where(first, 0.5 - 0.5 * sine, -sine)], axis=0))
     order = np.concatenate([even, odd])
     centred = np.arange(box) - box // 2
     cosine, sine = wave_tables(order, centred, extent)
@@ -92,9 +94,36 @@
     return pltpu.roll(block, lanes, 1)
 
 
-def early_kernel(defocus, centre_ref, weight_ref, mate_ref, peer_ref):
+def pack_kernel(*refs):
+    sources, held, (ends_ref, mate_ref, peer_ref, sem) = refs[:4], refs[4:8], refs[8:]
+    copies = [pltpu.make_async_copy(sources[k], held[k], sem.at[k]) for k in range(4)]
+    for copy in copies:
+        copy.start()
     me = lax.axis_index("tile")
-    focus_value = defocus[me]
+    tile_count = lax.axis_size("tile")
+    place = lax.rem(me + GRID // 2, tile_count)
+    centre_ref = held[0]
+    centre, lane, margin = centre_ref.shape[0], mate_ref.shape[1], ends_ref.shape[0]
+    copies[0].wait()
+    top = centre_ref[:margin].astype(jnp.float32)
+    bottom = centre_ref[centre - margin :].astype(jnp.float32)
+    ends_ref[...] = jnp.where(place < GRID, bottom, top).astype(jnp.bfloat16)
+    half = centre // 2
+    first = centre_ref[:, :lane].astype(jnp.float32)
+    last = centre_ref[:, centre - lane :].astype(jnp.float32)
+    low = lax.broadcasted_iota(jnp.int32, (half, lane), 1) < lane // 2
+    first = jnp.where(low, first[:half], swap_halves(first[half:], lane // 2))
+    last = jnp.where(low, swap_halves(last[:half], lane // 2), last[half:])
+    odd = lax.rem(me, 2) == 1
+    mate_ref[...] = jnp.where(odd, first, last).astype(jnp.bfloat16)
+    peer_ref[...] = jnp.where(odd, last, first).astype(jnp.bfloat16)
+    for copy in copies[1:]:
+        copy.wait()
+
+
+def early_kernel(defocus, weight_ref):
+    me = lax.axis_index("tile")
+    focus_value = defocus[0, me]
     lane = weight_ref.shape[1] // 2
     extent = 4 * lane
     edge = float(2 * lane)
@@ -133,16 +162,6 @@
                 )
             for k in range(4):
                 weight_ref[k, rows, cols] = parts[k]
-    centre = centre_ref.shape[0]
-    half = centre // 2
-    first = centre_ref[:, :lane].astype(jnp.float32)
-    last = centre_ref[:, centre - lane :].astype(jnp.float32)
-    low = lax.broadcasted_iota(jnp.int32, (half, lane), 1) < lane // 2
-    first = jnp.where(low, first[:half], swap_halves(first[half:], lane // 2))
-    last = jnp.where(low, swap_halves(last[:half], lane // 2), last[half:])
-    odd = lax.rem(me, 2) == 1
-    mate_ref[...] = jnp.where(odd, first, last).astype(jnp.bfloat16)
-    peer_ref[...] = jnp.where(odd, last, first).astype(jnp.bfloat16)
 
 
 def packed_sides(mate, peer, lane, start, stop, left_open, right_open):
@@ -212,134 +231,193 @@
                 filt[k, rows, cols] = weight_ref[k, rows, cols] * parts[k]
 
 
+def weave(*tracks):
+    steps = []
+    for order, track in enumerate(tracks):
+        steps += [((k + 0.5) / len(track), order, k, step) for k, step in enumerate(track)]
+    for *_, step in sorted(steps, key=lambda entry: entry[:3]):
+        step()
+
+
 def match_kernel(
-    orients, lengths, filt, near_ref, far_ref,
+    orients, lengths, wide, near_ref, far_ref,
     fwd_e, fwd_o, inv_e, inv_o, temp_rows, temp_cols,
     snr_ref, mean_ref, var_ref,
-    proj, mixed, combo_e, combo_o, out_buf, out_sem,
+    filt, proj, mixed, combos, out_buf, out_sem,
 ):
     me = lax.axis_index("tile")
-    half = filt.shape[1]
-    lane, extent = half // 2, 2 * half
+    half = wide.shape[1]
+    lane = half // 2
     centre = out_buf.shape[1]
+    box = near_ref.shape[1]
+    strip = combos.shape[3] // LMAX
     tile_count = lax.axis_size("tile")
     distances = flips(tile_count)
     held = near_ref.shape[0] // (tile_count // 2)
+    count = lengths[0, me]
+    bf16, f32 = jnp.bfloat16, jnp.float32
+    step = 16
+    col_first = lax.broadcasted_iota(jnp.int32, (step, half), 1) == 0
+    row_first = lax.broadcasted_iota(jnp.int32, (step, half), 0) == 0
+    corner = col_first & row_first
+    thin_first = col_first.astype(f32).astype(bf16) > 0
+    sign = 1.0 - 2.0 * (lax.broadcasted_iota(jnp.int32, (box, lane), 0) % 2).astype(f32)
+    box_col = lax.broadcasted_iota(jnp.int32, (box, lane), 1) == 0
+    edges, waves_of = {}, {}
 
     def chosen(slot):
-        orient = jnp.clip(orients[slot, me], 0, 2 * near_ref.shape[0] - 1)
+        orient = orients[slot, me]
+        if slot:
+            orient = jnp.where(slot < count, orient, orients[0, me])
+        orient = jnp.clip(orient, 0, 2 * near_ref.shape[0] - 1)
         apart = lax.div(orient, held) ^ me
         at = lax.rem(orient, held)
         for k, distance in enumerate(distances[:-1]):
             at = at + (lax.div(apart, distance) & 1) * (held << k)
         return jnp.where(apart & 1 == 1, far_ref[at], near_ref[at])
 
-    step = 16
-    lane_col = lax.broadcasted_iota(jnp.int32, (step, lane), 1) == 0
-    first_row = lax.broadcasted_iota(jnp.int32, (step, lane), 0) == 0
-    corner = lane_col & first_row
-    box = near_ref.shape[1]
-    sign = 1.0 - 2.0 * (lax.broadcasted_iota(jnp.int32, (box, lane), 0) % 2).astype(jnp.float32)
-    box_col = lax.broadcasted_iota(jnp.int32, (box, lane), 1) == 0
-    for slot in range(LMAX):
-        waves = dot(chosen(slot), temp_rows[...])
-        first_u, first_v = waves[:, :lane], waves[:, half : half + lane]
-        row_edge = -jnp.sum(first_u * sign, axis=0, keepdims=True)
-        col_edge = jnp.sum(first_v, axis=0, keepdims=True)
-        v_part = jnp.concatenate([jnp.where(box_col, 0.0, first_v), waves[:, half + lane :]], axis=1)
-        u_minus = jnp.concatenate([jnp.where(box_col, first_v, first_u), waves[:, lane:half]], axis=1)
-        plus = jnp.concatenate([waves[:, :half], v_part], axis=0).astype(jnp.bfloat16)
-        minus = jnp.concatenate([u_minus, v_part], axis=0).astype(jnp.bfloat16)
-        proj[: 2 * half] = dot(temp_cols[: 2 * half], plus)
-        proj[2 * half :] = dot(temp_cols[2 * half :], minus)
-        base = slot * extent
-        for start in range(0, half, step):
-            row_odd, at = start // lane, start % lane
-            for col_odd in range(2):
-                cols = slice(col_odd * lane, (col_odd + 1) * lane)
-                fpr, fpi, fmr, fmi = (filt[k, start : start + step, cols] for k in range(4))
-                ppr, ppi, pmr, pmi = (proj[k * half + start : k * half + start + step, cols] for k in range(4))
-                if start == 0 and col_odd == 0:
-                    ppi = jnp.where(corner, row_edge, ppi)
-                    pmi = jnp.where(corner, pmr, pmi)
-                    pmr = jnp.where(corner, col_edge, pmr)
-                plus_r, plus_i = fpr * ppr + fpi * ppi, fpi * ppr - fpr * ppi
-                minus_r, minus_i = fmr * pmr + fmi * pmi, fmi * pmr - fmr * pmi
-                cos_r, sin_r = plus_r + minus_r, minus_i - plus_i
-                cos_i, sin_i = plus_i + minus_i, plus_r - minus_r
-                if start == 0:
-                    cos_r = jnp.where(first_row, plus_r, cos_r)
-                    sin_r = jnp.where(first_row, minus_r, sin_r)
-                    cos_i = jnp.where(first_row, plus_i, cos_i)
-                    sin_i = jnp.where(first_row, minus_i, sin_i)
-                if col_odd == 0:
-                    cos_r = jnp.where(lane_col, plus_r, cos_r)
-                    sin_r = jnp.where(lane_col, -plus_i, sin_r)
-                    cos_i = jnp.where(lane_col, minus_r, cos_i)
-                    sin_i = jnp.where(lane_col, minus_i, sin_i)
-                    if start == 0:
-                        cos_r = jnp.where(corner, fpr * ppr, cos_r)
-                        sin_r = jnp.where(corner, fpi * ppi, sin_r)
-                        cos_i = jnp.where(corner, fmr * pmr, cos_i)
-                        sin_i = jnp.where(corner, fmi * pmi, sin_i)
-                at_r = slice(base + col_odd * lane, base + (col_odd + 1) * lane)
-                at_i = slice(base + half + col_odd * lane, base + half + (col_odd + 1) * lane)
-                mixed[row_odd, at : at + step, at_r] = cos_r.astype(jnp.bfloat16)
-                mixed[row_odd, lane + at : lane + at + step, at_r] = sin_r.astype(jnp.bfloat16)
-                mixed[row_odd, at : at + step, at_i] = cos_i.astype(jnp.bfloat16)
-                mixed[row_odd, lane + at : lane + at + step, at_i] = sin_i.astype(jnp.bfloat16)
-        even = dot(fwd_e[...], mixed[0, :, base : base + extent])
-        odd = dot(fwd_o[...], mixed[1, :, base : base + extent])
-        total = even + odd
-        for part in range(centre // lane):
-            if part * lane < half:
-                value = total[part * lane : (part + 1) * lane]
+    def project(slot):
+        def rows():
+            waves = dot(chosen(slot), temp_rows[...])
+            first_u, first_v = waves[:, :lane], waves[:, half : half + lane]
+            row_edge = -jnp.sum(first_u * sign, axis=0, keepdims=True)
+            col_edge = jnp.sum(first_v, axis=0, keepdims=True)
+            edges[slot] = (beside(row_edge, row_edge), beside(col_edge, col_edge))
+            v_part = beside(jnp.where(box_col, 0.0, first_v), waves[:, half + lane :])
+            u_minus = beside(jnp.where(box_col, first_v, first_u), waves[:, lane:half])
+            plus = jnp.concatenate([waves[:, :half], v_part], axis=0).astype(bf16)
+            minus = jnp.concatenate([u_minus, v_part], axis=0).astype(bf16)
+            waves_of[slot] = (plus, plus, minus, minus)
+
+        def cols(k):
+            here = slice(k * half, (k + 1) * half)
+            proj[slot % 2, here] = dot(temp_cols[here], waves_of[slot][k]).astype(bf16)
+
+        return [rows] + [functools.partial(cols, k) for k in range(4)]
+
+    def mix_first(slot, fs, ps):
+        fpr, fpi, fmr, fmi = (f.astype(f32) for f in fs)
+        ppr, ppi, pmr, pmi = (p.astype(f32) for p in ps)
+        row_edge, col_edge = edges[slot]
+        ppi = jnp.where(corner, row_edge, ppi)
+        pmi = jnp.where(corner, pmr, pmi)
+        pmr = jnp.where(corner, col_edge, pmr)
+        plus_r, plus_i = fpr * ppr + fpi * ppi, fpi * ppr - fpr * ppi
+        minus_r, minus_i = fmr * pmr + fmi * pmi, fmi * pmr - fmr * pmi
+        cos_r, sin_r = plus_r + minus_r, minus_i - plus_i
+        cos_i, sin_i = plus_i + minus_i, plus_r - minus_r
+        cos_i, sin_i = jnp.where(col_first, sin_i, cos_i), jnp.where(col_first, -cos_i, sin_i)
+        cos_r = jnp.where(row_first, plus_r, cos_r)
+        sin_r = jnp.where(row_first, minus_r, sin_r)
+        cos_i = jnp.where(row_first, plus_i, cos_i)
+        sin_i = jnp.where(row_first, minus_i, sin_i)
+        cos_r = jnp.where(corner, fpr * ppr + fmr * pmr, cos_r)
+        sin_r = jnp.where(corner, fpi * ppi + fmi * pmi, sin_r)
+        cos_i = jnp.where(corner, fpr * ppr - fmr * pmr, cos_i)
+        sin_i = jnp.where(corner, fpi * ppi - fmi * pmi, sin_i)
+        return cos_r.astype(bf16), sin_r.astype(bf16), cos_i.astype(bf16), sin_i.astype(bf16)
+
+    def mix(slot, start):
+        row_odd, at = start // lane, start % lane
+        buffer = slot % 2
+        fs = [filt[k, start : start + step] for k in range(4)]
+        ps = [proj[buffer, k * half + start : k * half + start + step] for k in range(4)]
+        if start == 0:
+            cos_r, sin_r, cos_i, sin_i = mix_first(slot, fs, ps)
+        else:
+            fpr, fpi, fmr, fmi = fs
+            ppr, ppi, pmr, pmi = ps
+            plus_r, plus_i = fpr * ppr + fpi * ppi, fpi * ppr - fpr * ppi
+            minus_r, minus_i = fmr * pmr + fmi * pmi, fmi * pmr - fmr * pmi
+            cos_r, sin_r = plus_r + minus_r, minus_i - plus_i
+            cos_i, sin_i = plus_i + minus_i, plus_r - minus_r
+            cos_i, sin_i = jnp.where(thin_first, sin_i, cos_i), jnp.where(thin_first, -cos_i, sin_i)
+        mixed[buffer, row_odd, 0, at : at + step] = cos_r
+        mixed[buffer, row_odd, 0, lane + at : lane + at + step] = sin_r
+        mixed[buffer, row_odd, 1, at : at + step] = cos_i
+        mixed[buffer, row_odd, 1, lane + at : lane + at + step] = sin_i
+
+    def combine(slot):
+        def rows(imag, first):
+            buffer = slot % 2
+            here = slice(first * lane, (first + 1) * lane)
+            even = dot(fwd_e[here], mixed[buffer, 0, imag])
+            odd = dot(fwd_o[here], mixed[buffer, 1, imag])
+            starts = [(first * lane, even + odd)]
+            if half + first * lane < centre:
+                starts.append((half + first * lane, even - odd))
+            for start, value in starts:
+                value = value.astype(bf16)
+                for k in range(lane // strip):
+                    place = slice(slot * strip, (slot + 1) * strip)
+                    piece = value[k * strip : (k + 1) * strip]
+                    combos[0, imag, start // strip + k, place] = piece[:, :lane]
+                    combos[1, imag, start // strip + k, place] = piece[:, lane:]
+
+        return [functools.partial(rows, imag, first) for imag in range(2) for first in range(half // lane)]
+
+    share = 1.0 / jnp.full((1, 1), count, jnp.int32).astype(f32)
+    shares = [jnp.where(slot < count, share, 0.0) for slot in range(LMAX)]
+    fields, out_copies = {}, []
+
+    def back(part):
+        fields[part] = (
+            dot(beside(combos[0, 0, part], combos[0, 1, part]), inv_e[...]),
+            dot(beside(combos[1, 0, part], combos[1, 1, part]), inv_o[...]),
+        )
+
+    def gather(part):
+        even, odd = fields.pop(part)
+        for slot in range(LMAX):
+            here = slice(slot * strip, (slot + 1) * strip)
+            near, far = even[here], odd[here]
+            score = beside(near + far, near[:, : centre - half] - far[:, : centre - half])
+            scaled = score * shares[slot]
+            if slot == 0:
+                best, mean, squares = score, scaled, scaled * score
             else:
-                near = slice(part * lane - half, (part + 1) * lane - half)
-                value = even[near] - odd[near]
-            value = value.astype(jnp.bfloat16)
-            here = slice(slot * lane, (slot + 1) * lane)
-            combo_e[part, here, :lane] = value[:, :lane]
-            combo_e[part, here, lane:] = value[:, half : half + lane]
-            combo_o[part, here, :lane] = value[:, lane:half]
-            combo_o[part, here, lane:] = value[:, half + lane :]
-
-    count = lengths[me]
-    inverse_count = 1.0 / jnp.full((1, 1), count, jnp.int32).astype(jnp.float32)
-    out_copies = []
-    for part in range(centre // lane):
-        even = dot(combo_e[part], inv_e[...])
-        odd = dot(combo_o[part], inv_o[...])
-        best = total = squares = None
-        for slot in range(LMAX):
-            here = slice(slot * lane, (slot + 1) * lane)
-            score = jnp.concatenate(
-                [even[here] + odd[here], even[here, : centre - half] - odd[here, : centre - half]], axis=1
-            )
-            if slot == 0:
-                best, total, squares = score, score, score * score
-            else:
-                taken = slot < count
-                kept = jnp.where(taken, score, 0.0)
-                best = jnp.maximum(best, jnp.where(taken, score, -jnp.inf))
-                total = total + kept
-                squares = squares + kept * kept
-        mean = total * inverse_count
-        variance = squares * inverse_count - mean * mean
-        snr = (best - mean) * lax.rsqrt(jnp.maximum(variance, var_floor))
-        rows = slice(part * lane, (part + 1) * lane)
-        for k, (value, out) in enumerate(((snr, snr_ref), (mean, mean_ref), (variance, var_ref))):
-            out_buf[k, rows] = value
+                best = jnp.maximum(best, score)
+                mean, squares = mean + scaled, squares + scaled * score
+        variance = squares - mean * mean
+        rows = slice(part * strip, (part + 1) * strip)
+        out_buf[0, rows] = (best - mean) * lax.rsqrt(jnp.maximum(variance, var_floor))
+        out_buf[1, rows] = mean
+        out_buf[2, rows] = variance
+        for k, out in enumerate((snr_ref, mean_ref, var_ref)):
             copy = pltpu.make_async_copy(out_buf.at[k, rows], out.at[0, rows], out_sem.at[k, part])
             copy.start()
             out_copies.append(copy)
+
+    def thin():
+        for k in range(4):
+            filt[k] = wide[k].astype(bf16)
+
+    parts = centre // strip
+    for tick in range(LMAX + 2):
+        products = project(tick) if tick < LMAX else []
+        if 0 <= tick - 2:
+            products = products + combine(tick - 2)
+        sums = [thin] if tick == 0 else []
+        if 0 <= tick - 1 < LMAX:
+            sums = [functools.partial(mix, tick - 1, start) for start in range(0, half, step)]
+        weave(products, sums)
+    for part in range(parts):
+        back(part)
+        gather(part)
     for copy in out_copies:
         copy.wait()
 
 
-def vmem_call(kernel, inputs, outs, scratch, scalars, limit, out_spec=pltpu.VMEM, cost=None):
+def beside(left, right):
+    return jnp.concatenate([left, right], axis=1)
+
+
+def vmem_call(kernel, inputs, outs, scratch, scalars, limit, out_spec=pltpu.VMEM, in_space=pltpu.VMEM):
+    if in_space == pltpu.HBM:
+        fixed = [pltpu.with_memory_space_constraint(array, pltpu.HBM) for array in inputs[scalars:]]
+        inputs = (*inputs[:scalars], *fixed)
     smem = pl.BlockSpec(memory_space=pltpu.SMEM)
-    vmem = pl.BlockSpec(memory_space=pltpu.VMEM)
+    vmem = pl.BlockSpec(memory_space=in_space)
     return pl.pallas_call(
         kernel,
         out_shape=tuple(jax.ShapeDtypeStruct(shape, dtype) for shape, dtype in outs),
@@ -347,14 +425,21 @@
         out_specs=tuple(pl.BlockSpec(memory_space=out_spec) for _ in outs),
         scratch_shapes=scratch,
         compiler_params=pltpu.CompilerParams(vmem_limit_bytes=limit << 20),
-        cost_estimate=cost,
     )(*inputs)
 
 
-def early(defocus, centre_block, extent):
-    centre, half, lane = centre_block.shape[0], extent // 2, extent // 4
+def pack(orient_list, lengths, defocus, centre_block, box):
+    centre = centre_block.shape[0]
+    lane = (centre + box) // 4
+    held = (centre_block, orient_list.T, lengths[None], defocus[None])
     strip = ((centre // 2, lane), jnp.bfloat16)
-    return vmem_call(early_kernel, (defocus, centre_block), (((4, half, half), jnp.float32), strip, strip), [], 1, 8)
+    outs = [(array.shape, array.dtype) for array in held] + [((box // 2, centre), jnp.bfloat16), strip, strip]
+    return vmem_call(pack_kernel, held, outs, [pltpu.SemaphoreType.DMA((4,))], 0, 8, in_space=pltpu.HBM)
+
+
+def early(defocus, extent):
+    half = extent // 2
+    return vmem_call(early_kernel, (defocus,), (((4, half, half), jnp.float32),), [], 1, 8)[0]
 
 
 def tile_spectrum(paired, pieces, weights, tables, extent):
@@ -369,17 +454,17 @@
 def match(orient_list, lengths, filt, near, far, tables, centre):
     half = filt.shape[1]
     lane, extent = half // 2, 2 * half
-    parts = centre // lane
+    strip = lane // 2
     out = ((1, centre, centre), jnp.float32)
     return vmem_call(
         match_kernel, (orient_list, lengths, filt, near, far, *tables[:2], *tables[4:]), (out, out, out),
         [
-            pltpu.VMEM((2 * extent, half), jnp.float32),
-            pltpu.VMEM((2, half, LMAX * extent), jnp.bfloat16),
-            pltpu.VMEM((parts, LMAX * lane, half), jnp.bfloat16),
-            pltpu.VMEM((parts, LMAX * lane, half), jnp.bfloat16),
+            pltpu.VMEM((4, half, half), jnp.bfloat16),
+            pltpu.VMEM((2, 2 * extent, half), jnp.bfloat16),
+            pltpu.VMEM((2, 2, 2, half, half), jnp.bfloat16),
+            pltpu.VMEM((2, 2, centre // strip, LMAX * strip, lane), jnp.bfloat16),
             pltpu.VMEM((3, centre, centre), jnp.float32),
-            pltpu.SemaphoreType.DMA((3, parts)),
+            pltpu.SemaphoreType.DMA((3, centre // strip)),
         ],
         2, 24, pl.ANY,
     )
@@ -404,12 +489,13 @@
     paired = tile_rows == 2
     if paired:
         odd = position % 2 == 1
-        lower_row = tile_row == tile_rows - 1
         distances = flips(tile_count)
         pair = send(templates, lambda i: i ^ distances[0])
-        start = jnp.where(lower_row, 0, centre - margin)
-        ends = send(lax.dynamic_slice_in_dim(centre_block, start, margin, 0), lambda i: i ^ GRID)
-        weights, to_mate, to_peer = early(defocus, centre_block, extent)
+        block, orients, counts, focus, to_ends, to_mate, to_peer = pack(
+            orient_list, lengths, defocus, centre_block, box
+        )
+        ends = send(to_ends, lambda i: i ^ GRID)
+        weights = early(focus, extent)
 
         def strip(own, use_first):
             edge = jnp.where(use_first, ends[:, :margin], ends[:, centre - margin :])
@@ -424,7 +510,7 @@
         from_mate = send(strip(to_mate, odd), lambda i: i ^ 1)
         near = jnp.concatenate([group[0], group[2], group[3], group[1]], axis=0)
         far = send(near, lambda i: i ^ 1)
-        filt = tile_spectrum(True, (centre_block, from_mate, from_peer, ends), weights, tables, extent)
+        filt = tile_spectrum(True, (block, from_mate, from_peer, ends), weights, tables, extent)
     else:
 
         def arrive(block, distance):
@@ -432,7 +518,8 @@
                 block, "tile", [((i + distance) % tile_count, i) for i in range(tile_count)]
             )
 
-        weights, _, _ = early(defocus, centre_block, extent)
+        _, orients, counts, focus, *_ = pack(orient_list, lengths, defocus, centre_block, box)
+        weights = early(focus, extent)
         right = arrive(centre_block[:, :margin], 1)
         left = arrive(centre_block[:, centre - margin :], -1)
         right = jnp.where(column == GRID - 1, jnp.zeros_like(right), right)
@@ -449,7 +536,7 @@
             near = jnp.concatenate([near, send(near, lambda i, d=distance: i ^ d)], axis=0)
         far = send(near, lambda i: i ^ 1)
         filt = tile_spectrum(False, (centre_block, cols, rows), weights, tables, extent)
-    return match(orient_list.T, lengths, filt, near, far, tables, centre)
+    return match(orients, counts, filt, near, far, tables, centre)
 
 
 def solution(mesh):

time: 29.6 us -> 27.6 us (0.932)
  local copies, waits for them, and re-layouts: 3.25 us -> 0.51 us
  starting transfers between devices: 11.5 us -> 13 us
  waiting for transfers between devices: 6.53 us -> 5.74 us
    unnamed x31 -> x21, local copies, waits for them, and re-layouts: 2.41 us -> 0.48 us
    ppermute x8, starting transfers between devices: 11.5 us -> 13 us  [send(): lax.ppermute(block, 'tile', [(i, target(i)) for i in range(tile_count)])]
    dynamic_slice x1 -> x0, local copies, waits for them, and re-layouts: 0.81 us -> none  [shards(): lax.dynamic_slice_in_dim(centre_block, start, margin, 0)]
    ppermute x8, waiting for transfers between devices: 6.53 us -> 5.74 us  [send(): lax.ppermute(block, 'tile', [(i, target(i)) for i in range(tile_count)])]
    pallas_call x3 -> x4, Pallas kernels: 7.06 us -> 7.15 us  [vmem_call(): pl.pallas_call(kernel, out_shape=tuple((jax.ShapeDtypeStruct(shape, dtype...]
  transfers between devices with their start and end apart: 8 -> 8, of which waited for: 2 -> 4; matrix products, arithmetic and copies ran while one was open for 4% -> 1% of each run, Pallas kernels for 6% -> 10%
where the time goes in v1:
time: 27.6 us; the launch traced here: 27.4 us
  starting transfers between devices  13 us (47%)
  Pallas kernels  7.15 us (26%)
  waiting for transfers between devices  5.74 us (21%)
  between operations  0.79 us (3%)
  local copies, waits for them, and re-layouts  0.51 us (2%)
    ppermute x8, starting transfers between devices, send(): lax.ppermute(block, 'tile', [(i, target(i)) for i in range(tile_count)])  13 us
    pallas_call x4, Pallas kernels, vmem_call(): pl.pallas_call(kernel, out_shape=tuple((jax.ShapeDtypeStruct(shape, dtype...  7.15 us
    ppermute x8, waiting for transfers between devices, send(): lax.ppermute(block, 'tile', [(i, target(i)) for i in range(tile_count)])  5.74 us
  transfers between devices with their start and end apart: 8, of which 4 were waited for; matrix products, arithmetic and copies ran while one was open for 1% of the time, Pallas kernels for 10%

profile of v1, /device:TPU:0, one launch (start us, length us, event | category | flops | bytes accessed | tf_op | source)
XLA Modules:
  0.0 27.4 jit_solution(50331712707076556)
XLA Ops:
  0.6 4.1 %collective-permute-start.3 = (bf16[1,128,128]{2,1,0:T(8,128)(2,1)}, bf16[1,128,128]{2,1,0:T(8,128)(2,1)S(1)}, u32[]{:S(2)}, u32[]{:S(2)}) collective-permute-start(bf16[1,128,128]{2,1,0:T(8,128)(2,1)} %param.14), channel_id=1, source_target_pairs={{0,8},{1,9},{2,10},{3,11},{4,12},{5,13},{6,14},{7,15},{8,0},{9,1},... | collective-permute-start | bytes 98312 | tf_op jit(solution)/shard_map/ppermute | solution.py:487
  4.8 1.1 %shard_map.148 = (bf16[384,384]{1,0:T(8,128)(2,1)S(1)}, s32[4,16]{1,0:T(4,128)S(1)}, s32[1,16]{1,0:T(1,128)S(1)}, f32[1,16]{1,0:T(1,128)S(1)}, bf16[64,384]{1,0:...) custom-call(bf16[384,384]{1,0:T(8,128)(2,1)} %bitcast.4, s32[4,16]{1,0:T(4,128)} %bitcast.5, ...), custom_call_target="tpu_custom_call" | custom-call | tf_op jit(solution)/shard_map/pallas_call | solution.py:421
  5.9 0.1 collective-permute-start
  6.0 1.2 %collective-permute-done.3 = bf16[1,128,128]{2,1,0:T(8,128)(2,1)S(1)} collective-permute-done((bf16[1,128,128]{2,1,0:T(8,128)(2,1)}, bf16[1,128,128]{2,1,0:T(8,128)(2,1)S(1)}, u32[]{:S(2)}, u32[]{:S(2)}) %collective-permute-start.3) | collective-permute-done | bytes 32800 | tf_op jit(solution)/shard_map/ppermute | solution.py:487
  7.2 2.8 %collective-permute-start.6 = (bf16[2,128,128]{2,1,0:T(8,128)(2,1)S(1)}, bf16[2,128,128]{2,1,0:T(8,128)(2,1)S(1)}, u32[]{:S(2)}, u32[]{:S(2)}) collective-permute-start(bf16[2,128,128]{2,1,0:T(8,128)(2,1)S(1)} %get-tuple-element.19), channel_id=1, source_target_pairs={{0,6},{1,7},{2,4},{3,5},{4,2},{5,3},{6,0},{7,1},{8,14},{9,15},{10,... | collective-permute-start | bytes 196616 | tf_op jit(solution)/shard_map/ppermute | solution.py:487
  10.0 0.5 %collective-permute-start.5 = (bf16[2,128,128]{2,1,0:T(8,128)(2,1)S(1)}, bf16[2,128,128]{2,1,0:T(8,128)(2,1)S(1)}, u32[]{:S(2)}, u32[]{:S(2)}) collective-permute-start(bf16[2,128,128]{2,1,0:T(8,128)(2,1)S(1)} %get-tuple-element.19), channel_id=1, source_target_pairs={{0,4},{1,5},{2,6},{3,7},{4,0},{5,1},{6,2},{7,3},{8,12},{9,13},{10,... | collective-permute-start | bytes 196616 | tf_op jit(solution)/shard_map/ppermute | solution.py:487
  10.5 0.5 %collective-permute-start.4 = (bf16[2,128,128]{2,1,0:T(8,128)(2,1)S(1)}, bf16[2,128,128]{2,1,0:T(8,128)(2,1)S(1)}, u32[]{:S(2)}, u32[]{:S(2)}) collective-permute-start(bf16[2,128,128]{2,1,0:T(8,128)(2,1)S(1)} %get-tuple-element.19), channel_id=1, source_target_pairs={{0,2},{1,3},{2,0},{3,1},{4,6},{5,7},{6,4},{7,5},{8,10},{9,11},{10,... | collective-permute-start | bytes 196616 | tf_op jit(solution)/shard_map/ppermute | solution.py:487
  11.0 0.1 collective-permute-done.refs_3_
  11.1 0.1 broadcast_select_fusion
  11.2 3.6 %collective-permute-done.4 = bf16[2,128,128]{2,1,0:T(8,128)(2,1)S(1)} collective-permute-done((bf16[2,128,128]{2,1,0:T(8,128)(2,1)S(1)}, bf16[2,128,128]{2,1,0:T(8,128)(2,1)S(1)}, u32[]{:S(2)}, u32[]{:S(2)}) %collective-permute-start.4) | collective-permute-done | bytes 65568 | tf_op jit(solution)/shard_map/ppermute | solution.py:487
  14.8 0.1 collective-permute-start.7
  14.9 0.1 maximum_maximum_fusion
  15.0 0.5 %collective-permute-start.1 = (bf16[224,128]{1,0:T(8,128)(2,1)S(1)}, bf16[224,128]{1,0:T(8,128)(2,1)S(1)}, u32[]{:S(2)}, u32[]{:S(2)}) collective-permute-start(bf16[224,128]{1,0:T(8,128)(2,1)S(1)} %maximum_maximum_fusion), channel_id=1, source_target_pairs={{0,1},{1,0},{2,3},{3,2},{4,5},{5,4},{6,7},{7,6},{8,9},{9,8},{10,11... | collective-permute-start | bytes 172040 | tf_op jit(solution)/shard_map/ppermute | solution.py:487
  15.5 0.1 maximum_maximum_fusion.1
  15.6 4.5 %collective-permute-start.2 = (bf16[224,128]{1,0:T(8,128)(2,1)S(1)}, bf16[224,128]{1,0:T(8,128)(2,1)S(1)}, u32[]{:S(2)}, u32[]{:S(2)}) collective-permute-start(bf16[224,128]{1,0:T(8,128)(2,1)S(1)} %maximum_maximum_fusion.1), channel_id=1, source_target_pairs={{0,15},{1,2},{2,1},{3,4},{4,3},{5,6},{6,5},{7,8},{8,7},{9,10},{10,... | collective-permute-start | bytes 172040 | tf_op jit(solution)/shard_map/ppermute | solution.py:487
  20.0 1.0 %shard_map.149.refs_4_ = f32[4,256,256]{2,1,0:T(8,128)S(1)} custom-call(f32[1,16]{1,0:T(1,128)S(1)} %get-tuple-element.16.defocus), custom_call_target="tpu_custom_call" | custom-call | tf_op jit(solution)/shard_map/pallas_call | solution.py:421
  21.0 0.9 %collective-permute-done.2.refs_2_ = bf16[224,128]{1,0:T(8,128)(2,1)S(1)} collective-permute-done((bf16[224,128]{1,0:T(8,128)(2,1)S(1)}, bf16[224,128]{1,0:T(8,128)(2,1)S(1)}, u32[]{:S(2)}, u32[]{:S(2)}) %collective-permute-start.2) | collective-permute-done | bytes 57376 | tf_op jit(solution)/shard_map/ppermute | solution.py:487
  21.9 0.0 copy-start
  22.0 0.7 %shard_map.150.wide = f32[4,256,256]{2,1,0:T(8,128)S(1)} custom-call(bf16[384,384]{1,0:T(8,128)(2,1)S(1)} %get-tuple-element.12.refs_0_, bf16[224,128]{1,0:T(8,128)(2,1)S(1)} %collective-permute-done.1.refs_1_, bf16[224,128]{1,0:T(8,128)(2,1)S(1)} %collective-permute-done.2.refs_2_, bf16[64,384]{1,0:T(8,128)(2,1)S(1)} %collective-permute-done.refs_3_, ...), custom_call_target="tpu_custom_call" | custom-call | tf_op jit(solution)/shard_map/pallas_call | solution.py:421
  22.6 0.3 %copy-done = bf16[1024,256]{1,0:T(8,128)(2,1)S(1)} copy-done((bf16[1024,256]{1,0:T(8,128)(2,1)S(1)}, bf16[1024,256]{1,0:T(8,128)(2,1)}, u32[]{:S(2)}) %copy-start) | copy-done | bytes 524312
  22.9 0.0 copy-done.5
  23.0 0.0 copy-done.6
  23.0 0.0 copy-done.7
  23.1 4.4 %shard_map.151 = (f32[1,384,384]{2,1,0:T(8,128)}, f32[1,384,384]{2,1,0:T(8,128)}, f32[1,384,384]{2,1,0:T(8,128)}) custom-call(s32[4,16]{1,0:T(4,128)S(1)} %get-tuple-element.10.orients, s32[1,16]{1,0:T(1,128)S(1)} %get-tuple-element.11.lengths, f32[4,256,256]{2,1,0:T(8,128)S(1)} %shard_map.150.wide, ...), custom_call_target="tpu_custom_call" | custom-call | tf_op jit(solution)/shard_map/pallas_call | solution.py:421
  (23 shorter events, 0.1 us)
Async XLA Ops:
  0.6 6.6 %collective-permute-start.3 = (bf16[1,128,128]{2,1,0:T(8,128)(2,1)}, bf16[1,128,128]{2,1,0:T(8,128)(2,1)S(1)}, u32[]{:S(2)}, u32[]{:S(2)}) collective-permute-start(bf16[1,128,128]{2,1,0:T(8,128)(2,1)} %param.14), channel_id=1, source_target_pairs={{0,8},{1,9},{2,10},{3,11},{4,12},{5,13},{6,14},{7,15},{8,0},{9,1},... | collective-permute-start | bytes 98312 | tf_op jit(solution)/shard_map/ppermute | solution.py:487
  4.8 1.2 %copy-start.8 = (bf16[1,128,128]{2,1,0:T(8,128)(2,1)S(1)}, bf16[1,128,128]{2,1,0:T(8,128)(2,1)}, u32[]{:S(2)}) copy-start(bf16[1,128,128]{2,1,0:T(8,128)(2,1)} %param.14) | copy-start | bytes 98308
  5.9 5.2 %collective-permute-start = (bf16[64,384]{1,0:T(8,128)(2,1)S(1)}, bf16[64,384]{1,0:T(8,128)(2,1)S(1)}, u32[]{:S(2)}, u32[]{:S(2)}) collective-permute-start(bf16[64,384]{1,0:T(8,128)(2,1)S(1)} %get-tuple-element.14), channel_id=1, source_target_pairs={{0,8},{1,9},{2,10},{3,11},{4,12},{5,13},{6,14},{7,15},{8,0},{9,1},... | collective-permute-start | bytes 147464 | tf_op jit(solution)/shard_map/ppermute | solution.py:487
  7.2 7.6 %collective-permute-start.6 = (bf16[2,128,128]{2,1,0:T(8,128)(2,1)S(1)}, bf16[2,128,128]{2,1,0:T(8,128)(2,1)S(1)}, u32[]{:S(2)}, u32[]{:S(2)}) collective-permute-start(bf16[2,128,128]{2,1,0:T(8,128)(2,1)S(1)} %get-tuple-element.19), channel_id=1, source_target_pairs={{0,6},{1,7},{2,4},{3,5},{4,2},{5,3},{6,0},{7,1},{8,14},{9,15},{10,... | collective-permute-start | bytes 196616 | tf_op jit(solution)/shard_map/ppermute | solution.py:487
  10.0 4.8 %collective-permute-start.5 = (bf16[2,128,128]{2,1,0:T(8,128)(2,1)S(1)}, bf16[2,128,128]{2,1,0:T(8,128)(2,1)S(1)}, u32[]{:S(2)}, u32[]{:S(2)}) collective-permute-start(bf16[2,128,128]{2,1,0:T(8,128)(2,1)S(1)} %get-tuple-element.19), channel_id=1, source_target_pairs={{0,4},{1,5},{2,6},{3,7},{4,0},{5,1},{6,2},{7,3},{8,12},{9,13},{10,... | collective-permute-start | bytes 196616 | tf_op jit(solution)/shard_map/ppermute | solution.py:487
  10.5 4.3 %collective-permute-start.4 = (bf16[2,128,128]{2,1,0:T(8,128)(2,1)S(1)}, bf16[2,128,128]{2,1,0:T(8,128)(2,1)S(1)}, u32[]{:S(2)}, u32[]{:S(2)}) collective-permute-start(bf16[2,128,128]{2,1,0:T(8,128)(2,1)S(1)} %get-tuple-element.19), channel_id=1, source_target_pairs={{0,2},{1,3},{2,0},{3,1},{4,6},{5,7},{6,4},{7,5},{8,10},{9,11},{10,... | collective-permute-start | bytes 196616 | tf_op jit(solution)/shard_map/ppermute | solution.py:487
  14.8 7.8 %collective-permute-start.7 = (bf16[8,128,128]{2,1,0:T(8,128)(2,1)S(1)}, bf16[8,128,128]{2,1,0:T(8,128)(2,1)S(1)}, u32[]{:S(2)}, u32[]{:S(2)}) collective-permute-start(bf16[8,128,128]{2,1,0:T(8,128)(2,1)S(1)} %constant_dynamic-update-slice_fusion.2.near_ref), channel_id=1, source_target_pairs={{0,1},{1,0},{2,3},{3,2},{4,5},{5,4},{6,7},{7,6},{8,9},{9,8},{10,11... | collective-permute-start | bytes 786440 | tf_op jit(solution)/shard_map/ppermute | solution.py:487
  15.0 6.0 %collective-permute-start.1 = (bf16[224,128]{1,0:T(8,128)(2,1)S(1)}, bf16[224,128]{1,0:T(8,128)(2,1)S(1)}, u32[]{:S(2)}, u32[]{:S(2)}) collective-permute-start(bf16[224,128]{1,0:T(8,128)(2,1)S(1)} %maximum_maximum_fusion), channel_id=1, source_target_pairs={{0,1},{1,0},{2,3},{3,2},{4,5},{5,4},{6,7},{7,6},{8,9},{9,8},{10,11... | collective-permute-start | bytes 172040 | tf_op jit(solution)/shard_map/ppermute | solution.py:487
  15.6 6.3 %collective-permute-start.2 = (bf16[224,128]{1,0:T(8,128)(2,1)S(1)}, bf16[224,128]{1,0:T(8,128)(2,1)S(1)}, u32[]{:S(2)}, u32[]{:S(2)}) collective-permute-start(bf16[224,128]{1,0:T(8,128)(2,1)S(1)} %maximum_maximum_fusion.1), channel_id=1, source_target_pairs={{0,15},{1,2},{2,1},{3,4},{4,3},{5,6},{6,5},{7,8},{8,7},{9,10},{10,... | collective-permute-start | bytes 172040 | tf_op jit(solution)/shard_map/ppermute | solution.py:487
  20.0 1.9 %copy-start.1 = (bf16[256,256]{1,0:T(8,128)(2,1)S(1)}, bf16[256,256]{1,0:T(8,128)(2,1)}, u32[]{:S(2)}) copy-start(bf16[256,256]{1,0:T(8,128)(2,1)} %constant.35.clone.refs_6_.fwd_o) | copy-start | bytes 393220
  20.0 1.9 %copy-start.2 = (bf16[256,256]{1,0:T(8,128)(2,1)S(1)}, bf16[256,256]{1,0:T(8,128)(2,1)}, u32[]{:S(2)}) copy-start(bf16[256,256]{1,0:T(8,128)(2,1)} %constant.34.clone.refs_5_.fwd_e) | copy-start | bytes 393220
  20.0 1.9 %copy-start.3 = (bf16[256,256]{1,0:T(8,128)(2,1)S(1)}, bf16[256,256]{1,0:T(8,128)(2,1)}, u32[]{:S(2)}) copy-start(bf16[256,256]{1,0:T(8,128)(2,1)} %constant.37.clone.refs_8_) | copy-start | bytes 393220
  20.0 1.9 %copy-start.4 = (bf16[256,256]{1,0:T(8,128)(2,1)S(1)}, bf16[256,256]{1,0:T(8,128)(2,1)}, u32[]{:S(2)}) copy-start(bf16[256,256]{1,0:T(8,128)(2,1)} %constant.36.clone.refs_7_) | copy-start | bytes 393220
  21.9 1.0 %copy-start = (bf16[1024,256]{1,0:T(8,128)(2,1)S(1)}, bf16[1024,256]{1,0:T(8,128)(2,1)}, u32[]{:S(2)}) copy-start(bf16[1024,256]{1,0:T(8,128)(2,1)} %constant.41.clone.temp_cols) | copy-start | bytes 1572868
  21.9 1.1 %copy-start.5 = (bf16[128,512]{1,0:T(8,128)(2,1)S(1)}, bf16[128,512]{1,0:T(8,128)(2,1)}, u32[]{:S(2)}) copy-start(bf16[128,512]{1,0:T(8,128)(2,1)} %constant.40.clone.temp_rows) | copy-start | bytes 393220
  21.9 1.1 %copy-start.6 = (bf16[256,256]{1,0:T(8,128)(2,1)S(1)}, bf16[256,256]{1,0:T(8,128)(2,1)}, u32[]{:S(2)}) copy-start(bf16[256,256]{1,0:T(8,128)(2,1)} %constant.39.clone.inv_o) | copy-start | bytes 393220
  21.9 1.1 %copy-start.7 = (bf16[256,256]{1,0:T(8,128)(2,1)S(1)}, bf16[256,256]{1,0:T(8,128)(2,1)}, u32[]{:S(2)}) copy-start(bf16[256,256]{1,0:T(8,128)(2,1)} %constant.38.clone.inv_e) | copy-start | bytes 393220

commit v2 on v1

--- a/solution.py
+++ b/solution.py
@@ -239,31 +239,17 @@
         step()
 
 
-def match_kernel(
-    orients, lengths, wide, near_ref, far_ref,
-    fwd_e, fwd_o, inv_e, inv_o, temp_rows, temp_cols,
-    snr_ref, mean_ref, var_ref,
-    filt, proj, mixed, combos, out_buf, out_sem,
-):
+def project_kernel(orients, lengths, near_ref, far_ref, temp_rows, temp_cols, proj, edges):
     me = lax.axis_index("tile")
-    half = wide.shape[1]
+    half = temp_cols.shape[1]
     lane = half // 2
-    centre = out_buf.shape[1]
     box = near_ref.shape[1]
-    strip = combos.shape[3] // LMAX
     tile_count = lax.axis_size("tile")
     distances = flips(tile_count)
     held = near_ref.shape[0] // (tile_count // 2)
     count = lengths[0, me]
-    bf16, f32 = jnp.bfloat16, jnp.float32
-    step = 16
-    col_first = lax.broadcasted_iota(jnp.int32, (step, half), 1) == 0
-    row_first = lax.broadcasted_iota(jnp.int32, (step, half), 0) == 0
-    corner = col_first & row_first
-    thin_first = col_first.astype(f32).astype(bf16) > 0
-    sign = 1.0 - 2.0 * (lax.broadcasted_iota(jnp.int32, (box, lane), 0) % 2).astype(f32)
+    sign = 1.0 - 2.0 * (lax.broadcasted_iota(jnp.int32, (box, lane), 0) % 2).astype(jnp.float32)
     box_col = lax.broadcasted_iota(jnp.int32, (box, lane), 1) == 0
-    edges, waves_of = {}, {}
 
     def chosen(slot):
         orient = orients[slot, me]
@@ -276,29 +262,45 @@
             at = at + (lax.div(apart, distance) & 1) * (held << k)
         return jnp.where(apart & 1 == 1, far_ref[at], near_ref[at])
 
-    def project(slot):
-        def rows():
-            waves = dot(chosen(slot), temp_rows[...])
-            first_u, first_v = waves[:, :lane], waves[:, half : half + lane]
-            row_edge = -jnp.sum(first_u * sign, axis=0, keepdims=True)
-            col_edge = jnp.sum(first_v, axis=0, keepdims=True)
-            edges[slot] = (beside(row_edge, row_edge), beside(col_edge, col_edge))
-            v_part = beside(jnp.where(box_col, 0.0, first_v), waves[:, half + lane :])
-            u_minus = beside(jnp.where(box_col, first_v, first_u), waves[:, lane:half])
-            plus = jnp.concatenate([waves[:, :half], v_part], axis=0).astype(bf16)
-            minus = jnp.concatenate([u_minus, v_part], axis=0).astype(bf16)
-            waves_of[slot] = (plus, plus, minus, minus)
-
-        def cols(k):
+    for slot in range(LMAX):
+        waves = dot(chosen(slot), temp_rows[...])
+        first_u, first_v = waves[:, :lane], waves[:, half : half + lane]
+        row_edge = -jnp.sum(first_u * sign, axis=0, keepdims=True)
+        col_edge = jnp.sum(first_v, axis=0, keepdims=True)
+        edges[slot, :1] = beside(row_edge, row_edge)
+        edges[slot, 1:2] = beside(col_edge, col_edge)
+        v_part = beside(jnp.where(box_col, 0.0, first_v), waves[:, half + lane :])
+        u_minus = beside(jnp.where(box_col, first_v, first_u), waves[:, lane:half])
+        plus = jnp.concatenate([waves[:, :half], v_part], axis=0).astype(jnp.bfloat16)
+        minus = jnp.concatenate([u_minus, v_part], axis=0).astype(jnp.bfloat16)
+        for k, half_waves in enumerate((plus, plus, minus, minus)):
             here = slice(k * half, (k + 1) * half)
-            proj[slot % 2, here] = dot(temp_cols[here], waves_of[slot][k]).astype(bf16)
-
-        return [rows] + [functools.partial(cols, k) for k in range(4)]
+            proj[slot, here] = dot(temp_cols[here], half_waves).astype(jnp.bfloat16)
+
+
+def match_kernel(
+    lengths, wide, proj, edges,
+    fwd_e, fwd_o, inv_e, inv_o,
+    snr_ref, mean_ref, var_ref,
+    filt, mixed, combos, out_buf, out_sem,
+):
+    me = lax.axis_index("tile")
+    half = wide.shape[1]
+    lane = half // 2
+    centre = out_buf.shape[1]
+    strip = combos.shape[3] // LMAX
+    count = lengths[0, me]
+    bf16, f32 = jnp.bfloat16, jnp.float32
+    step = 16
+    col_first = lax.broadcasted_iota(jnp.int32, (step, half), 1) == 0
+    row_first = lax.broadcasted_iota(jnp.int32, (step, half), 0) == 0
+    corner = col_first & row_first
+    thin_first = col_first.astype(f32).astype(bf16) > 0
 
     def mix_first(slot, fs, ps):
         fpr, fpi, fmr, fmi = (f.astype(f32) for f in fs)
         ppr, ppi, pmr, pmi = (p.astype(f32) for p in ps)
-        row_edge, col_edge = edges[slot]
+        row_edge, col_edge = edges[slot, :1], edges[slot, 1:2]
         ppi = jnp.where(corner, row_edge, ppi)
         pmi = jnp.where(corner, pmr, pmi)
         pmr = jnp.where(corner, col_edge, pmr)
@@ -321,7 +323,7 @@
         row_odd, at = start // lane, start % lane
         buffer = slot % 2
         fs = [filt[k, start : start + step] for k in range(4)]
-        ps = [proj[buffer, k * half + start : k * half + start + step] for k in range(4)]
+        ps = [proj[slot, k * half + start : k * half + start + step] for k in range(4)]
         if start == 0:
             cos_r, sin_r, cos_i, sin_i = mix_first(slot, fs, ps)
         else:
@@ -354,7 +356,7 @@
                     combos[0, imag, start // strip + k, place] = piece[:, :lane]
                     combos[1, imag, start // strip + k, place] = piece[:, lane:]
 
-        return [functools.partial(rows, imag, first) for imag in range(2) for first in range(half // lane)]
+        return [functools.partial(rows, imag, first) for first in range(half // lane) for imag in range(2)]
 
     share = 1.0 / jnp.full((1, 1), count, jnp.int32).astype(f32)
     shares = [jnp.where(slot < count, share, 0.0) for slot in range(LMAX)]
@@ -392,18 +394,18 @@
         for k in range(4):
             filt[k] = wide[k].astype(bf16)
 
-    parts = centre // strip
-    for tick in range(LMAX + 2):
-        products = project(tick) if tick < LMAX else []
-        if 0 <= tick - 2:
-            products = products + combine(tick - 2)
-        sums = [thin] if tick == 0 else []
-        if 0 <= tick - 1 < LMAX:
-            sums = [functools.partial(mix, tick - 1, start) for start in range(0, half, step)]
-        weave(products, sums)
-    for part in range(parts):
-        back(part)
-        gather(part)
+    thin()
+    for tick in range(LMAX):
+        products = combine(tick - 1) if tick else []
+        weave(products, [functools.partial(mix, tick, start) for start in range(0, half, step)])
+    last = combine(LMAX - 1)
+    for first in range(half // lane):
+        for _ in range(2):
+            last.pop(0)()
+        for start in range(first * lane, centre, half):
+            for part in range(start // strip, (start + lane) // strip):
+                back(part)
+                gather(part)
     for copy in out_copies:
         copy.wait()
 
@@ -451,22 +453,27 @@
     return filt
 
 
-def match(orient_list, lengths, filt, near, far, tables, centre):
+def project(orient_list, lengths, near, far, tables, extent):
+    half = extent // 2
+    outs = (((LMAX, 2 * extent, half), jnp.bfloat16), ((LMAX, 8, half), jnp.float32))
+    return vmem_call(project_kernel, (orient_list, lengths, near, far, *tables[6:]), outs, [], 2, 12)
+
+
+def match(lengths, filt, proj, edges, tables, centre):
     half = filt.shape[1]
-    lane, extent = half // 2, 2 * half
+    lane = half // 2
     strip = lane // 2
     out = ((1, centre, centre), jnp.float32)
     return vmem_call(
-        match_kernel, (orient_list, lengths, filt, near, far, *tables[:2], *tables[4:]), (out, out, out),
+        match_kernel, (lengths, filt, proj, edges, *tables[:2], *tables[4:6]), (out, out, out),
         [
             pltpu.VMEM((4, half, half), jnp.bfloat16),
-            pltpu.VMEM((2, 2 * extent, half), jnp.bfloat16),
             pltpu.VMEM((2, 2, 2, half, half), jnp.bfloat16),
             pltpu.VMEM((2, 2, centre // strip, LMAX * strip, lane), jnp.bfloat16),
             pltpu.VMEM((3, centre, centre), jnp.float32),
             pltpu.SemaphoreType.DMA((3, centre // strip)),
         ],
-        2, 24, pl.ANY,
+        1, 20, pl.ANY,
     )
 
 
@@ -510,6 +517,7 @@
         from_mate = send(strip(to_mate, odd), lambda i: i ^ 1)
         near = jnp.concatenate([group[0], group[2], group[3], group[1]], axis=0)
         far = send(near, lambda i: i ^ 1)
+        proj, edges = project(orients, counts, near, far, tables, extent)
         filt = tile_spectrum(True, (block, from_mate, from_peer, ends), weights, tables, extent)
     else:
 
@@ -535,8 +543,9 @@
         for distance in flips(tile_count)[:-1]:
             near = jnp.concatenate([near, send(near, lambda i, d=distance: i ^ d)], axis=0)
         far = send(near, lambda i: i ^ 1)
+        proj, edges = project(orients, counts, near, far, tables, extent)
         filt = tile_spectrum(False, (centre_block, cols, rows), weights, tables, extent)
-    return match(orients, counts, filt, near, far, tables, centre)
+    return match(counts, filt, proj, edges, tables, centre)
 
 
 def solution(mesh):

time: 27.6 us -> 28.4 us (1.029)
  waiting for transfers between devices: 5.74 us -> 4.79 us
  Pallas kernels: 7.15 us -> 8.1 us
  starting transfers between devices: 13 us -> 13.4 us
  local copies, waits for them, and re-layouts: 0.51 us -> 0.88 us
    pallas_call x4 -> x5, Pallas kernels: 7.15 us -> 8.1 us  [vmem_call(): pl.pallas_call(kernel, out_shape=tuple((jax.ShapeDtypeStruct(shape, dtype...]
    ppermute x8, waiting for transfers between devices: 5.74 us -> 4.79 us  [send(): lax.ppermute(block, 'tile', [(i, target(i)) for i in range(tile_count)])]
    unnamed x21 -> x19, local copies, waits for them, and re-layouts: 0.48 us -> 0.84 us
    ppermute x8, starting transfers between devices: 13 us -> 13.4 us  [send(): lax.ppermute(block, 'tile', [(i, target(i)) for i in range(tile_count)])]
  transfers between devices with their start and end apart: 8 -> 8, of which waited for: 4 -> 4; matrix products, arithmetic and copies ran while one was open for 1% -> 4% of each run, Pallas kernels for 10% -> 10%
where the time goes in v2:
time: 28.4 us; the launch traced here: 28.2 us
  starting transfers between devices  13.4 us (47%)
  Pallas kernels  8.1 us (29%)
  waiting for transfers between devices  4.79 us (17%)
  local copies, waits for them, and re-layouts  0.88 us (3%)
  between operations  0.83 us (3%)
    ppermute x8, starting transfers between devices, send(): lax.ppermute(block, 'tile', [(i, target(i)) for i in range(tile_count)])  13.4 us
    pallas_call x5, Pallas kernels, vmem_call(): pl.pallas_call(kernel, out_shape=tuple((jax.ShapeDtypeStruct(shape, dtype...  8.1 us
    ppermute x8, waiting for transfers between devices, send(): lax.ppermute(block, 'tile', [(i, target(i)) for i in range(tile_count)])  4.79 us
    unnamed x19, local copies, waits for them, and re-layouts  0.84 us
  transfers between devices with their start and end apart: 8, of which 4 were waited for; matrix products, arithmetic and copies ran while one was open for 4% of the time, Pallas kernels for 10%

profile of v2, /device:TPU:0, one launch (start us, length us, event | category | flops | bytes accessed | tf_op | source)
XLA Modules:
  0.0 28.2 jit_solution(7727686124170783349)
XLA Ops:
  0.6 0.0 copy-start
  0.6 0.0 copy-start.1
  0.7 0.0 copy-start.7
  0.7 4.1 %collective-permute-start.3 = (bf16[1,128,128]{2,1,0:T(8,128)(2,1)}, bf16[1,128,128]{2,1,0:T(8,128)(2,1)S(1)}, u32[]{:S(2)}, u32[]{:S(2)}) collective-permute-start(bf16[1,128,128]{2,1,0:T(8,128)(2,1)} %param.14), channel_id=1, source_target_pairs={{0,8},{1,9},{2,10},{3,11},{4,12},{5,13},{6,14},{7,15},{8,0},{9,1},... | collective-permute-start | bytes 98312 | tf_op jit(solution)/shard_map/ppermute | solution.py:494
  4.8 1.1 %shard_map.148 = (bf16[384,384]{1,0:T(8,128)(2,1)S(1)}, s32[4,16]{1,0:T(4,128)S(1)}, s32[1,16]{1,0:T(1,128)S(1)}, f32[1,16]{1,0:T(1,128)S(1)}, bf16[64,384]{1,0:...) custom-call(bf16[384,384]{1,0:T(8,128)(2,1)} %bitcast.4, s32[4,16]{1,0:T(4,128)} %bitcast.5, ...), custom_call_target="tpu_custom_call" | custom-call | tf_op jit(solution)/shard_map/pallas_call | solution.py:423
  5.9 0.2 collective-permute-start
  6.1 0.8 %constant_dynamic-update-slice_fusion.1 = (bf16[2,128,128]{2,1,0:T(8,128)(2,1)S(1)}, bf16[8,128,128]{2,1,0:T(8,128)(2,1)S(1)}) fusion(bf16[1,128,128]{2,1,0:T(8,128)(2,1)} %param.14), kind=kLoop, calls=%fused_computation.3 | loop fusion | bytes 98304
  6.9 0.3 %collective-permute-done.3 = bf16[1,128,128]{2,1,0:T(8,128)(2,1)S(1)} collective-permute-done((bf16[1,128,128]{2,1,0:T(8,128)(2,1)}, bf16[1,128,128]{2,1,0:T(8,128)(2,1)S(1)}, u32[]{:S(2)}, u32[]{:S(2)}) %collective-permute-start.3) | collective-permute-done | bytes 32800 | tf_op jit(solution)/shard_map/ppermute | solution.py:494
  7.3 2.8 %collective-permute-start.6 = (bf16[2,128,128]{2,1,0:T(8,128)(2,1)S(1)}, bf16[2,128,128]{2,1,0:T(8,128)(2,1)S(1)}, u32[]{:S(2)}, u32[]{:S(2)}) collective-permute-start(bf16[2,128,128]{2,1,0:T(8,128)(2,1)S(1)} %get-tuple-element.23), channel_id=1, source_target_pairs={{0,6},{1,7},{2,4},{3,5},{4,2},{5,3},{6,0},{7,1},{8,14},{9,15},{10,... | collective-permute-start | bytes 196616 | tf_op jit(solution)/shard_map/ppermute | solution.py:494
  10.1 0.4 %collective-permute-start.5 = (bf16[2,128,128]{2,1,0:T(8,128)(2,1)S(1)}, bf16[2,128,128]{2,1,0:T(8,128)(2,1)S(1)}, u32[]{:S(2)}, u32[]{:S(2)}) collective-permute-start(bf16[2,128,128]{2,1,0:T(8,128)(2,1)S(1)} %get-tuple-element.23), channel_id=1, source_target_pairs={{0,4},{1,5},{2,6},{3,7},{4,0},{5,1},{6,2},{7,3},{8,12},{9,13},{10,... | collective-permute-start | bytes 196616 | tf_op jit(solution)/shard_map/ppermute | solution.py:494
  10.5 0.6 %collective-permute-start.4 = (bf16[2,128,128]{2,1,0:T(8,128)(2,1)S(1)}, bf16[2,128,128]{2,1,0:T(8,128)(2,1)S(1)}, u32[]{:S(2)}, u32[]{:S(2)}) collective-permute-start(bf16[2,128,128]{2,1,0:T(8,128)(2,1)S(1)} %get-tuple-element.23), channel_id=1, source_target_pairs={{0,2},{1,3},{2,0},{3,1},{4,6},{5,7},{6,4},{7,5},{8,10},{9,11},{10,... | collective-permute-start | bytes 196616 | tf_op jit(solution)/shard_map/ppermute | solution.py:494
  11.2 0.1 collective-permute-done.refs_3_
  11.2 0.1 broadcast_select_fusion
  11.3 3.5 %collective-permute-done.4 = bf16[2,128,128]{2,1,0:T(8,128)(2,1)S(1)} collective-permute-done((bf16[2,128,128]{2,1,0:T(8,128)(2,1)S(1)}, bf16[2,128,128]{2,1,0:T(8,128)(2,1)S(1)}, u32[]{:S(2)}, u32[]{:S(2)}) %collective-permute-start.4) | collective-permute-done | bytes 65568 | tf_op jit(solution)/shard_map/ppermute | solution.py:494
  14.9 0.1 collective-permute-start.7
  15.0 0.1 maximum_maximum_fusion
  15.0 0.5 %collective-permute-start.1 = (bf16[224,128]{1,0:T(8,128)(2,1)S(1)}, bf16[224,128]{1,0:T(8,128)(2,1)S(1)}, u32[]{:S(2)}, u32[]{:S(2)}) collective-permute-start(bf16[224,128]{1,0:T(8,128)(2,1)S(1)} %maximum_maximum_fusion), channel_id=1, source_target_pairs={{0,1},{1,0},{2,3},{3,2},{4,5},{5,4},{6,7},{7,6},{8,9},{9,8},{10,11... | collective-permute-start | bytes 172040 | tf_op jit(solution)/shard_map/ppermute | solution.py:494
  15.5 0.1 maximum_maximum_fusion.1
  15.6 4.6 %collective-permute-start.2 = (bf16[224,128]{1,0:T(8,128)(2,1)S(1)}, bf16[224,128]{1,0:T(8,128)(2,1)S(1)}, u32[]{:S(2)}, u32[]{:S(2)}) collective-permute-start(bf16[224,128]{1,0:T(8,128)(2,1)S(1)} %maximum_maximum_fusion.1), channel_id=1, source_target_pairs={{0,15},{1,2},{2,1},{3,4},{4,3},{5,6},{6,5},{7,8},{8,7},{9,10},{10,... | collective-permute-start | bytes 172040 | tf_op jit(solution)/shard_map/ppermute | solution.py:494
  20.2 1.0 %shard_map.149.refs_4_ = f32[4,256,256]{2,1,0:T(8,128)S(1)} custom-call(f32[1,16]{1,0:T(1,128)S(1)} %get-tuple-element.17.defocus), custom_call_target="tpu_custom_call" | custom-call | tf_op jit(solution)/shard_map/pallas_call | solution.py:423
  21.2 0.9 %collective-permute-done.2.refs_2_ = bf16[224,128]{1,0:T(8,128)(2,1)S(1)} collective-permute-done((bf16[224,128]{1,0:T(8,128)(2,1)S(1)}, bf16[224,128]{1,0:T(8,128)(2,1)S(1)}, u32[]{:S(2)}, u32[]{:S(2)}) %collective-permute-start.2) | collective-permute-done | bytes 57376 | tf_op jit(solution)/shard_map/ppermute | solution.py:494
  22.1 0.7 %shard_map.150.wide = f32[4,256,256]{2,1,0:T(8,128)S(1)} custom-call(bf16[384,384]{1,0:T(8,128)(2,1)S(1)} %get-tuple-element.13.refs_0_, bf16[224,128]{1,0:T(8,128)(2,1)S(1)} %collective-permute-done.1.refs_1_, bf16[224,128]{1,0:T(8,128)(2,1)S(1)} %collective-permute-done.2.refs_2_, bf16[64,384]{1,0:T(8,128)(2,1)S(1)} %collective-permute-done.refs_3_, ...), custom_call_target="tpu_custom_call" | custom-call | tf_op jit(solution)/shard_map/pallas_call | solution.py:423
  22.8 2.0 %shard_map.151 = (bf16[4,1024,256]{2,1,0:T(8,128)(2,1)S(1)}, f32[4,8,256]{2,1,0:T(8,128)S(1)}) custom-call(s32[4,16]{1,0:T(4,128)S(1)} %get-tuple-element.18.orients, s32[1,16]{1,0:T(1,128)S(1)} %get-tuple-element.12.lengths, bf16[8,128,128]{2,1,0:T(8,128)(2,1)S(1)} %constant_dynamic-update-slice_fusion.2.near_ref, ...), custom_call_target="tpu_custom_call" | custom-call | tf_op jit(solution)/shard_map/pallas_call | solution.py:423
  24.8 3.4 %shard_map.152 = (f32[1,384,384]{2,1,0:T(8,128)}, f32[1,384,384]{2,1,0:T(8,128)}, f32[1,384,384]{2,1,0:T(8,128)}) custom-call(s32[1,16]{1,0:T(1,128)S(1)} %get-tuple-element.12.lengths, f32[4,256,256]{2,1,0:T(8,128)S(1)} %shard_map.150.wide, bf16[4,1024,256]{2,1,0:T(8,128)(2,1)S(1)} %get-tuple-element.19.proj, f32[4,8,256]{2,1,0:T(8,128)S(1)} %get-tuple-element.20.edges, ...), custom_call_target="tpu_custom_call" | custom-call | tf_op jit(solution)/shard_map/pallas_call | solution.py:423
  (22 shorter events, 0.1 us)
Async XLA Ops:
  0.6 21.5 %copy-start = (bf16[256,256]{1,0:T(8,128)(2,1)S(1)}, bf16[256,256]{1,0:T(8,128)(2,1)}, u32[]{:S(2)}) copy-start(bf16[256,256]{1,0:T(8,128)(2,1)} %constant.35.clone.refs_6_.fwd_o) | copy-start | bytes 393220
  0.6 21.4 %copy-start.1 = (bf16[256,256]{1,0:T(8,128)(2,1)S(1)}, bf16[256,256]{1,0:T(8,128)(2,1)}, u32[]{:S(2)}) copy-start(bf16[256,256]{1,0:T(8,128)(2,1)} %constant.34.clone.refs_5_.fwd_e) | copy-start | bytes 393220
  0.7 21.4 %copy-start.6 = (bf16[256,256]{1,0:T(8,128)(2,1)S(1)}, bf16[256,256]{1,0:T(8,128)(2,1)}, u32[]{:S(2)}) copy-start(bf16[256,256]{1,0:T(8,128)(2,1)} %constant.37.clone.refs_8_) | copy-start | bytes 393220
  0.7 21.4 %copy-start.7 = (bf16[256,256]{1,0:T(8,128)(2,1)S(1)}, bf16[256,256]{1,0:T(8,128)(2,1)}, u32[]{:S(2)}) copy-start(bf16[256,256]{1,0:T(8,128)(2,1)} %constant.36.clone.refs_7_) | copy-start | bytes 393220
  0.7 6.6 %collective-permute-start.3 = (bf16[1,128,128]{2,1,0:T(8,128)(2,1)}, bf16[1,128,128]{2,1,0:T(8,128)(2,1)S(1)}, u32[]{:S(2)}, u32[]{:S(2)}) collective-permute-start(bf16[1,128,128]{2,1,0:T(8,128)(2,1)} %param.14), channel_id=1, source_target_pairs={{0,8},{1,9},{2,10},{3,11},{4,12},{5,13},{6,14},{7,15},{8,0},{9,1},... | collective-permute-start | bytes 98312 | tf_op jit(solution)/shard_map/ppermute | solution.py:494
  5.9 5.3 %collective-permute-start = (bf16[64,384]{1,0:T(8,128)(2,1)S(1)}, bf16[64,384]{1,0:T(8,128)(2,1)S(1)}, u32[]{:S(2)}, u32[]{:S(2)}) collective-permute-start(bf16[64,384]{1,0:T(8,128)(2,1)S(1)} %get-tuple-element.15), channel_id=1, source_target_pairs={{0,8},{1,9},{2,10},{3,11},{4,12},{5,13},{6,14},{7,15},{8,0},{9,1},... | collective-permute-start | bytes 147464 | tf_op jit(solution)/shard_map/ppermute | solution.py:494
  7.3 7.6 %collective-permute-start.6 = (bf16[2,128,128]{2,1,0:T(8,128)(2,1)S(1)}, bf16[2,128,128]{2,1,0:T(8,128)(2,1)S(1)}, u32[]{:S(2)}, u32[]{:S(2)}) collective-permute-start(bf16[2,128,128]{2,1,0:T(8,128)(2,1)S(1)} %get-tuple-element.23), channel_id=1, source_target_pairs={{0,6},{1,7},{2,4},{3,5},{4,2},{5,3},{6,0},{7,1},{8,14},{9,15},{10,... | collective-permute-start | bytes 196616 | tf_op jit(solution)/shard_map/ppermute | solution.py:494
  10.1 4.7 %collective-permute-start.5 = (bf16[2,128,128]{2,1,0:T(8,128)(2,1)S(1)}, bf16[2,128,128]{2,1,0:T(8,128)(2,1)S(1)}, u32[]{:S(2)}, u32[]{:S(2)}) collective-permute-start(bf16[2,128,128]{2,1,0:T(8,128)(2,1)S(1)} %get-tuple-element.23), channel_id=1, source_target_pairs={{0,4},{1,5},{2,6},{3,7},{4,0},{5,1},{6,2},{7,3},{8,12},{9,13},{10,... | collective-permute-start | bytes 196616 | tf_op jit(solution)/shard_map/ppermute | solution.py:494
  10.5 4.3 %collective-permute-start.4 = (bf16[2,128,128]{2,1,0:T(8,128)(2,1)S(1)}, bf16[2,128,128]{2,1,0:T(8,128)(2,1)S(1)}, u32[]{:S(2)}, u32[]{:S(2)}) collective-permute-start(bf16[2,128,128]{2,1,0:T(8,128)(2,1)S(1)} %get-tuple-element.23), channel_id=1, source_target_pairs={{0,2},{1,3},{2,0},{3,1},{4,6},{5,7},{6,4},{7,5},{8,10},{9,11},{10,... | collective-permute-start | bytes 196616 | tf_op jit(solution)/shard_map/ppermute | solution.py:494
  14.9 7.9 %collective-permute-start.7 = (bf16[8,128,128]{2,1,0:T(8,128)(2,1)S(1)}, bf16[8,128,128]{2,1,0:T(8,128)(2,1)S(1)}, u32[]{:S(2)}, u32[]{:S(2)}) collective-permute-start(bf16[8,128,128]{2,1,0:T(8,128)(2,1)S(1)} %constant_dynamic-update-slice_fusion.2.near_ref), channel_id=1, source_target_pairs={{0,1},{1,0},{2,3},{3,2},{4,5},{5,4},{6,7},{7,6},{8,9},{9,8},{10,11... | collective-permute-start | bytes 786440 | tf_op jit(solution)/shard_map/ppermute | solution.py:494
  15.0 6.2 %collective-permute-start.1 = (bf16[224,128]{1,0:T(8,128)(2,1)S(1)}, bf16[224,128]{1,0:T(8,128)(2,1)S(1)}, u32[]{:S(2)}, u32[]{:S(2)}) collective-permute-start(bf16[224,128]{1,0:T(8,128)(2,1)S(1)} %maximum_maximum_fusion), channel_id=1, source_target_pairs={{0,1},{1,0},{2,3},{3,2},{4,5},{5,4},{6,7},{7,6},{8,9},{9,8},{10,11... | collective-permute-start | bytes 172040 | tf_op jit(solution)/shard_map/ppermute | solution.py:494
  15.6 7.2 %copy-start.2 = (bf16[1024,256]{1,0:T(8,128)(2,1)S(1)}, bf16[1024,256]{1,0:T(8,128)(2,1)}, u32[]{:S(2)}) copy-start(bf16[1024,256]{1,0:T(8,128)(2,1)} %constant.41.clone.temp_cols) | copy-start | bytes 1572868
  15.6 7.2 %copy-start.5 = (bf16[128,512]{1,0:T(8,128)(2,1)S(1)}, bf16[128,512]{1,0:T(8,128)(2,1)}, u32[]{:S(2)}) copy-start(bf16[128,512]{1,0:T(8,128)(2,1)} %constant.40.clone.temp_rows) | copy-start | bytes 393220
  15.6 6.5 %collective-permute-start.2 = (bf16[224,128]{1,0:T(8,128)(2,1)S(1)}, bf16[224,128]{1,0:T(8,128)(2,1)S(1)}, u32[]{:S(2)}, u32[]{:S(2)}) collective-permute-start(bf16[224,128]{1,0:T(8,128)(2,1)S(1)} %maximum_maximum_fusion.1), channel_id=1, source_target_pairs={{0,15},{1,2},{2,1},{3,4},{4,3},{5,6},{6,5},{7,8},{8,7},{9,10},{10,... | collective-permute-start | bytes 172040 | tf_op jit(solution)/shard_map/ppermute | solution.py:494
  22.1 2.7 %copy-start.3 = (bf16[256,256]{1,0:T(8,128)(2,1)S(1)}, bf16[256,256]{1,0:T(8,128)(2,1)}, u32[]{:S(2)}) copy-start(bf16[256,256]{1,0:T(8,128)(2,1)} %constant.39.clone.inv_o) | copy-start | bytes 393220
  22.1 2.7 %copy-start.4 = (bf16[256,256]{1,0:T(8,128)(2,1)S(1)}, bf16[256,256]{1,0:T(8,128)(2,1)}, u32[]{:S(2)}) copy-start(bf16[256,256]{1,0:T(8,128)(2,1)} %constant.38.clone.inv_e) | copy-start | bytes 393220

commit v3 on v1

--- a/solution.py
+++ b/solution.py
@@ -95,8 +95,8 @@
 
 
 def pack_kernel(*refs):
-    sources, held, (ends_ref, mate_ref, peer_ref, sem) = refs[:4], refs[4:8], refs[8:]
-    copies = [pltpu.make_async_copy(sources[k], held[k], sem.at[k]) for k in range(4)]
+    sources, held, (ends_ref, mate_ref, peer_ref, sem) = refs[:5], refs[5:10], refs[10:]
+    copies = [pltpu.make_async_copy(sources[k], held[k], sem.at[k]) for k in range(5)]
     for copy in copies:
         copy.start()
     me = lax.axis_index("tile")
@@ -183,7 +183,8 @@
     else:
         centre_ref, cols_ref, rows_ref, weight_ref = refs[:4]
         refs = refs[4:]
-    fwd_e, fwd_o, fwd_et, fwd_ot, filt, uv = refs
+    fwd_e, fwd_o, fwd_et, fwd_ot = refs[:4]
+    filt, uv = refs[-2:]
     centre, extent = centre_ref.shape[0], uv.shape[0]
     half, lane = extent // 2, extent // 4
     if paired:
@@ -243,7 +244,7 @@
     orients, lengths, wide, near_ref, far_ref,
     fwd_e, fwd_o, inv_e, inv_o, temp_rows, temp_cols,
     snr_ref, mean_ref, var_ref,
-    filt, proj, mixed, combos, out_buf, out_sem,
+    filt, waves, proj, mixed, combos, out_buf, out_sem,
 ):
     me = lax.axis_index("tile")
     half = wide.shape[1]
@@ -263,7 +264,7 @@
     thin_first = col_first.astype(f32).astype(bf16) > 0
     sign = 1.0 - 2.0 * (lax.broadcasted_iota(jnp.int32, (box, lane), 0) % 2).astype(f32)
     box_col = lax.broadcasted_iota(jnp.int32, (box, lane), 1) == 0
-    edges, waves_of = {}, {}
+    edges = {}
 
     def chosen(slot):
         orient = orients[slot, me]
@@ -276,24 +277,28 @@
             at = at + (lax.div(apart, distance) & 1) * (held << k)
         return jnp.where(apart & 1 == 1, far_ref[at], near_ref[at])
 
+    def rows_first():
+        stacked = jnp.concatenate([chosen(slot) for slot in range(LMAX)], axis=0)
+        first_u, rest_u = dot(stacked, temp_rows[:, :lane]), dot(stacked, temp_rows[:, lane:half])
+        first_v, rest_v = dot(stacked, temp_rows[:, half : half + lane]), dot(stacked, temp_rows[:, half + lane :])
+        for slot in range(LMAX):
+            rows = slice(slot * box, (slot + 1) * box)
+            u, v = first_u[rows], first_v[rows]
+            row_edge = -jnp.sum(u * sign, axis=0, keepdims=True)
+            col_edge = jnp.sum(v, axis=0, keepdims=True)
+            edges[slot] = (beside(row_edge, row_edge), beside(col_edge, col_edge))
+            v_part = beside(jnp.where(box_col, 0.0, v), rest_v[rows]).astype(bf16)
+            waves[slot, 0, :box] = beside(u, rest_u[rows]).astype(bf16)
+            waves[slot, 1, :box] = beside(jnp.where(box_col, v, u), rest_u[rows]).astype(bf16)
+            waves[slot, 0, box:] = v_part
+            waves[slot, 1, box:] = v_part
+
     def project(slot):
-        def rows():
-            waves = dot(chosen(slot), temp_rows[...])
-            first_u, first_v = waves[:, :lane], waves[:, half : half + lane]
-            row_edge = -jnp.sum(first_u * sign, axis=0, keepdims=True)
-            col_edge = jnp.sum(first_v, axis=0, keepdims=True)
-            edges[slot] = (beside(row_edge, row_edge), beside(col_edge, col_edge))
-            v_part = beside(jnp.where(box_col, 0.0, first_v), waves[:, half + lane :])
-            u_minus = beside(jnp.where(box_col, first_v, first_u), waves[:, lane:half])
-            plus = jnp.concatenate([waves[:, :half], v_part], axis=0).astype(bf16)
-            minus = jnp.concatenate([u_minus, v_part], axis=0).astype(bf16)
-            waves_of[slot] = (plus, plus, minus, minus)
-
         def cols(k):
             here = slice(k * half, (k + 1) * half)
-            proj[slot % 2, here] = dot(temp_cols[here], waves_of[slot][k]).astype(bf16)
-
-        return [rows] + [functools.partial(cols, k) for k in range(4)]
+            proj[slot % 2, here] = dot(temp_cols[here], waves[slot, k // 2]).astype(bf16)
+
+        return [functools.partial(cols, k) for k in range(4)]
 
     def mix_first(slot, fs, ps):
         fpr, fpi, fmr, fmi = (f.astype(f32) for f in fs)
@@ -332,17 +337,16 @@
             cos_r, sin_r = plus_r + minus_r, minus_i - plus_i
             cos_i, sin_i = plus_i + minus_i, plus_r - minus_r
             cos_i, sin_i = jnp.where(thin_first, sin_i, cos_i), jnp.where(thin_first, -cos_i, sin_i)
-        mixed[buffer, row_odd, 0, at : at + step] = cos_r
-        mixed[buffer, row_odd, 0, lane + at : lane + at + step] = sin_r
-        mixed[buffer, row_odd, 1, at : at + step] = cos_i
-        mixed[buffer, row_odd, 1, lane + at : lane + at + step] = sin_i
-
-    def combine(slot):
-        def rows(imag, first):
-            buffer = slot % 2
+        mixed[slot, row_odd, 0, at : at + step] = cos_r
+        mixed[slot, row_odd, 0, lane + at : lane + at + step] = sin_r
+        mixed[slot, row_odd, 1, at : at + step] = cos_i
+        mixed[slot, row_odd, 1, lane + at : lane + at + step] = sin_i
+
+    def combine(slot, first):
+        def rows(imag):
             here = slice(first * lane, (first + 1) * lane)
-            even = dot(fwd_e[here], mixed[buffer, 0, imag])
-            odd = dot(fwd_o[here], mixed[buffer, 1, imag])
+            even = dot(fwd_e[here], mixed[slot, 0, imag])
+            odd = dot(fwd_o[here], mixed[slot, 1, imag])
             starts = [(first * lane, even + odd)]
             if half + first * lane < centre:
                 starts.append((half + first * lane, even - odd))
@@ -354,7 +358,7 @@
                     combos[0, imag, start // strip + k, place] = piece[:, :lane]
                     combos[1, imag, start // strip + k, place] = piece[:, lane:]
 
-        return [functools.partial(rows, imag, first) for imag in range(2) for first in range(half // lane)]
+        return [functools.partial(rows, imag) for imag in range(2)]
 
     share = 1.0 / jnp.full((1, 1), count, jnp.int32).astype(f32)
     shares = [jnp.where(slot < count, share, 0.0) for slot in range(LMAX)]
@@ -392,18 +396,25 @@
         for k in range(4):
             filt[k] = wide[k].astype(bf16)
 
-    parts = centre // strip
-    for tick in range(LMAX + 2):
+    rows_first()
+    thin()
+    for tick in range(LMAX + 1):
         products = project(tick) if tick < LMAX else []
-        if 0 <= tick - 2:
-            products = products + combine(tick - 2)
-        sums = [thin] if tick == 0 else []
-        if 0 <= tick - 1 < LMAX:
-            sums = [functools.partial(mix, tick - 1, start) for start in range(0, half, step)]
+        if tick > 1:
+            products = products + combine(tick - 2, 0)
+        sums = [functools.partial(mix, tick - 1, start) for start in range(0, half, step)] if tick else []
         weave(products, sums)
-    for part in range(parts):
-        back(part)
-        gather(part)
+    for step_ in combine(LMAX - 1, 0):
+        step_()
+    for first in range(half // lane):
+        later = []
+        if first + 1 < half // lane:
+            later = [step_ for slot in range(LMAX) for step_ in combine(slot, first + 1)]
+        ready = []
+        for start in range(first * lane, centre, half):
+            for part in range(start // strip, (start + lane) // strip):
+                ready += [functools.partial(back, part), functools.partial(gather, part)]
+        weave(later, ready)
     for copy in out_copies:
         copy.wait()
 
@@ -428,13 +439,13 @@
     )(*inputs)
 
 
-def pack(orient_list, lengths, defocus, centre_block, box):
-    centre = centre_block.shape[0]
+def pack(orient_list, lengths, defocus, centre_block, templates):
+    centre, box = centre_block.shape[0], templates.shape[1]
     lane = (centre + box) // 4
-    held = (centre_block, orient_list.T, lengths[None], defocus[None])
+    held = (centre_block, orient_list.T, lengths[None], defocus[None], templates)
     strip = ((centre // 2, lane), jnp.bfloat16)
     outs = [(array.shape, array.dtype) for array in held] + [((box // 2, centre), jnp.bfloat16), strip, strip]
-    return vmem_call(pack_kernel, held, outs, [pltpu.SemaphoreType.DMA((4,))], 0, 8, in_space=pltpu.HBM)
+    return vmem_call(pack_kernel, held, outs, [pltpu.SemaphoreType.DMA((5,))], 0, 8, in_space=pltpu.HBM)
 
 
 def early(defocus, extent):
@@ -445,7 +456,7 @@
 def tile_spectrum(paired, pieces, weights, tables, extent):
     half = extent // 2
     (filt,) = vmem_call(
-        functools.partial(tile_kernel, paired), (*pieces, weights, *tables[:4]),
+        functools.partial(tile_kernel, paired), (*pieces, weights, *tables),
         (((4, half, half), jnp.float32),), [pltpu.VMEM((extent, extent), jnp.float32)], 0, 16,
     )
     return filt
@@ -460,8 +471,9 @@
         match_kernel, (orient_list, lengths, filt, near, far, *tables[:2], *tables[4:]), (out, out, out),
         [
             pltpu.VMEM((4, half, half), jnp.bfloat16),
+            pltpu.VMEM((LMAX, 2, 2 * near.shape[1], half), jnp.bfloat16),
             pltpu.VMEM((2, 2 * extent, half), jnp.bfloat16),
-            pltpu.VMEM((2, 2, 2, half, half), jnp.bfloat16),
+            pltpu.VMEM((LMAX, 2, 2, half, half), jnp.bfloat16),
             pltpu.VMEM((2, 2, centre // strip, LMAX * strip, lane), jnp.bfloat16),
             pltpu.VMEM((3, centre, centre), jnp.float32),
             pltpu.SemaphoreType.DMA((3, centre // strip)),
@@ -491,8 +503,8 @@
         odd = position % 2 == 1
         distances = flips(tile_count)
         pair = send(templates, lambda i: i ^ distances[0])
-        block, orients, counts, focus, to_ends, to_mate, to_peer = pack(
-            orient_list, lengths, defocus, centre_block, box
+        block, orients, counts, focus, own, to_ends, to_mate, to_peer = pack(
+            orient_list, lengths, defocus, centre_block, templates
         )
         ends = send(to_ends, lambda i: i ^ GRID)
         weights = early(focus, extent)
@@ -502,7 +514,7 @@
             edge = jnp.concatenate([edge[: margin // 2], edge[margin // 2 :]], axis=1)
             return jnp.concatenate([own, edge], axis=0)
 
-        two = jnp.concatenate([templates, pair], axis=0)
+        two = jnp.concatenate([own, pair], axis=0)
         group = [two]
         for apart in (distances[2] | distances[1], distances[1], distances[2]):
             group.append(send(two, lambda i, apart=apart: i ^ apart))
@@ -518,7 +530,7 @@
                 block, "tile", [((i + distance) % tile_count, i) for i in range(tile_count)]
             )
 
-        _, orients, counts, focus, *_ = pack(orient_list, lengths, defocus, centre_block, box)
+        _, orients, counts, focus, *_ = pack(orient_list, lengths, defocus, centre_block, templates)
         weights = early(focus, extent)
         right = arrive(centre_block[:, :margin], 1)
         left = arrive(centre_block[:, centre - margin :], -1)

time: 27.6 us -> 26.8 us (0.971)
  local copies, waits for them, and re-layouts: 0.51 us -> 0.11 us
  Pallas kernels: 7.15 us -> 6.76 us
    unnamed x21 -> x19, local copies, waits for them, and re-layouts: 0.48 us -> 0.08 us
    pallas_call x4, Pallas kernels: 7.15 us -> 6.76 us  [vmem_call(): pl.pallas_call(kernel, out_shape=tuple((jax.ShapeDtypeStruct(shape, dtype...]
where the time goes in v3:
time: 26.8 us; the launch traced here: 26.7 us
  starting transfers between devices  13 us (49%)
  Pallas kernels  6.76 us (25%)
  waiting for transfers between devices  5.74 us (21%)
  between operations  0.81 us (3%)
    ppermute x8, starting transfers between devices, send(): lax.ppermute(block, 'tile', [(i, target(i)) for i in range(tile_count)])  13 us
    pallas_call x4, Pallas kernels, vmem_call(): pl.pallas_call(kernel, out_shape=tuple((jax.ShapeDtypeStruct(shape, dtype...  6.76 us
    ppermute x8, waiting for transfers between devices, send(): lax.ppermute(block, 'tile', [(i, target(i)) for i in range(tile_count)])  5.74 us
  transfers between devices with their start and end apart: 8, of which 4 were waited for; matrix products, arithmetic and copies ran while one was open for 1% of the time, Pallas kernels for 10%

profile of v3, /device:TPU:0, one launch (start us, length us, event | category | flops | bytes accessed | tf_op | source)
XLA Modules:
  0.0 26.7 jit_solution(15412777132221115401)
XLA Ops:
  0.6 4.1 %collective-permute-start.3 = (bf16[1,128,128]{2,1,0:T(8,128)(2,1)}, bf16[1,128,128]{2,1,0:T(8,128)(2,1)S(1)}, u32[]{:S(2)}, u32[]{:S(2)}) collective-permute-start(bf16[1,128,128]{2,1,0:T(8,128)(2,1)} %refs_4_.1), channel_id=1, source_target_pairs={{0,8},{1,9},{2,10},{3,11},{4,12},{5,13},{6,14},{7,15},{8,0},{9,1},... | collective-permute-start | bytes 98312 | tf_op jit(solution)/shard_map/ppermute | solution.py:499
  4.8 1.1 %shard_map.148 = (bf16[384,384]{1,0:T(8,128)(2,1)S(1)}, s32[4,16]{1,0:T(4,128)S(1)}, s32[1,16]{1,0:T(1,128)S(1)}, f32[1,16]{1,0:T(1,128)S(1)}, bf16[1,128,128]{2...) custom-call(bf16[384,384]{1,0:T(8,128)(2,1)} %bitcast.4, ...), custom_call_target="tpu_custom_call" | custom-call | tf_op jit(solution)/shard_map/pallas_call | solution.py:432
  5.9 0.1 collective-permute-start
  6.0 1.2 %collective-permute-done.3 = bf16[1,128,128]{2,1,0:T(8,128)(2,1)S(1)} collective-permute-done((bf16[1,128,128]{2,1,0:T(8,128)(2,1)}, bf16[1,128,128]{2,1,0:T(8,128)(2,1)S(1)}, u32[]{:S(2)}, u32[]{:S(2)}) %collective-permute-start.3) | collective-permute-done | bytes 32800 | tf_op jit(solution)/shard_map/ppermute | solution.py:499
  7.2 2.8 %collective-permute-start.6 = (bf16[2,128,128]{2,1,0:T(8,128)(2,1)S(1)}, bf16[2,128,128]{2,1,0:T(8,128)(2,1)S(1)}, u32[]{:S(2)}, u32[]{:S(2)}) collective-permute-start(bf16[2,128,128]{2,1,0:T(8,128)(2,1)S(1)} %get-tuple-element.21), channel_id=1, source_target_pairs={{0,6},{1,7},{2,4},{3,5},{4,2},{5,3},{6,0},{7,1},{8,14},{9,15},{10,... | collective-permute-start | bytes 196616 | tf_op jit(solution)/shard_map/ppermute | solution.py:499
  10.0 0.5 %collective-permute-start.5 = (bf16[2,128,128]{2,1,0:T(8,128)(2,1)S(1)}, bf16[2,128,128]{2,1,0:T(8,128)(2,1)S(1)}, u32[]{:S(2)}, u32[]{:S(2)}) collective-permute-start(bf16[2,128,128]{2,1,0:T(8,128)(2,1)S(1)} %get-tuple-element.21), channel_id=1, source_target_pairs={{0,4},{1,5},{2,6},{3,7},{4,0},{5,1},{6,2},{7,3},{8,12},{9,13},{10,... | collective-permute-start | bytes 196616 | tf_op jit(solution)/shard_map/ppermute | solution.py:499
  10.5 0.5 %collective-permute-start.4 = (bf16[2,128,128]{2,1,0:T(8,128)(2,1)S(1)}, bf16[2,128,128]{2,1,0:T(8,128)(2,1)S(1)}, u32[]{:S(2)}, u32[]{:S(2)}) collective-permute-start(bf16[2,128,128]{2,1,0:T(8,128)(2,1)S(1)} %get-tuple-element.21), channel_id=1, source_target_pairs={{0,2},{1,3},{2,0},{3,1},{4,6},{5,7},{6,4},{7,5},{8,10},{9,11},{10,... | collective-permute-start | bytes 196616 | tf_op jit(solution)/shard_map/ppermute | solution.py:499
  11.0 0.1 collective-permute-done.refs_3_
  11.1 0.1 broadcast_select_fusion
  11.2 3.6 %collective-permute-done.4 = bf16[2,128,128]{2,1,0:T(8,128)(2,1)S(1)} collective-permute-done((bf16[2,128,128]{2,1,0:T(8,128)(2,1)S(1)}, bf16[2,128,128]{2,1,0:T(8,128)(2,1)S(1)}, u32[]{:S(2)}, u32[]{:S(2)}) %collective-permute-start.4) | collective-permute-done | bytes 65568 | tf_op jit(solution)/shard_map/ppermute | solution.py:499
  14.8 0.0 copy-start.7
  14.8 0.0 collective-permute-done.6
  14.8 0.0 copy-start.6
  14.9 0.1 collective-permute-start.7
  14.9 0.0 copy-start.5
  14.9 0.1 maximum_maximum_fusion
  15.0 0.5 %collective-permute-start.1 = (bf16[224,128]{1,0:T(8,128)(2,1)S(1)}, bf16[224,128]{1,0:T(8,128)(2,1)S(1)}, u32[]{:S(2)}, u32[]{:S(2)}) collective-permute-start(bf16[224,128]{1,0:T(8,128)(2,1)S(1)} %maximum_maximum_fusion), channel_id=1, source_target_pairs={{0,1},{1,0},{2,3},{3,2},{4,5},{5,4},{6,7},{7,6},{8,9},{9,8},{10,11... | collective-permute-start | bytes 172040 | tf_op jit(solution)/shard_map/ppermute | solution.py:499
  15.5 0.1 maximum_maximum_fusion.1
  15.6 4.5 %collective-permute-start.2 = (bf16[224,128]{1,0:T(8,128)(2,1)S(1)}, bf16[224,128]{1,0:T(8,128)(2,1)S(1)}, u32[]{:S(2)}, u32[]{:S(2)}) collective-permute-start(bf16[224,128]{1,0:T(8,128)(2,1)S(1)} %maximum_maximum_fusion.1), channel_id=1, source_target_pairs={{0,15},{1,2},{2,1},{3,4},{4,3},{5,6},{6,5},{7,8},{8,7},{9,10},{10,... | collective-permute-start | bytes 172040 | tf_op jit(solution)/shard_map/ppermute | solution.py:499
  20.1 0.0 copy-start.4
  20.1 1.0 %shard_map.149.refs_4_ = f32[4,256,256]{2,1,0:T(8,128)S(1)} custom-call(f32[1,16]{1,0:T(1,128)S(1)} %get-tuple-element.17.defocus), custom_call_target="tpu_custom_call" | custom-call | tf_op jit(solution)/shard_map/pallas_call | solution.py:432
  21.1 0.8 %collective-permute-done.2.refs_2_ = bf16[224,128]{1,0:T(8,128)(2,1)S(1)} collective-permute-done((bf16[224,128]{1,0:T(8,128)(2,1)S(1)}, bf16[224,128]{1,0:T(8,128)(2,1)S(1)}, u32[]{:S(2)}, u32[]{:S(2)}) %collective-permute-start.2) | collective-permute-done | bytes 57376 | tf_op jit(solution)/shard_map/ppermute | solution.py:499
  22.0 0.7 %shard_map.150.wide = f32[4,256,256]{2,1,0:T(8,128)S(1)} custom-call(bf16[384,384]{1,0:T(8,128)(2,1)S(1)} %get-tuple-element.13.refs_0_, bf16[224,128]{1,0:T(8,128)(2,1)S(1)} %collective-permute-done.1.refs_1_, bf16[224,128]{1,0:T(8,128)(2,1)S(1)} %collective-permute-done.2.refs_2_, bf16[64,384]{1,0:T(8,128)(2,1)S(1)} %collective-permute-done.refs_3_, ...), custom_call_target="tpu_custom_call" | custom-call | tf_op jit(solution)/shard_map/pallas_call | solution.py:432
  22.7 4.0 %shard_map.151 = (f32[1,384,384]{2,1,0:T(8,128)}, f32[1,384,384]{2,1,0:T(8,128)}, f32[1,384,384]{2,1,0:T(8,128)}) custom-call(s32[4,16]{1,0:T(4,128)S(1)} %get-tuple-element.11.orients, s32[1,16]{1,0:T(1,128)S(1)} %get-tuple-element.12.lengths, f32[4,256,256]{2,1,0:T(8,128)S(1)} %shard_map.150.wide, ...), custom_call_target="tpu_custom_call" | custom-call | tf_op jit(solution)/shard_map/pallas_call | solution.py:432
  (21 shorter events, 0.1 us)
Async XLA Ops:
  0.6 6.6 %collective-permute-start.3 = (bf16[1,128,128]{2,1,0:T(8,128)(2,1)}, bf16[1,128,128]{2,1,0:T(8,128)(2,1)S(1)}, u32[]{:S(2)}, u32[]{:S(2)}) collective-permute-start(bf16[1,128,128]{2,1,0:T(8,128)(2,1)} %refs_4_.1), channel_id=1, source_target_pairs={{0,8},{1,9},{2,10},{3,11},{4,12},{5,13},{6,14},{7,15},{8,0},{9,1},... | collective-permute-start | bytes 98312 | tf_op jit(solution)/shard_map/ppermute | solution.py:499
  5.9 5.2 %collective-permute-start = (bf16[64,384]{1,0:T(8,128)(2,1)S(1)}, bf16[64,384]{1,0:T(8,128)(2,1)S(1)}, u32[]{:S(2)}, u32[]{:S(2)}) collective-permute-start(bf16[64,384]{1,0:T(8,128)(2,1)S(1)} %get-tuple-element.15), channel_id=1, source_target_pairs={{0,8},{1,9},{2,10},{3,11},{4,12},{5,13},{6,14},{7,15},{8,0},{9,1},... | collective-permute-start | bytes 147464 | tf_op jit(solution)/shard_map/ppermute | solution.py:499
  7.2 7.6 %collective-permute-start.6 = (bf16[2,128,128]{2,1,0:T(8,128)(2,1)S(1)}, bf16[2,128,128]{2,1,0:T(8,128)(2,1)S(1)}, u32[]{:S(2)}, u32[]{:S(2)}) collective-permute-start(bf16[2,128,128]{2,1,0:T(8,128)(2,1)S(1)} %get-tuple-element.21), channel_id=1, source_target_pairs={{0,6},{1,7},{2,4},{3,5},{4,2},{5,3},{6,0},{7,1},{8,14},{9,15},{10,... | collective-permute-start | bytes 196616 | tf_op jit(solution)/shard_map/ppermute | solution.py:499
  10.0 4.8 %collective-permute-start.5 = (bf16[2,128,128]{2,1,0:T(8,128)(2,1)S(1)}, bf16[2,128,128]{2,1,0:T(8,128)(2,1)S(1)}, u32[]{:S(2)}, u32[]{:S(2)}) collective-permute-start(bf16[2,128,128]{2,1,0:T(8,128)(2,1)S(1)} %get-tuple-element.21), channel_id=1, source_target_pairs={{0,4},{1,5},{2,6},{3,7},{4,0},{5,1},{6,2},{7,3},{8,12},{9,13},{10,... | collective-permute-start | bytes 196616 | tf_op jit(solution)/shard_map/ppermute | solution.py:499
  10.5 4.3 %collective-permute-start.4 = (bf16[2,128,128]{2,1,0:T(8,128)(2,1)S(1)}, bf16[2,128,128]{2,1,0:T(8,128)(2,1)S(1)}, u32[]{:S(2)}, u32[]{:S(2)}) collective-permute-start(bf16[2,128,128]{2,1,0:T(8,128)(2,1)S(1)} %get-tuple-element.21), channel_id=1, source_target_pairs={{0,2},{1,3},{2,0},{3,1},{4,6},{5,7},{6,4},{7,5},{8,10},{9,11},{10,... | collective-permute-start | bytes 196616 | tf_op jit(solution)/shard_map/ppermute | solution.py:499
  14.8 7.1 %copy-start.7 = (bf16[256,256]{1,0:T(8,128)(2,1)S(1)}, bf16[256,256]{1,0:T(8,128)(2,1)}, u32[]{:S(2)}) copy-start(bf16[256,256]{1,0:T(8,128)(2,1)} %constant.36.clone.refs_7_) | copy-start | bytes 393220
  14.8 7.1 %copy-start.6 = (bf16[256,256]{1,0:T(8,128)(2,1)S(1)}, bf16[256,256]{1,0:T(8,128)(2,1)}, u32[]{:S(2)}) copy-start(bf16[256,256]{1,0:T(8,128)(2,1)} %constant.37.clone.refs_8_) | copy-start | bytes 393220
  14.9 7.8 %collective-permute-start.7 = (bf16[8,128,128]{2,1,0:T(8,128)(2,1)S(1)}, bf16[8,128,128]{2,1,0:T(8,128)(2,1)S(1)}, u32[]{:S(2)}, u32[]{:S(2)}) collective-permute-start(bf16[8,128,128]{2,1,0:T(8,128)(2,1)S(1)} %constant_dynamic-update-slice_fusion.2.near_ref), channel_id=1, source_target_pairs={{0,1},{1,0},{2,3},{3,2},{4,5},{5,4},{6,7},{7,6},{8,9},{9,8},{10,11... | collective-permute-start | bytes 786440 | tf_op jit(solution)/shard_map/ppermute | solution.py:499
  14.9 7.0 %copy-start.5 = (bf16[256,256]{1,0:T(8,128)(2,1)S(1)}, bf16[256,256]{1,0:T(8,128)(2,1)}, u32[]{:S(2)}) copy-start(bf16[256,256]{1,0:T(8,128)(2,1)} %constant.34.clone.refs_5_.fwd_e) | copy-start | bytes 393220
  15.0 6.0 %collective-permute-start.1 = (bf16[224,128]{1,0:T(8,128)(2,1)S(1)}, bf16[224,128]{1,0:T(8,128)(2,1)S(1)}, u32[]{:S(2)}, u32[]{:S(2)}) collective-permute-start(bf16[224,128]{1,0:T(8,128)(2,1)S(1)} %maximum_maximum_fusion), channel_id=1, source_target_pairs={{0,1},{1,0},{2,3},{3,2},{4,5},{5,4},{6,7},{7,6},{8,9},{9,8},{10,11... | collective-permute-start | bytes 172040 | tf_op jit(solution)/shard_map/ppermute | solution.py:499
  15.6 6.3 %collective-permute-start.2 = (bf16[224,128]{1,0:T(8,128)(2,1)S(1)}, bf16[224,128]{1,0:T(8,128)(2,1)S(1)}, u32[]{:S(2)}, u32[]{:S(2)}) collective-permute-start(bf16[224,128]{1,0:T(8,128)(2,1)S(1)} %maximum_maximum_fusion.1), channel_id=1, source_target_pairs={{0,15},{1,2},{2,1},{3,4},{4,3},{5,6},{6,5},{7,8},{8,7},{9,10},{10,... | collective-permute-start | bytes 172040 | tf_op jit(solution)/shard_map/ppermute | solution.py:499
  20.1 1.9 %copy-start = (bf16[1024,256]{1,0:T(8,128)(2,1)S(1)}, bf16[1024,256]{1,0:T(8,128)(2,1)}, u32[]{:S(2)}) copy-start(bf16[1024,256]{1,0:T(8,128)(2,1)} %constant.41.clone.refs_12_.temp_cols) | copy-start | bytes 1572868
  20.1 1.9 %copy-start.1 = (bf16[128,512]{1,0:T(8,128)(2,1)S(1)}, bf16[128,512]{1,0:T(8,128)(2,1)}, u32[]{:S(2)}) copy-start(bf16[128,512]{1,0:T(8,128)(2,1)} %constant.40.clone.refs_11_.temp_rows) | copy-start | bytes 393220
  20.1 1.9 %copy-start.2 = (bf16[256,256]{1,0:T(8,128)(2,1)S(1)}, bf16[256,256]{1,0:T(8,128)(2,1)}, u32[]{:S(2)}) copy-start(bf16[256,256]{1,0:T(8,128)(2,1)} %constant.39.clone.refs_10_.inv_o) | copy-start | bytes 393220
  20.1 1.9 %copy-start.3 = (bf16[256,256]{1,0:T(8,128)(2,1)S(1)}, bf16[256,256]{1,0:T(8,128)(2,1)}, u32[]{:S(2)}) copy-start(bf16[256,256]{1,0:T(8,128)(2,1)} %constant.38.clone.refs_9_.inv_e) | copy-start | bytes 393220
  20.1 1.9 %copy-start.4 = (bf16[256,256]{1,0:T(8,128)(2,1)S(1)}, bf16[256,256]{1,0:T(8,128)(2,1)}, u32[]{:S(2)}) copy-start(bf16[256,256]{1,0:T(8,128)(2,1)} %constant.35.clone.refs_6_.fwd_o) | copy-start | bytes 393220

commit v4 on v3

--- a/solution.py
+++ b/solution.py
@@ -176,60 +176,62 @@
     return jnp.concatenate([upper, lower], axis=0)
 
 
-def tile_kernel(paired, *refs):
-    if paired:
-        centre_ref, mate_ref, peer_ref, ends_ref, weight_ref = refs[:5]
-        refs = refs[5:]
-    else:
-        centre_ref, cols_ref, rows_ref, weight_ref = refs[:4]
-        refs = refs[4:]
-    fwd_e, fwd_o, fwd_et, fwd_ot = refs[:4]
-    filt, uv = refs[-2:]
+def tile_steps(paired, pieces, weight_ref, tables, filt, uv):
+    fwd_e, fwd_o, fwd_et, fwd_ot = tables
+    centre_ref = pieces[0]
     centre, extent = centre_ref.shape[0], uv.shape[0]
     half, lane = extent // 2, extent // 4
-    if paired:
-        place = lax.rem(lax.axis_index("tile") + GRID // 2, 2 * GRID)
-        column, upper_row = lax.rem(place, GRID), place < GRID
-        opens = (column != 0, column != GRID - 1)
-        side = packed_sides(mate_ref, peer_ref, lane, 0, centre // 2, *opens)
-        corners = packed_sides(mate_ref, peer_ref, lane, centre // 2, mate_ref.shape[0], *opens)
-        ends = jnp.concatenate([ends_ref[...].astype(jnp.float32), corners], axis=1)
-        rim = jnp.concatenate([jnp.where(upper_row, ends, 0.0), jnp.where(upper_row, 0.0, ends)], axis=0)
-    else:
-        side = cols_ref[...].astype(jnp.float32)
-        rim = rows_ref[...].astype(jnp.float32)
-    own = centre_ref[...].astype(jnp.float32)
-    far = jnp.concatenate([own[:, half:], side], axis=1)
-    near = own[:, :half]
-    uv[:centre, :half] = dot((near + far).astype(jnp.bfloat16), fwd_e[...])
-    uv[:centre, half:] = dot((near - far).astype(jnp.bfloat16), fwd_o[...])
-    near, far = rim[:, :half], rim[:, half:]
-    uv[centre:, :half] = dot((near + far).astype(jnp.bfloat16), fwd_e[...])
-    uv[centre:, half:] = dot((near - far).astype(jnp.bfloat16), fwd_o[...])
-    near, far = uv[:half, :], uv[half:, :]
-    spectra = (
-        dot(fwd_et[...], (near + far).astype(jnp.bfloat16)),
-        dot(fwd_ot[...], (near - far).astype(jnp.bfloat16)),
-    )
-    i = lax.broadcasted_iota(jnp.int32, (lane, lane), 0)
-    j = lax.broadcasted_iota(jnp.int32, (lane, lane), 1)
-    for row_odd in range(2):
-        for col_odd in range(2):
-            block = spectra[row_odd]
-            left, right = block[:lane], block[lane:]
-            u, v = 2 * col_odd * lane, (2 * col_odd + 1) * lane
-            uc, vc, us, vs = left[:, u : u + lane], left[:, v : v + lane], right[:, u : u + lane], right[:, v : v + lane]
-            parts = [uc - vs, -(us + vc), uc + vs, us - vc]
-            if not row_odd:
-                row_first = i == 0
-                parts = [jnp.where(row_first, a, b) for a, b in zip((uc, -vc, us, -vs), parts)]
-            if not col_odd:
-                col_first = j == 0
-                parts = [jnp.where(col_first, a, b) for a, b in zip((uc, -us, vc, vs), parts)]
-            rows = slice(row_odd * lane, (row_odd + 1) * lane)
-            cols = slice(col_odd * lane, (col_odd + 1) * lane)
-            for k in range(4):
-                filt[k, rows, cols] = weight_ref[k, rows, cols] * parts[k]
+    held = {}
+
+    def assemble():
+        if paired:
+            _, mate_ref, peer_ref, ends_ref = pieces
+            place = lax.rem(lax.axis_index("tile") + GRID // 2, 2 * GRID)
+            column, upper_row = lax.rem(place, GRID), place < GRID
+            opens = (column != 0, column != GRID - 1)
+            held["side"] = packed_sides(mate_ref, peer_ref, lane, 0, centre // 2, *opens)
+            corners = packed_sides(mate_ref, peer_ref, lane, centre // 2, mate_ref.shape[0], *opens)
+            ends = jnp.concatenate([ends_ref[...].astype(jnp.float32), corners], axis=1)
+            held["rim"] = jnp.concatenate([jnp.where(upper_row, ends, 0.0), jnp.where(upper_row, 0.0, ends)], axis=0)
+        else:
+            held["side"] = pieces[1][...].astype(jnp.float32)
+            held["rim"] = pieces[2][...].astype(jnp.float32)
+
+    def own_rows(first):
+        rows = slice(first * lane, (first + 1) * lane)
+        own = centre_ref[rows].astype(jnp.float32)
+        far = jnp.concatenate([own[:, half:], held["side"][rows]], axis=1)
+        near = own[:, :half]
+        uv[rows, :half] = dot((near + far).astype(jnp.bfloat16), fwd_e[...])
+        uv[rows, half:] = dot((near - far).astype(jnp.bfloat16), fwd_o[...])
+
+    def rim_rows():
+        near, far = held["rim"][:, :half], held["rim"][:, half:]
+        uv[centre:, :half] = dot((near + far).astype(jnp.bfloat16), fwd_e[...])
+        uv[centre:, half:] = dot((near - far).astype(jnp.bfloat16), fwd_o[...])
+
+    def columns(row_odd, col_odd):
+        cols = slice(col_odd * half, (col_odd + 1) * half)
+        near, far = uv[:half, cols], uv[half:, cols]
+        total = near - far if row_odd else near + far
+        block = dot((fwd_ot if row_odd else fwd_et)[...], total.astype(jnp.bfloat16))
+        i = lax.broadcasted_iota(jnp.int32, (lane, lane), 0)
+        j = lax.broadcasted_iota(jnp.int32, (lane, lane), 1)
+        uc, vc, us, vs = block[:lane, :lane], block[:lane, lane:], block[lane:, :lane], block[lane:, lane:]
+        parts = [uc - vs, -(us + vc), uc + vs, us - vc]
+        if not row_odd:
+            row_first = i == 0
+            parts = [jnp.where(row_first, a, b) for a, b in zip((uc, -vc, us, -vs), parts)]
+        if not col_odd:
+            col_first = j == 0
+            parts = [jnp.where(col_first, a, b) for a, b in zip((uc, -us, vc, vs), parts)]
+        rows = slice(row_odd * lane, (row_odd + 1) * lane)
+        cols = slice(col_odd * lane, (col_odd + 1) * lane)
+        for k in range(4):
+            filt[k, rows, cols] = (weight_ref[k, rows, cols] * parts[k]).astype(jnp.bfloat16)
+
+    steps = [assemble] + [functools.partial(own_rows, first) for first in range(centre // lane)] + [rim_rows]
+    return steps + [functools.partial(columns, r, c) for r in range(2) for c in range(2)]
 
 
 def weave(*tracks):
@@ -240,14 +242,14 @@
         step()
 
 
-def match_kernel(
-    orients, lengths, wide, near_ref, far_ref,
-    fwd_e, fwd_o, inv_e, inv_o, temp_rows, temp_cols,
-    snr_ref, mean_ref, var_ref,
-    filt, waves, proj, mixed, combos, out_buf, out_sem,
-):
+def match_kernel(paired, orients, lengths, *refs):
+    count_in = 4 if paired else 3
+    pieces, (weight_ref, near_ref, far_ref) = refs[:count_in], refs[count_in : count_in + 3]
+    fwd_e, fwd_o, fwd_et, fwd_ot, inv_e, inv_o, temp_rows, temp_cols = refs[count_in + 3 : count_in + 11]
+    snr_ref, mean_ref, var_ref = refs[count_in + 11 : count_in + 14]
+    filt, uv, waves, proj, mixed, combos, out_buf, out_sem = refs[count_in + 14 :]
     me = lax.axis_index("tile")
-    half = wide.shape[1]
+    half = filt.shape[1]
     lane = half // 2
     centre = out_buf.shape[1]
     box = near_ref.shape[1]
@@ -392,17 +394,13 @@
             copy.start()
             out_copies.append(copy)
 
-    def thin():
-        for k in range(4):
-            filt[k] = wide[k].astype(bf16)
-
-    rows_first()
-    thin()
-    for tick in range(LMAX + 1):
-        products = project(tick) if tick < LMAX else []
+    tile = tile_steps(paired, pieces, weight_ref, (fwd_e, fwd_o, fwd_et, fwd_ot), filt, uv)
+    weave(tile, [rows_first] + project(0) + project(1))
+    for tick in range(1, LMAX + 1):
+        products = project(tick) if 1 < tick < LMAX else []
         if tick > 1:
             products = products + combine(tick - 2, 0)
-        sums = [functools.partial(mix, tick - 1, start) for start in range(0, half, step)] if tick else []
+        sums = [functools.partial(mix, tick - 1, start) for start in range(0, half, step)]
         weave(products, sums)
     for step_ in combine(LMAX - 1, 0):
         step_()
@@ -453,24 +451,17 @@
     return vmem_call(early_kernel, (defocus,), (((4, half, half), jnp.float32),), [], 1, 8)[0]
 
 
-def tile_spectrum(paired, pieces, weights, tables, extent):
-    half = extent // 2
-    (filt,) = vmem_call(
-        functools.partial(tile_kernel, paired), (*pieces, weights, *tables),
-        (((4, half, half), jnp.float32),), [pltpu.VMEM((extent, extent), jnp.float32)], 0, 16,
-    )
-    return filt
-
-
-def match(orient_list, lengths, filt, near, far, tables, centre):
-    half = filt.shape[1]
+def match(orient_list, lengths, pieces, weights, near, far, tables):
+    centre, half = pieces[0].shape[0], weights.shape[1]
     lane, extent = half // 2, 2 * half
     strip = lane // 2
     out = ((1, centre, centre), jnp.float32)
+    kernel = functools.partial(match_kernel, len(pieces) == 4)
     return vmem_call(
-        match_kernel, (orient_list, lengths, filt, near, far, *tables[:2], *tables[4:]), (out, out, out),
+        kernel, (orient_list, lengths, *pieces, weights, near, far, *tables), (out, out, out),
         [
             pltpu.VMEM((4, half, half), jnp.bfloat16),
+            pltpu.VMEM((extent, extent), jnp.float32),
             pltpu.VMEM((LMAX, 2, 2 * near.shape[1], half), jnp.bfloat16),
             pltpu.VMEM((2, 2 * extent, half), jnp.bfloat16),
             pltpu.VMEM((LMAX, 2, 2, half, half), jnp.bfloat16),
@@ -522,7 +513,7 @@
         from_mate = send(strip(to_mate, odd), lambda i: i ^ 1)
         near = jnp.concatenate([group[0], group[2], group[3], group[1]], axis=0)
         far = send(near, lambda i: i ^ 1)
-        filt = tile_spectrum(True, (block, from_mate, from_peer, ends), weights, tables, extent)
+        pieces = (block, from_mate, from_peer, ends)
     else:
 
         def arrive(block, distance):
@@ -547,8 +538,8 @@
         for distance in flips(tile_count)[:-1]:
             near = jnp.concatenate([near, send(near, lambda i, d=distance: i ^ d)], axis=0)
         far = send(near, lambda i: i ^ 1)
-        filt = tile_spectrum(False, (centre_block, cols, rows), weights, tables, extent)
-    return match(orients, counts, filt, near, far, tables, centre)
+        pieces = (centre_block, cols, rows)
+    return match(orients, counts, pieces, weights, near, far, tables)
 
 
 def solution(mesh):

time: 26.8 us -> 26.6 us (level)
    pallas_call x4 -> x3, Pallas kernels: 6.76 us -> 6.56 us  [vmem_call(): pl.pallas_call(kernel, out_shape=tuple((jax.ShapeDtypeStruct(shape, dtype...]
  transfers between devices with their start and end apart: 8 -> 8, of which waited for: 4 -> 4; matrix products, arithmetic and copies ran while one was open for 1% -> 1% of each run, Pallas kernels for 10% -> 8%
where the time goes in v4:
time: 26.6 us; the launch traced here: 26.5 us
  starting transfers between devices  13 us (49%)
  Pallas kernels  6.56 us (25%)
  waiting for transfers between devices  5.74 us (22%)
  between operations  0.8 us (3%)
    ppermute x8, starting transfers between devices, send(): lax.ppermute(block, 'tile', [(i, target(i)) for i in range(tile_count)])  13 us
    pallas_call x3, Pallas kernels, vmem_call(): pl.pallas_call(kernel, out_shape=tuple((jax.ShapeDtypeStruct(shape, dtype...  6.56 us
    ppermute x8, waiting for transfers between devices, send(): lax.ppermute(block, 'tile', [(i, target(i)) for i in range(tile_count)])  5.74 us
  transfers between devices with their start and end apart: 8, of which 4 were waited for; matrix products, arithmetic and copies ran while one was open for 1% of the time, Pallas kernels for 8%

profile of v4, /device:TPU:0, one launch (start us, length us, event | category | flops | bytes accessed | tf_op | source)
XLA Modules:
  0.0 26.5 jit_solution(10136580786038076808)
XLA Ops:
  0.6 4.1 %collective-permute-start.3 = (bf16[1,128,128]{2,1,0:T(8,128)(2,1)}, bf16[1,128,128]{2,1,0:T(8,128)(2,1)S(1)}, u32[]{:S(2)}, u32[]{:S(2)}) collective-permute-start(bf16[1,128,128]{2,1,0:T(8,128)(2,1)} %refs_4_.1), channel_id=1, source_target_pairs={{0,8},{1,9},{2,10},{3,11},{4,12},{5,13},{6,14},{7,15},{8,0},{9,1},... | collective-permute-start | bytes 98312 | tf_op jit(solution)/shard_map/ppermute | solution.py:490
  4.8 1.1 %shard_map.148 = (bf16[384,384]{1,0:T(8,128)(2,1)S(1)}, s32[4,16]{1,0:T(4,128)S(1)}, s32[1,16]{1,0:T(1,128)S(1)}, f32[1,16]{1,0:T(1,128)S(1)}, bf16[1,128,128]{2...) custom-call(bf16[384,384]{1,0:T(8,128)(2,1)} %bitcast.4, ...), custom_call_target="tpu_custom_call" | custom-call | tf_op jit(solution)/shard_map/pallas_call | solution.py:430
  5.9 0.1 collective-permute-start
  6.0 1.2 %collective-permute-done.3 = bf16[1,128,128]{2,1,0:T(8,128)(2,1)S(1)} collective-permute-done((bf16[1,128,128]{2,1,0:T(8,128)(2,1)}, bf16[1,128,128]{2,1,0:T(8,128)(2,1)S(1)}, u32[]{:S(2)}, u32[]{:S(2)}) %collective-permute-start.3) | collective-permute-done | bytes 32800 | tf_op jit(solution)/shard_map/ppermute | solution.py:490
  7.2 2.8 %collective-permute-start.6 = (bf16[2,128,128]{2,1,0:T(8,128)(2,1)S(1)}, bf16[2,128,128]{2,1,0:T(8,128)(2,1)S(1)}, u32[]{:S(2)}, u32[]{:S(2)}) collective-permute-start(bf16[2,128,128]{2,1,0:T(8,128)(2,1)S(1)} %get-tuple-element.21), channel_id=1, source_target_pairs={{0,6},{1,7},{2,4},{3,5},{4,2},{5,3},{6,0},{7,1},{8,14},{9,15},{10,... | collective-permute-start | bytes 196616 | tf_op jit(solution)/shard_map/ppermute | solution.py:490
  10.0 0.5 %collective-permute-start.5 = (bf16[2,128,128]{2,1,0:T(8,128)(2,1)S(1)}, bf16[2,128,128]{2,1,0:T(8,128)(2,1)S(1)}, u32[]{:S(2)}, u32[]{:S(2)}) collective-permute-start(bf16[2,128,128]{2,1,0:T(8,128)(2,1)S(1)} %get-tuple-element.21), channel_id=1, source_target_pairs={{0,4},{1,5},{2,6},{3,7},{4,0},{5,1},{6,2},{7,3},{8,12},{9,13},{10,... | collective-permute-start | bytes 196616 | tf_op jit(solution)/shard_map/ppermute | solution.py:490
  10.5 0.5 %collective-permute-start.4 = (bf16[2,128,128]{2,1,0:T(8,128)(2,1)S(1)}, bf16[2,128,128]{2,1,0:T(8,128)(2,1)S(1)}, u32[]{:S(2)}, u32[]{:S(2)}) collective-permute-start(bf16[2,128,128]{2,1,0:T(8,128)(2,1)S(1)} %get-tuple-element.21), channel_id=1, source_target_pairs={{0,2},{1,3},{2,0},{3,1},{4,6},{5,7},{6,4},{7,5},{8,10},{9,11},{10,... | collective-permute-start | bytes 196616 | tf_op jit(solution)/shard_map/ppermute | solution.py:490
  11.0 0.1 collective-permute-done.refs_3_
  11.1 0.1 broadcast_select_fusion
  11.2 3.6 %collective-permute-done.4 = bf16[2,128,128]{2,1,0:T(8,128)(2,1)S(1)} collective-permute-done((bf16[2,128,128]{2,1,0:T(8,128)(2,1)S(1)}, bf16[2,128,128]{2,1,0:T(8,128)(2,1)S(1)}, u32[]{:S(2)}, u32[]{:S(2)}) %collective-permute-start.4) | collective-permute-done | bytes 65568 | tf_op jit(solution)/shard_map/ppermute | solution.py:490
  14.8 0.0 collective-permute-done.5
  14.8 0.0 collective-permute-done.6
  14.8 0.0 copy-start.6
  14.8 0.0 copy-start.7
  14.9 0.1 collective-permute-start.7
  14.9 0.1 maximum_maximum_fusion
  15.0 0.5 %collective-permute-start.1 = (bf16[224,128]{1,0:T(8,128)(2,1)S(1)}, bf16[224,128]{1,0:T(8,128)(2,1)S(1)}, u32[]{:S(2)}, u32[]{:S(2)}) collective-permute-start(bf16[224,128]{1,0:T(8,128)(2,1)S(1)} %maximum_maximum_fusion), channel_id=1, source_target_pairs={{0,1},{1,0},{2,3},{3,2},{4,5},{5,4},{6,7},{7,6},{8,9},{9,8},{10,11... | collective-permute-start | bytes 172040 | tf_op jit(solution)/shard_map/ppermute | solution.py:490
  15.5 0.1 maximum_maximum_fusion.1
  15.6 4.5 %collective-permute-start.2 = (bf16[224,128]{1,0:T(8,128)(2,1)S(1)}, bf16[224,128]{1,0:T(8,128)(2,1)S(1)}, u32[]{:S(2)}, u32[]{:S(2)}) collective-permute-start(bf16[224,128]{1,0:T(8,128)(2,1)S(1)} %maximum_maximum_fusion.1), channel_id=1, source_target_pairs={{0,15},{1,2},{2,1},{3,4},{4,3},{5,6},{6,5},{7,8},{8,7},{9,10},{10,... | collective-permute-start | bytes 172040 | tf_op jit(solution)/shard_map/ppermute | solution.py:490
  20.1 0.0 copy-start.4
  20.1 1.0 %shard_map.149.refs_4_ = f32[4,256,256]{2,1,0:T(8,128)S(1)} custom-call(f32[1,16]{1,0:T(1,128)S(1)} %get-tuple-element.17.defocus), custom_call_target="tpu_custom_call" | custom-call | tf_op jit(solution)/shard_map/pallas_call | solution.py:430
  21.1 0.0 collective-permute-done.1.refs_1_
  21.1 0.9 %collective-permute-done.2.refs_2_ = bf16[224,128]{1,0:T(8,128)(2,1)S(1)} collective-permute-done((bf16[224,128]{1,0:T(8,128)(2,1)S(1)}, bf16[224,128]{1,0:T(8,128)(2,1)S(1)}, u32[]{:S(2)}, u32[]{:S(2)}) %collective-permute-start.2) | collective-permute-done | bytes 57376 | tf_op jit(solution)/shard_map/ppermute | solution.py:490
  22.0 4.5 %shard_map.150 = (f32[1,384,384]{2,1,0:T(8,128)}, f32[1,384,384]{2,1,0:T(8,128)}, f32[1,384,384]{2,1,0:T(8,128)}) custom-call(s32[4,16]{1,0:T(4,128)S(1)} %get-tuple-element.11.orients, s32[1,16]{1,0:T(1,128)S(1)} %get-tuple-element.12.lengths, bf16[384,384]{1,0:T(8,128)(2,1)S(1)} %get-tuple-element.13.refs_0_, ...), custom_call_target="tpu_custom_call" | custom-call | tf_op jit(solution)/shard_map/pallas_call | solution.py:430
  (20 shorter events, 0.1 us)
Async XLA Ops:
  0.6 6.6 %collective-permute-start.3 = (bf16[1,128,128]{2,1,0:T(8,128)(2,1)}, bf16[1,128,128]{2,1,0:T(8,128)(2,1)S(1)}, u32[]{:S(2)}, u32[]{:S(2)}) collective-permute-start(bf16[1,128,128]{2,1,0:T(8,128)(2,1)} %refs_4_.1), channel_id=1, source_target_pairs={{0,8},{1,9},{2,10},{3,11},{4,12},{5,13},{6,14},{7,15},{8,0},{9,1},... | collective-permute-start | bytes 98312 | tf_op jit(solution)/shard_map/ppermute | solution.py:490
  5.9 5.2 %collective-permute-start = (bf16[64,384]{1,0:T(8,128)(2,1)S(1)}, bf16[64,384]{1,0:T(8,128)(2,1)S(1)}, u32[]{:S(2)}, u32[]{:S(2)}) collective-permute-start(bf16[64,384]{1,0:T(8,128)(2,1)S(1)} %get-tuple-element.15), channel_id=1, source_target_pairs={{0,8},{1,9},{2,10},{3,11},{4,12},{5,13},{6,14},{7,15},{8,0},{9,1},... | collective-permute-start | bytes 147464 | tf_op jit(solution)/shard_map/ppermute | solution.py:490
  7.2 7.6 %collective-permute-start.6 = (bf16[2,128,128]{2,1,0:T(8,128)(2,1)S(1)}, bf16[2,128,128]{2,1,0:T(8,128)(2,1)S(1)}, u32[]{:S(2)}, u32[]{:S(2)}) collective-permute-start(bf16[2,128,128]{2,1,0:T(8,128)(2,1)S(1)} %get-tuple-element.21), channel_id=1, source_target_pairs={{0,6},{1,7},{2,4},{3,5},{4,2},{5,3},{6,0},{7,1},{8,14},{9,15},{10,... | collective-permute-start | bytes 196616 | tf_op jit(solution)/shard_map/ppermute | solution.py:490
  10.0 4.8 %collective-permute-start.5 = (bf16[2,128,128]{2,1,0:T(8,128)(2,1)S(1)}, bf16[2,128,128]{2,1,0:T(8,128)(2,1)S(1)}, u32[]{:S(2)}, u32[]{:S(2)}) collective-permute-start(bf16[2,128,128]{2,1,0:T(8,128)(2,1)S(1)} %get-tuple-element.21), channel_id=1, source_target_pairs={{0,4},{1,5},{2,6},{3,7},{4,0},{5,1},{6,2},{7,3},{8,12},{9,13},{10,... | collective-permute-start | bytes 196616 | tf_op jit(solution)/shard_map/ppermute | solution.py:490
  10.5 4.3 %collective-permute-start.4 = (bf16[2,128,128]{2,1,0:T(8,128)(2,1)S(1)}, bf16[2,128,128]{2,1,0:T(8,128)(2,1)S(1)}, u32[]{:S(2)}, u32[]{:S(2)}) collective-permute-start(bf16[2,128,128]{2,1,0:T(8,128)(2,1)S(1)} %get-tuple-element.21), channel_id=1, source_target_pairs={{0,2},{1,3},{2,0},{3,1},{4,6},{5,7},{6,4},{7,5},{8,10},{9,11},{10,... | collective-permute-start | bytes 196616 | tf_op jit(solution)/shard_map/ppermute | solution.py:490
  14.8 7.1 %copy-start.6 = (bf16[256,256]{1,0:T(8,128)(2,1)S(1)}, bf16[256,256]{1,0:T(8,128)(2,1)}, u32[]{:S(2)}) copy-start(bf16[256,256]{1,0:T(8,128)(2,1)} %constant.35.clone.refs_8_) | copy-start | bytes 393220
  14.8 7.1 %copy-start.7 = (bf16[256,256]{1,0:T(8,128)(2,1)S(1)}, bf16[256,256]{1,0:T(8,128)(2,1)}, u32[]{:S(2)}) copy-start(bf16[256,256]{1,0:T(8,128)(2,1)} %constant.34.clone.refs_7_) | copy-start | bytes 393220
  14.9 7.1 %collective-permute-start.7 = (bf16[8,128,128]{2,1,0:T(8,128)(2,1)S(1)}, bf16[8,128,128]{2,1,0:T(8,128)(2,1)S(1)}, u32[]{:S(2)}, u32[]{:S(2)}) collective-permute-start(bf16[8,128,128]{2,1,0:T(8,128)(2,1)S(1)} %constant_dynamic-update-slice_fusion.2.refs_5_), channel_id=1, source_target_pairs={{0,1},{1,0},{2,3},{3,2},{4,5},{5,4},{6,7},{7,6},{8,9},{9,8},{10,11... | collective-permute-start | bytes 786440 | tf_op jit(solution)/shard_map/ppermute | solution.py:490
  15.0 6.0 %collective-permute-start.1 = (bf16[224,128]{1,0:T(8,128)(2,1)S(1)}, bf16[224,128]{1,0:T(8,128)(2,1)S(1)}, u32[]{:S(2)}, u32[]{:S(2)}) collective-permute-start(bf16[224,128]{1,0:T(8,128)(2,1)S(1)} %maximum_maximum_fusion), channel_id=1, source_target_pairs={{0,1},{1,0},{2,3},{3,2},{4,5},{5,4},{6,7},{7,6},{8,9},{9,8},{10,11... | collective-permute-start | bytes 172040 | tf_op jit(solution)/shard_map/ppermute | solution.py:490
  15.5 6.4 %copy-start.5 = (bf16[256,256]{1,0:T(8,128)(2,1)S(1)}, bf16[256,256]{1,0:T(8,128)(2,1)}, u32[]{:S(2)}) copy-start(bf16[256,256]{1,0:T(8,128)(2,1)} %constant.36.clone.refs_9_) | copy-start | bytes 393220
  15.6 6.3 %collective-permute-start.2 = (bf16[224,128]{1,0:T(8,128)(2,1)S(1)}, bf16[224,128]{1,0:T(8,128)(2,1)S(1)}, u32[]{:S(2)}, u32[]{:S(2)}) collective-permute-start(bf16[224,128]{1,0:T(8,128)(2,1)S(1)} %maximum_maximum_fusion.1), channel_id=1, source_target_pairs={{0,15},{1,2},{2,1},{3,4},{4,3},{5,6},{6,5},{7,8},{8,7},{9,10},{10,... | collective-permute-start | bytes 172040 | tf_op jit(solution)/shard_map/ppermute | solution.py:490
  20.1 1.9 %copy-start = (bf16[1024,256]{1,0:T(8,128)(2,1)S(1)}, bf16[1024,256]{1,0:T(8,128)(2,1)}, u32[]{:S(2)}) copy-start(bf16[1024,256]{1,0:T(8,128)(2,1)} %constant.41.clone.refs_14_) | copy-start | bytes 1572868
  20.1 1.9 %copy-start.1 = (bf16[128,512]{1,0:T(8,128)(2,1)S(1)}, bf16[128,512]{1,0:T(8,128)(2,1)}, u32[]{:S(2)}) copy-start(bf16[128,512]{1,0:T(8,128)(2,1)} %constant.40.clone.refs_13_) | copy-start | bytes 393220
  20.1 1.9 %copy-start.2 = (bf16[256,256]{1,0:T(8,128)(2,1)S(1)}, bf16[256,256]{1,0:T(8,128)(2,1)}, u32[]{:S(2)}) copy-start(bf16[256,256]{1,0:T(8,128)(2,1)} %constant.39.clone.refs_12_) | copy-start | bytes 393220
  20.1 1.9 %copy-start.3 = (bf16[256,256]{1,0:T(8,128)(2,1)S(1)}, bf16[256,256]{1,0:T(8,128)(2,1)}, u32[]{:S(2)}) copy-start(bf16[256,256]{1,0:T(8,128)(2,1)} %constant.38.clone.refs_11_) | copy-start | bytes 393220
  20.1 1.9 %copy-start.4 = (bf16[256,256]{1,0:T(8,128)(2,1)S(1)}, bf16[256,256]{1,0:T(8,128)(2,1)}, u32[]{:S(2)}) copy-start(bf16[256,256]{1,0:T(8,128)(2,1)} %constant.37.clone.refs_10_) | copy-start | bytes 393220

commit v5 on v4

--- a/solution.py
+++ b/solution.py
@@ -344,21 +344,17 @@
         mixed[slot, row_odd, 1, at : at + step] = cos_i
         mixed[slot, row_odd, 1, lane + at : lane + at + step] = sin_i
 
-    def combine(slot, first):
+    def combine(slot):
         def rows(imag):
-            here = slice(first * lane, (first + 1) * lane)
-            even = dot(fwd_e[here], mixed[slot, 0, imag])
-            odd = dot(fwd_o[here], mixed[slot, 1, imag])
-            starts = [(first * lane, even + odd)]
-            if half + first * lane < centre:
-                starts.append((half + first * lane, even - odd))
-            for start, value in starts:
+            even = dot(fwd_e[...], mixed[slot, 0, imag])
+            odd = dot(fwd_o[...], mixed[slot, 1, imag])
+            place = slice(slot * strip, (slot + 1) * strip)
+            for start in range(0, centre, strip):
+                here = slice(start % half, start % half + strip)
+                value = even[here] + odd[here] if start < half else even[here] - odd[here]
                 value = value.astype(bf16)
-                for k in range(lane // strip):
-                    place = slice(slot * strip, (slot + 1) * strip)
-                    piece = value[k * strip : (k + 1) * strip]
-                    combos[0, imag, start // strip + k, place] = piece[:, :lane]
-                    combos[1, imag, start // strip + k, place] = piece[:, lane:]
+                combos[0, imag, start // strip, place] = value[:, :lane]
+                combos[1, imag, start // strip, place] = value[:, lane:]
 
         return [functools.partial(rows, imag) for imag in range(2)]
 
@@ -399,20 +395,14 @@
     for tick in range(1, LMAX + 1):
         products = project(tick) if 1 < tick < LMAX else []
         if tick > 1:
-            products = products + combine(tick - 2, 0)
+            products = products + combine(tick - 2)
         sums = [functools.partial(mix, tick - 1, start) for start in range(0, half, step)]
         weave(products, sums)
-    for step_ in combine(LMAX - 1, 0):
+    for step_ in combine(LMAX - 1):
         step_()
-    for first in range(half // lane):
-        later = []
-        if first + 1 < half // lane:
-            later = [step_ for slot in range(LMAX) for step_ in combine(slot, first + 1)]
-        ready = []
-        for start in range(first * lane, centre, half):
-            for part in range(start // strip, (start + lane) // strip):
-                ready += [functools.partial(back, part), functools.partial(gather, part)]
-        weave(later, ready)
+    for part in range(centre // strip):
+        back(part)
+        gather(part)
     for copy in out_copies:
         copy.wait()
 

time: 26.6 us -> 26.6 us (level)
  no operation moved by 1% of the time
where the time goes in v5:
time: 26.6 us; the launch traced here: 26.4 us
  starting transfers between devices  13 us (49%)
  Pallas kernels  6.52 us (25%)
  waiting for transfers between devices  5.74 us (22%)
  between operations  0.8 us (3%)
    ppermute x8, starting transfers between devices, send(): lax.ppermute(block, 'tile', [(i, target(i)) for i in range(tile_count)])  13 us
    pallas_call x3, Pallas kernels, vmem_call(): pl.pallas_call(kernel, out_shape=tuple((jax.ShapeDtypeStruct(shape, dtype...  6.52 us
    ppermute x8, waiting for transfers between devices, send(): lax.ppermute(block, 'tile', [(i, target(i)) for i in range(tile_count)])  5.74 us
  transfers between devices with their start and end apart: 8, of which 4 were waited for; matrix products, arithmetic and copies ran while one was open for 1% of the time, Pallas kernels for 8%

profile of v5, /device:TPU:0, one launch (start us, length us, event | category | flops | bytes accessed | tf_op | source)
XLA Modules:
  0.0 26.4 jit_solution(11288771054409219844)
XLA Ops:
  0.6 4.1 %collective-permute-start.3 = (bf16[1,128,128]{2,1,0:T(8,128)(2,1)}, bf16[1,128,128]{2,1,0:T(8,128)(2,1)S(1)}, u32[]{:S(2)}, u32[]{:S(2)}) collective-permute-start(bf16[1,128,128]{2,1,0:T(8,128)(2,1)} %refs_4_.1), channel_id=1, source_target_pairs={{0,8},{1,9},{2,10},{3,11},{4,12},{5,13},{6,14},{7,15},{8,0},{9,1},... | collective-permute-start | bytes 98312 | tf_op jit(solution)/shard_map/ppermute | solution.py:480
  4.8 1.1 %shard_map.148 = (bf16[384,384]{1,0:T(8,128)(2,1)S(1)}, s32[4,16]{1,0:T(4,128)S(1)}, s32[1,16]{1,0:T(1,128)S(1)}, f32[1,16]{1,0:T(1,128)S(1)}, bf16[1,128,128]{2...) custom-call(bf16[384,384]{1,0:T(8,128)(2,1)} %bitcast.4, ...), custom_call_target="tpu_custom_call" | custom-call | tf_op jit(solution)/shard_map/pallas_call | solution.py:420
  5.9 0.1 collective-permute-start
  6.0 1.2 %collective-permute-done.3 = bf16[1,128,128]{2,1,0:T(8,128)(2,1)S(1)} collective-permute-done((bf16[1,128,128]{2,1,0:T(8,128)(2,1)}, bf16[1,128,128]{2,1,0:T(8,128)(2,1)S(1)}, u32[]{:S(2)}, u32[]{:S(2)}) %collective-permute-start.3) | collective-permute-done | bytes 32800 | tf_op jit(solution)/shard_map/ppermute | solution.py:480
  7.2 2.8 %collective-permute-start.6 = (bf16[2,128,128]{2,1,0:T(8,128)(2,1)S(1)}, bf16[2,128,128]{2,1,0:T(8,128)(2,1)S(1)}, u32[]{:S(2)}, u32[]{:S(2)}) collective-permute-start(bf16[2,128,128]{2,1,0:T(8,128)(2,1)S(1)} %get-tuple-element.21), channel_id=1, source_target_pairs={{0,6},{1,7},{2,4},{3,5},{4,2},{5,3},{6,0},{7,1},{8,14},{9,15},{10,... | collective-permute-start | bytes 196616 | tf_op jit(solution)/shard_map/ppermute | solution.py:480
  10.0 0.5 %collective-permute-start.5 = (bf16[2,128,128]{2,1,0:T(8,128)(2,1)S(1)}, bf16[2,128,128]{2,1,0:T(8,128)(2,1)S(1)}, u32[]{:S(2)}, u32[]{:S(2)}) collective-permute-start(bf16[2,128,128]{2,1,0:T(8,128)(2,1)S(1)} %get-tuple-element.21), channel_id=1, source_target_pairs={{0,4},{1,5},{2,6},{3,7},{4,0},{5,1},{6,2},{7,3},{8,12},{9,13},{10,... | collective-permute-start | bytes 196616 | tf_op jit(solution)/shard_map/ppermute | solution.py:480
  10.5 0.5 %collective-permute-start.4 = (bf16[2,128,128]{2,1,0:T(8,128)(2,1)S(1)}, bf16[2,128,128]{2,1,0:T(8,128)(2,1)S(1)}, u32[]{:S(2)}, u32[]{:S(2)}) collective-permute-start(bf16[2,128,128]{2,1,0:T(8,128)(2,1)S(1)} %get-tuple-element.21), channel_id=1, source_target_pairs={{0,2},{1,3},{2,0},{3,1},{4,6},{5,7},{6,4},{7,5},{8,10},{9,11},{10,... | collective-permute-start | bytes 196616 | tf_op jit(solution)/shard_map/ppermute | solution.py:480
  11.0 0.1 collective-permute-done.refs_3_
  11.1 0.1 broadcast_select_fusion
  11.2 3.6 %collective-permute-done.4 = bf16[2,128,128]{2,1,0:T(8,128)(2,1)S(1)} collective-permute-done((bf16[2,128,128]{2,1,0:T(8,128)(2,1)S(1)}, bf16[2,128,128]{2,1,0:T(8,128)(2,1)S(1)}, u32[]{:S(2)}, u32[]{:S(2)}) %collective-permute-start.4) | collective-permute-done | bytes 65568 | tf_op jit(solution)/shard_map/ppermute | solution.py:480
  14.8 0.0 collective-permute-done.5
  14.8 0.0 collective-permute-done.6
  14.8 0.0 copy-start.6
  14.8 0.0 copy-start.7
  14.9 0.1 collective-permute-start.7
  14.9 0.1 maximum_maximum_fusion
  15.0 0.5 %collective-permute-start.1 = (bf16[224,128]{1,0:T(8,128)(2,1)S(1)}, bf16[224,128]{1,0:T(8,128)(2,1)S(1)}, u32[]{:S(2)}, u32[]{:S(2)}) collective-permute-start(bf16[224,128]{1,0:T(8,128)(2,1)S(1)} %maximum_maximum_fusion), channel_id=1, source_target_pairs={{0,1},{1,0},{2,3},{3,2},{4,5},{5,4},{6,7},{7,6},{8,9},{9,8},{10,11... | collective-permute-start | bytes 172040 | tf_op jit(solution)/shard_map/ppermute | solution.py:480
  15.5 0.1 maximum_maximum_fusion.1
  15.6 4.5 %collective-permute-start.2 = (bf16[224,128]{1,0:T(8,128)(2,1)S(1)}, bf16[224,128]{1,0:T(8,128)(2,1)S(1)}, u32[]{:S(2)}, u32[]{:S(2)}) collective-permute-start(bf16[224,128]{1,0:T(8,128)(2,1)S(1)} %maximum_maximum_fusion.1), channel_id=1, source_target_pairs={{0,15},{1,2},{2,1},{3,4},{4,3},{5,6},{6,5},{7,8},{8,7},{9,10},{10,... | collective-permute-start | bytes 172040 | tf_op jit(solution)/shard_map/ppermute | solution.py:480
  20.1 0.0 copy-start.4
  20.1 1.0 %shard_map.149.refs_4_ = f32[4,256,256]{2,1,0:T(8,128)S(1)} custom-call(f32[1,16]{1,0:T(1,128)S(1)} %get-tuple-element.17.defocus), custom_call_target="tpu_custom_call" | custom-call | tf_op jit(solution)/shard_map/pallas_call | solution.py:420
  21.1 0.0 collective-permute-done.1.refs_1_
  21.1 0.9 %collective-permute-done.2.refs_2_ = bf16[224,128]{1,0:T(8,128)(2,1)S(1)} collective-permute-done((bf16[224,128]{1,0:T(8,128)(2,1)S(1)}, bf16[224,128]{1,0:T(8,128)(2,1)S(1)}, u32[]{:S(2)}, u32[]{:S(2)}) %collective-permute-start.2) | collective-permute-done | bytes 57376 | tf_op jit(solution)/shard_map/ppermute | solution.py:480
  22.0 4.4 %shard_map.150 = (f32[1,384,384]{2,1,0:T(8,128)}, f32[1,384,384]{2,1,0:T(8,128)}, f32[1,384,384]{2,1,0:T(8,128)}) custom-call(s32[4,16]{1,0:T(4,128)S(1)} %get-tuple-element.11.orients, s32[1,16]{1,0:T(1,128)S(1)} %get-tuple-element.12.lengths, bf16[384,384]{1,0:T(8,128)(2,1)S(1)} %get-tuple-element.13.refs_0_, ...), custom_call_target="tpu_custom_call" | custom-call | tf_op jit(solution)/shard_map/pallas_call | solution.py:420
  (20 shorter events, 0.1 us)
Async XLA Ops:
  0.6 6.6 %collective-permute-start.3 = (bf16[1,128,128]{2,1,0:T(8,128)(2,1)}, bf16[1,128,128]{2,1,0:T(8,128)(2,1)S(1)}, u32[]{:S(2)}, u32[]{:S(2)}) collective-permute-start(bf16[1,128,128]{2,1,0:T(8,128)(2,1)} %refs_4_.1), channel_id=1, source_target_pairs={{0,8},{1,9},{2,10},{3,11},{4,12},{5,13},{6,14},{7,15},{8,0},{9,1},... | collective-permute-start | bytes 98312 | tf_op jit(solution)/shard_map/ppermute | solution.py:480
  5.9 5.2 %collective-permute-start = (bf16[64,384]{1,0:T(8,128)(2,1)S(1)}, bf16[64,384]{1,0:T(8,128)(2,1)S(1)}, u32[]{:S(2)}, u32[]{:S(2)}) collective-permute-start(bf16[64,384]{1,0:T(8,128)(2,1)S(1)} %get-tuple-element.15), channel_id=1, source_target_pairs={{0,8},{1,9},{2,10},{3,11},{4,12},{5,13},{6,14},{7,15},{8,0},{9,1},... | collective-permute-start | bytes 147464 | tf_op jit(solution)/shard_map/ppermute | solution.py:480
  7.2 7.6 %collective-permute-start.6 = (bf16[2,128,128]{2,1,0:T(8,128)(2,1)S(1)}, bf16[2,128,128]{2,1,0:T(8,128)(2,1)S(1)}, u32[]{:S(2)}, u32[]{:S(2)}) collective-permute-start(bf16[2,128,128]{2,1,0:T(8,128)(2,1)S(1)} %get-tuple-element.21), channel_id=1, source_target_pairs={{0,6},{1,7},{2,4},{3,5},{4,2},{5,3},{6,0},{7,1},{8,14},{9,15},{10,... | collective-permute-start | bytes 196616 | tf_op jit(solution)/shard_map/ppermute | solution.py:480
  10.0 4.8 %collective-permute-start.5 = (bf16[2,128,128]{2,1,0:T(8,128)(2,1)S(1)}, bf16[2,128,128]{2,1,0:T(8,128)(2,1)S(1)}, u32[]{:S(2)}, u32[]{:S(2)}) collective-permute-start(bf16[2,128,128]{2,1,0:T(8,128)(2,1)S(1)} %get-tuple-element.21), channel_id=1, source_target_pairs={{0,4},{1,5},{2,6},{3,7},{4,0},{5,1},{6,2},{7,3},{8,12},{9,13},{10,... | collective-permute-start | bytes 196616 | tf_op jit(solution)/shard_map/ppermute | solution.py:480
  10.5 4.3 %collective-permute-start.4 = (bf16[2,128,128]{2,1,0:T(8,128)(2,1)S(1)}, bf16[2,128,128]{2,1,0:T(8,128)(2,1)S(1)}, u32[]{:S(2)}, u32[]{:S(2)}) collective-permute-start(bf16[2,128,128]{2,1,0:T(8,128)(2,1)S(1)} %get-tuple-element.21), channel_id=1, source_target_pairs={{0,2},{1,3},{2,0},{3,1},{4,6},{5,7},{6,4},{7,5},{8,10},{9,11},{10,... | collective-permute-start | bytes 196616 | tf_op jit(solution)/shard_map/ppermute | solution.py:480
  14.8 7.1 %copy-start.6 = (bf16[256,256]{1,0:T(8,128)(2,1)S(1)}, bf16[256,256]{1,0:T(8,128)(2,1)}, u32[]{:S(2)}) copy-start(bf16[256,256]{1,0:T(8,128)(2,1)} %constant.35.clone.refs_8_) | copy-start | bytes 393220
  14.8 7.1 %copy-start.7 = (bf16[256,256]{1,0:T(8,128)(2,1)S(1)}, bf16[256,256]{1,0:T(8,128)(2,1)}, u32[]{:S(2)}) copy-start(bf16[256,256]{1,0:T(8,128)(2,1)} %constant.34.clone.refs_7_) | copy-start | bytes 393220
  14.9 7.1 %collective-permute-start.7 = (bf16[8,128,128]{2,1,0:T(8,128)(2,1)S(1)}, bf16[8,128,128]{2,1,0:T(8,128)(2,1)S(1)}, u32[]{:S(2)}, u32[]{:S(2)}) collective-permute-start(bf16[8,128,128]{2,1,0:T(8,128)(2,1)S(1)} %constant_dynamic-update-slice_fusion.2.refs_5_), channel_id=1, source_target_pairs={{0,1},{1,0},{2,3},{3,2},{4,5},{5,4},{6,7},{7,6},{8,9},{9,8},{10,11... | collective-permute-start | bytes 786440 | tf_op jit(solution)/shard_map/ppermute | solution.py:480
  15.0 6.0 %collective-permute-start.1 = (bf16[224,128]{1,0:T(8,128)(2,1)S(1)}, bf16[224,128]{1,0:T(8,128)(2,1)S(1)}, u32[]{:S(2)}, u32[]{:S(2)}) collective-permute-start(bf16[224,128]{1,0:T(8,128)(2,1)S(1)} %maximum_maximum_fusion), channel_id=1, source_target_pairs={{0,1},{1,0},{2,3},{3,2},{4,5},{5,4},{6,7},{7,6},{8,9},{9,8},{10,11... | collective-permute-start | bytes 172040 | tf_op jit(solution)/shard_map/ppermute | solution.py:480
  15.5 6.4 %copy-start.5 = (bf16[256,256]{1,0:T(8,128)(2,1)S(1)}, bf16[256,256]{1,0:T(8,128)(2,1)}, u32[]{:S(2)}) copy-start(bf16[256,256]{1,0:T(8,128)(2,1)} %constant.36.clone.refs_9_) | copy-start | bytes 393220
  15.6 6.3 %collective-permute-start.2 = (bf16[224,128]{1,0:T(8,128)(2,1)S(1)}, bf16[224,128]{1,0:T(8,128)(2,1)S(1)}, u32[]{:S(2)}, u32[]{:S(2)}) collective-permute-start(bf16[224,128]{1,0:T(8,128)(2,1)S(1)} %maximum_maximum_fusion.1), channel_id=1, source_target_pairs={{0,15},{1,2},{2,1},{3,4},{4,3},{5,6},{6,5},{7,8},{8,7},{9,10},{10,... | collective-permute-start | bytes 172040 | tf_op jit(solution)/shard_map/ppermute | solution.py:480
  20.1 1.9 %copy-start = (bf16[1024,256]{1,0:T(8,128)(2,1)S(1)}, bf16[1024,256]{1,0:T(8,128)(2,1)}, u32[]{:S(2)}) copy-start(bf16[1024,256]{1,0:T(8,128)(2,1)} %constant.41.clone.refs_14_) | copy-start | bytes 1572868
  20.1 1.9 %copy-start.1 = (bf16[128,512]{1,0:T(8,128)(2,1)S(1)}, bf16[128,512]{1,0:T(8,128)(2,1)}, u32[]{:S(2)}) copy-start(bf16[128,512]{1,0:T(8,128)(2,1)} %constant.40.clone.refs_13_) | copy-start | bytes 393220
  20.1 1.9 %copy-start.2 = (bf16[256,256]{1,0:T(8,128)(2,1)S(1)}, bf16[256,256]{1,0:T(8,128)(2,1)}, u32[]{:S(2)}) copy-start(bf16[256,256]{1,0:T(8,128)(2,1)} %constant.39.clone.refs_12_) | copy-start | bytes 393220
  20.1 1.9 %copy-start.3 = (bf16[256,256]{1,0:T(8,128)(2,1)S(1)}, bf16[256,256]{1,0:T(8,128)(2,1)}, u32[]{:S(2)}) copy-start(bf16[256,256]{1,0:T(8,128)(2,1)} %constant.38.clone.refs_11_) | copy-start | bytes 393220
  20.1 1.9 %copy-start.4 = (bf16[256,256]{1,0:T(8,128)(2,1)S(1)}, bf16[256,256]{1,0:T(8,128)(2,1)}, u32[]{:S(2)}) copy-start(bf16[256,256]{1,0:T(8,128)(2,1)} %constant.37.clone.refs_10_) | copy-start | bytes 393220

commit v6 on v4

--- a/solution.py
+++ b/solution.py
@@ -242,31 +242,18 @@
         step()
 
 
-def match_kernel(paired, orients, lengths, *refs):
-    count_in = 4 if paired else 3
-    pieces, (weight_ref, near_ref, far_ref) = refs[:count_in], refs[count_in : count_in + 3]
-    fwd_e, fwd_o, fwd_et, fwd_ot, inv_e, inv_o, temp_rows, temp_cols = refs[count_in + 3 : count_in + 11]
-    snr_ref, mean_ref, var_ref = refs[count_in + 11 : count_in + 14]
-    filt, uv, waves, proj, mixed, combos, out_buf, out_sem = refs[count_in + 14 :]
+def rows_kernel(orients, lengths, near_ref, far_ref, temp_rows, waves, edges):
     me = lax.axis_index("tile")
-    half = filt.shape[1]
+    half = waves.shape[3]
     lane = half // 2
-    centre = out_buf.shape[1]
     box = near_ref.shape[1]
-    strip = combos.shape[3] // LMAX
     tile_count = lax.axis_size("tile")
     distances = flips(tile_count)
     held = near_ref.shape[0] // (tile_count // 2)
     count = lengths[0, me]
     bf16, f32 = jnp.bfloat16, jnp.float32
-    step = 16
-    col_first = lax.broadcasted_iota(jnp.int32, (step, half), 1) == 0
-    row_first = lax.broadcasted_iota(jnp.int32, (step, half), 0) == 0
-    corner = col_first & row_first
-    thin_first = col_first.astype(f32).astype(bf16) > 0
     sign = 1.0 - 2.0 * (lax.broadcasted_iota(jnp.int32, (box, lane), 0) % 2).astype(f32)
     box_col = lax.broadcasted_iota(jnp.int32, (box, lane), 1) == 0
-    edges = {}
 
     def chosen(slot):
         orient = orients[slot, me]
@@ -279,21 +266,40 @@
             at = at + (lax.div(apart, distance) & 1) * (held << k)
         return jnp.where(apart & 1 == 1, far_ref[at], near_ref[at])
 
-    def rows_first():
-        stacked = jnp.concatenate([chosen(slot) for slot in range(LMAX)], axis=0)
-        first_u, rest_u = dot(stacked, temp_rows[:, :lane]), dot(stacked, temp_rows[:, lane:half])
-        first_v, rest_v = dot(stacked, temp_rows[:, half : half + lane]), dot(stacked, temp_rows[:, half + lane :])
-        for slot in range(LMAX):
-            rows = slice(slot * box, (slot + 1) * box)
-            u, v = first_u[rows], first_v[rows]
-            row_edge = -jnp.sum(u * sign, axis=0, keepdims=True)
-            col_edge = jnp.sum(v, axis=0, keepdims=True)
-            edges[slot] = (beside(row_edge, row_edge), beside(col_edge, col_edge))
-            v_part = beside(jnp.where(box_col, 0.0, v), rest_v[rows]).astype(bf16)
-            waves[slot, 0, :box] = beside(u, rest_u[rows]).astype(bf16)
-            waves[slot, 1, :box] = beside(jnp.where(box_col, v, u), rest_u[rows]).astype(bf16)
-            waves[slot, 0, box:] = v_part
-            waves[slot, 1, box:] = v_part
+    stacked = jnp.concatenate([chosen(slot) for slot in range(LMAX)], axis=0)
+    first_u, rest_u = dot(stacked, temp_rows[:, :lane]), dot(stacked, temp_rows[:, lane:half])
+    first_v, rest_v = dot(stacked, temp_rows[:, half : half + lane]), dot(stacked, temp_rows[:, half + lane :])
+    for slot in range(LMAX):
+        rows = slice(slot * box, (slot + 1) * box)
+        u, v = first_u[rows], first_v[rows]
+        row_edge = -jnp.sum(u * sign, axis=0, keepdims=True)
+        col_edge = jnp.sum(v, axis=0, keepdims=True)
+        edges[slot, :1], edges[slot, 1:2] = beside(row_edge, row_edge), beside(col_edge, col_edge)
+        v_part = beside(jnp.where(box_col, 0.0, v), rest_v[rows]).astype(bf16)
+        waves[slot, 0, :box] = beside(u, rest_u[rows]).astype(bf16)
+        waves[slot, 1, :box] = beside(jnp.where(box_col, v, u), rest_u[rows]).astype(bf16)
+        waves[slot, 0, box:] = v_part
+        waves[slot, 1, box:] = v_part
+
+
+def match_kernel(paired, lengths, *refs):
+    count_in = 4 if paired else 3
+    pieces, (weight_ref, waves, edges) = refs[:count_in], refs[count_in : count_in + 3]
+    fwd_e, fwd_o, fwd_et, fwd_ot, inv_e, inv_o, temp_cols = refs[count_in + 3 : count_in + 10]
+    snr_ref, mean_ref, var_ref = refs[count_in + 10 : count_in + 13]
+    filt, uv, proj, mixed, combos, out_buf, out_sem = refs[count_in + 13 :]
+    me = lax.axis_index("tile")
+    half = filt.shape[1]
+    lane = half // 2
+    centre = out_buf.shape[1]
+    strip = combos.shape[3] // LMAX
+    count = lengths[0, me]
+    bf16, f32 = jnp.bfloat16, jnp.float32
+    step = 16
+    col_first = lax.broadcasted_iota(jnp.int32, (step, half), 1) == 0
+    row_first = lax.broadcasted_iota(jnp.int32, (step, half), 0) == 0
+    corner = col_first & row_first
+    thin_first = col_first.astype(f32).astype(bf16) > 0
 
     def project(slot):
         def cols(k):
@@ -305,7 +311,7 @@
     def mix_first(slot, fs, ps):
         fpr, fpi, fmr, fmi = (f.astype(f32) for f in fs)
         ppr, ppi, pmr, pmi = (p.astype(f32) for p in ps)
-        row_edge, col_edge = edges[slot]
+        row_edge, col_edge = edges[slot, :1], edges[slot, 1:2]
         ppi = jnp.where(corner, row_edge, ppi)
         pmi = jnp.where(corner, pmr, pmi)
         pmr = jnp.where(corner, col_edge, pmr)
@@ -395,7 +401,7 @@
             out_copies.append(copy)
 
     tile = tile_steps(paired, pieces, weight_ref, (fwd_e, fwd_o, fwd_et, fwd_ot), filt, uv)
-    weave(tile, [rows_first] + project(0) + project(1))
+    weave(tile, project(0) + project(1))
     for tick in range(1, LMAX + 1):
         products = project(tick) if 1 < tick < LMAX else []
         if tick > 1:
@@ -451,25 +457,30 @@
     return vmem_call(early_kernel, (defocus,), (((4, half, half), jnp.float32),), [], 1, 8)[0]
 
 
-def match(orient_list, lengths, pieces, weights, near, far, tables):
+def rows(orient_list, lengths, near, far, tables, half):
+    box = near.shape[1]
+    outs = (((LMAX, 2, 2 * box, half), jnp.bfloat16), ((LMAX, 8, half), jnp.float32))
+    return vmem_call(rows_kernel, (orient_list, lengths, near, far, tables[6]), outs, [], 2, 8)
+
+
+def match(lengths, pieces, weights, waves, edges, tables):
     centre, half = pieces[0].shape[0], weights.shape[1]
     lane, extent = half // 2, 2 * half
     strip = lane // 2
     out = ((1, centre, centre), jnp.float32)
     kernel = functools.partial(match_kernel, len(pieces) == 4)
     return vmem_call(
-        kernel, (orient_list, lengths, *pieces, weights, near, far, *tables), (out, out, out),
+        kernel, (lengths, *pieces, weights, waves, edges, *tables[:6], tables[7]), (out, out, out),
         [
             pltpu.VMEM((4, half, half), jnp.bfloat16),
             pltpu.VMEM((extent, extent), jnp.float32),
-            pltpu.VMEM((LMAX, 2, 2 * near.shape[1], half), jnp.bfloat16),
             pltpu.VMEM((2, 2 * extent, half), jnp.bfloat16),
             pltpu.VMEM((LMAX, 2, 2, half, half), jnp.bfloat16),
             pltpu.VMEM((2, 2, centre // strip, LMAX * strip, lane), jnp.bfloat16),
             pltpu.VMEM((3, centre, centre), jnp.float32),
             pltpu.SemaphoreType.DMA((3, centre // strip)),
         ],
-        2, 24, pl.ANY,
+        1, 24, pl.ANY,
     )
 
 
@@ -533,13 +544,14 @@
         above = arrive(wide[centre - margin :], -GRID)
         below = jnp.where(tile_row == tile_rows - 1, jnp.zeros_like(below), below)
         above = jnp.where(tile_row == 0, jnp.zeros_like(above), above)
-        rows = jnp.concatenate([below, above], axis=0)
+        rims = jnp.concatenate([below, above], axis=0)
         near = templates
         for distance in flips(tile_count)[:-1]:
             near = jnp.concatenate([near, send(near, lambda i, d=distance: i ^ d)], axis=0)
         far = send(near, lambda i: i ^ 1)
-        pieces = (centre_block, cols, rows)
-    return match(orients, counts, pieces, weights, near, far, tables)
+        pieces = (centre_block, cols, rims)
+    waves, edges = rows(orients, counts, near, far, tables, extent // 2)
+    return match(counts, pieces, weights, waves, edges, tables)
 
 
 def solution(mesh):

time: 26.6 us -> 26.6 us (level)
  waiting for transfers between devices: 5.74 us -> 4.89 us
  Pallas kernels: 6.56 us -> 7.25 us
    ppermute x8, waiting for transfers between devices: 5.74 us -> 4.89 us  [send(): lax.ppermute(block, 'tile', [(i, target(i)) for i in range(tile_count)])]
    pallas_call x3 -> x4, Pallas kernels: 6.56 us -> 7.25 us  [vmem_call(): pl.pallas_call(kernel, out_shape=tuple((jax.ShapeDtypeStruct(shape, dtype...]
  transfers between devices with their start and end apart: 8 -> 8, of which waited for: 4 -> 3; matrix products, arithmetic and copies ran while one was open for 1% -> 1% of each run, Pallas kernels for 8% -> 11%
where the time goes in v6:
time: 26.6 us; the launch traced here: 26.4 us
  starting transfers between devices  13 us (49%)
  Pallas kernels  7.25 us (27%)
  waiting for transfers between devices  4.89 us (18%)
  between operations  0.82 us (3%)
    ppermute x8, starting transfers between devices, send(): lax.ppermute(block, 'tile', [(i, target(i)) for i in range(tile_count)])  13 us
    pallas_call x4, Pallas kernels, vmem_call(): pl.pallas_call(kernel, out_shape=tuple((jax.ShapeDtypeStruct(shape, dtype...  7.25 us
    ppermute x8, waiting for transfers between devices, send(): lax.ppermute(block, 'tile', [(i, target(i)) for i in range(tile_count)])  4.89 us
  transfers between devices with their start and end apart: 8, of which 3 were waited for; matrix products, arithmetic and copies ran while one was open for 1% of the time, Pallas kernels for 11%

profile of v6, /device:TPU:0, one launch (start us, length us, event | category | flops | bytes accessed | tf_op | source)
XLA Modules:
  0.0 26.4 jit_solution(3067594276842932810)
XLA Ops:
  0.6 4.1 %collective-permute-start.3 = (bf16[1,128,128]{2,1,0:T(8,128)(2,1)}, bf16[1,128,128]{2,1,0:T(8,128)(2,1)S(1)}, u32[]{:S(2)}, u32[]{:S(2)}) collective-permute-start(bf16[1,128,128]{2,1,0:T(8,128)(2,1)} %refs_4_.1), channel_id=1, source_target_pairs={{0,8},{1,9},{2,10},{3,11},{4,12},{5,13},{6,14},{7,15},{8,0},{9,1},... | collective-permute-start | bytes 98312 | tf_op jit(solution)/shard_map/ppermute | solution.py:501
  4.8 1.1 %shard_map.148 = (bf16[384,384]{1,0:T(8,128)(2,1)S(1)}, s32[4,16]{1,0:T(4,128)S(1)}, s32[1,16]{1,0:T(1,128)S(1)}, f32[1,16]{1,0:T(1,128)S(1)}, bf16[1,128,128]{2...) custom-call(bf16[384,384]{1,0:T(8,128)(2,1)} %bitcast.4, ...), custom_call_target="tpu_custom_call" | custom-call | tf_op jit(solution)/shard_map/pallas_call | solution.py:436
  5.9 0.1 collective-permute-start
  6.0 1.2 %collective-permute-done.3 = bf16[1,128,128]{2,1,0:T(8,128)(2,1)S(1)} collective-permute-done((bf16[1,128,128]{2,1,0:T(8,128)(2,1)}, bf16[1,128,128]{2,1,0:T(8,128)(2,1)S(1)}, u32[]{:S(2)}, u32[]{:S(2)}) %collective-permute-start.3) | collective-permute-done | bytes 32800 | tf_op jit(solution)/shard_map/ppermute | solution.py:501
  7.2 2.8 %collective-permute-start.6 = (bf16[2,128,128]{2,1,0:T(8,128)(2,1)S(1)}, bf16[2,128,128]{2,1,0:T(8,128)(2,1)S(1)}, u32[]{:S(2)}, u32[]{:S(2)}) collective-permute-start(bf16[2,128,128]{2,1,0:T(8,128)(2,1)S(1)} %get-tuple-element.25), channel_id=1, source_target_pairs={{0,6},{1,7},{2,4},{3,5},{4,2},{5,3},{6,0},{7,1},{8,14},{9,15},{10,... | collective-permute-start | bytes 196616 | tf_op jit(solution)/shard_map/ppermute | solution.py:501
  10.0 0.5 %collective-permute-start.5 = (bf16[2,128,128]{2,1,0:T(8,128)(2,1)S(1)}, bf16[2,128,128]{2,1,0:T(8,128)(2,1)S(1)}, u32[]{:S(2)}, u32[]{:S(2)}) collective-permute-start(bf16[2,128,128]{2,1,0:T(8,128)(2,1)S(1)} %get-tuple-element.25), channel_id=1, source_target_pairs={{0,4},{1,5},{2,6},{3,7},{4,0},{5,1},{6,2},{7,3},{8,12},{9,13},{10,... | collective-permute-start | bytes 196616 | tf_op jit(solution)/shard_map/ppermute | solution.py:501
  10.5 0.5 %collective-permute-start.4 = (bf16[2,128,128]{2,1,0:T(8,128)(2,1)S(1)}, bf16[2,128,128]{2,1,0:T(8,128)(2,1)S(1)}, u32[]{:S(2)}, u32[]{:S(2)}) collective-permute-start(bf16[2,128,128]{2,1,0:T(8,128)(2,1)S(1)} %get-tuple-element.25), channel_id=1, source_target_pairs={{0,2},{1,3},{2,0},{3,1},{4,6},{5,7},{6,4},{7,5},{8,10},{9,11},{10,... | collective-permute-start | bytes 196616 | tf_op jit(solution)/shard_map/ppermute | solution.py:501
  11.0 0.1 collective-permute-done.refs_3_
  11.1 0.1 broadcast_select_fusion
  11.2 3.6 %collective-permute-done.4 = bf16[2,128,128]{2,1,0:T(8,128)(2,1)S(1)} collective-permute-done((bf16[2,128,128]{2,1,0:T(8,128)(2,1)S(1)}, bf16[2,128,128]{2,1,0:T(8,128)(2,1)S(1)}, u32[]{:S(2)}, u32[]{:S(2)}) %collective-permute-start.4) | collective-permute-done | bytes 65568 | tf_op jit(solution)/shard_map/ppermute | solution.py:501
  14.8 0.1 collective-permute-start.7
  14.9 0.1 maximum_maximum_fusion
  15.0 0.5 %collective-permute-start.1 = (bf16[224,128]{1,0:T(8,128)(2,1)S(1)}, bf16[224,128]{1,0:T(8,128)(2,1)S(1)}, u32[]{:S(2)}, u32[]{:S(2)}) collective-permute-start(bf16[224,128]{1,0:T(8,128)(2,1)S(1)} %maximum_maximum_fusion), channel_id=1, source_target_pairs={{0,1},{1,0},{2,3},{3,2},{4,5},{5,4},{6,7},{7,6},{8,9},{9,8},{10,11... | collective-permute-start | bytes 172040 | tf_op jit(solution)/shard_map/ppermute | solution.py:501
  15.5 0.1 maximum_maximum_fusion.1
  15.6 4.5 %collective-permute-start.2 = (bf16[224,128]{1,0:T(8,128)(2,1)S(1)}, bf16[224,128]{1,0:T(8,128)(2,1)S(1)}, u32[]{:S(2)}, u32[]{:S(2)}) collective-permute-start(bf16[224,128]{1,0:T(8,128)(2,1)S(1)} %maximum_maximum_fusion.1), channel_id=1, source_target_pairs={{0,15},{1,2},{2,1},{3,4},{4,3},{5,6},{6,5},{7,8},{8,7},{9,10},{10,... | collective-permute-start | bytes 172040 | tf_op jit(solution)/shard_map/ppermute | solution.py:501
  20.0 0.0 copy-start.5
  20.0 0.0 copy-start.6
  20.1 1.0 %shard_map.149.refs_4_ = f32[4,256,256]{2,1,0:T(8,128)S(1)} custom-call(f32[1,16]{1,0:T(1,128)S(1)} %get-tuple-element.18.defocus), custom_call_target="tpu_custom_call" | custom-call | tf_op jit(solution)/shard_map/pallas_call | solution.py:436
  21.0 0.0 copy-start
  21.1 0.0 copy-start.1
  21.1 0.9 %shard_map.150 = (bf16[4,2,256,256]{3,2,1,0:T(8,128)(2,1)S(1)}, f32[4,8,256]{2,1,0:T(8,128)S(1)}) custom-call(s32[4,16]{1,0:T(4,128)S(1)} %get-tuple-element.19.orients, s32[1,16]{1,0:T(1,128)S(1)} %get-tuple-element.13.lengths, bf16[8,128,128]{2,1,0:T(8,128)(2,1)S(1)} %constant_dynamic-update-slice_fusion.2.near_ref, ...), custom_call_target="tpu_custom_call" | custom-call | tf_op jit(solution)/shard_map/pallas_call | solution.py:436
  22.0 0.1 copy-done
  22.1 0.0 copy-done.1
  22.1 4.3 %shard_map.151 = (f32[1,384,384]{2,1,0:T(8,128)}, f32[1,384,384]{2,1,0:T(8,128)}, f32[1,384,384]{2,1,0:T(8,128)}) custom-call(s32[1,16]{1,0:T(1,128)S(1)} %get-tuple-element.13.lengths, bf16[384,384]{1,0:T(8,128)(2,1)S(1)} %get-tuple-element.14.refs_0_, bf16[224,128]{1,0:T(8,128)(2,1)S(1)} %collective-permute-done.1.refs_1_, ...), custom_call_target="tpu_custom_call" | custom-call | tf_op jit(solution)/shard_map/pallas_call | solution.py:436
  (21 shorter events, 0.1 us)
Async XLA Ops:
  0.6 6.6 %collective-permute-start.3 = (bf16[1,128,128]{2,1,0:T(8,128)(2,1)}, bf16[1,128,128]{2,1,0:T(8,128)(2,1)S(1)}, u32[]{:S(2)}, u32[]{:S(2)}) collective-permute-start(bf16[1,128,128]{2,1,0:T(8,128)(2,1)} %refs_4_.1), channel_id=1, source_target_pairs={{0,8},{1,9},{2,10},{3,11},{4,12},{5,13},{6,14},{7,15},{8,0},{9,1},... | collective-permute-start | bytes 98312 | tf_op jit(solution)/shard_map/ppermute | solution.py:501
  5.9 5.2 %collective-permute-start = (bf16[64,384]{1,0:T(8,128)(2,1)S(1)}, bf16[64,384]{1,0:T(8,128)(2,1)S(1)}, u32[]{:S(2)}, u32[]{:S(2)}) collective-permute-start(bf16[64,384]{1,0:T(8,128)(2,1)S(1)} %get-tuple-element.16), channel_id=1, source_target_pairs={{0,8},{1,9},{2,10},{3,11},{4,12},{5,13},{6,14},{7,15},{8,0},{9,1},... | collective-permute-start | bytes 147464 | tf_op jit(solution)/shard_map/ppermute | solution.py:501
  7.2 7.6 %collective-permute-start.6 = (bf16[2,128,128]{2,1,0:T(8,128)(2,1)S(1)}, bf16[2,128,128]{2,1,0:T(8,128)(2,1)S(1)}, u32[]{:S(2)}, u32[]{:S(2)}) collective-permute-start(bf16[2,128,128]{2,1,0:T(8,128)(2,1)S(1)} %get-tuple-element.25), channel_id=1, source_target_pairs={{0,6},{1,7},{2,4},{3,5},{4,2},{5,3},{6,0},{7,1},{8,14},{9,15},{10,... | collective-permute-start | bytes 196616 | tf_op jit(solution)/shard_map/ppermute | solution.py:501
  10.0 4.8 %collective-permute-start.5 = (bf16[2,128,128]{2,1,0:T(8,128)(2,1)S(1)}, bf16[2,128,128]{2,1,0:T(8,128)(2,1)S(1)}, u32[]{:S(2)}, u32[]{:S(2)}) collective-permute-start(bf16[2,128,128]{2,1,0:T(8,128)(2,1)S(1)} %get-tuple-element.25), channel_id=1, source_target_pairs={{0,4},{1,5},{2,6},{3,7},{4,0},{5,1},{6,2},{7,3},{8,12},{9,13},{10,... | collective-permute-start | bytes 196616 | tf_op jit(solution)/shard_map/ppermute | solution.py:501
  10.5 4.3 %collective-permute-start.4 = (bf16[2,128,128]{2,1,0:T(8,128)(2,1)S(1)}, bf16[2,128,128]{2,1,0:T(8,128)(2,1)S(1)}, u32[]{:S(2)}, u32[]{:S(2)}) collective-permute-start(bf16[2,128,128]{2,1,0:T(8,128)(2,1)S(1)} %get-tuple-element.25), channel_id=1, source_target_pairs={{0,2},{1,3},{2,0},{3,1},{4,6},{5,7},{6,4},{7,5},{8,10},{9,11},{10,... | collective-permute-start | bytes 196616 | tf_op jit(solution)/shard_map/ppermute | solution.py:501
  14.8 6.2 %collective-permute-start.7 = (bf16[8,128,128]{2,1,0:T(8,128)(2,1)S(1)}, bf16[8,128,128]{2,1,0:T(8,128)(2,1)S(1)}, u32[]{:S(2)}, u32[]{:S(2)}) collective-permute-start(bf16[8,128,128]{2,1,0:T(8,128)(2,1)S(1)} %constant_dynamic-update-slice_fusion.2.near_ref), channel_id=1, source_target_pairs={{0,1},{1,0},{2,3},{3,2},{4,5},{5,4},{6,7},{7,6},{8,9},{9,8},{10,11... | collective-permute-start | bytes 786440 | tf_op jit(solution)/shard_map/ppermute | solution.py:501
  15.0 7.0 %collective-permute-start.1 = (bf16[224,128]{1,0:T(8,128)(2,1)S(1)}, bf16[224,128]{1,0:T(8,128)(2,1)S(1)}, u32[]{:S(2)}, u32[]{:S(2)}) collective-permute-start(bf16[224,128]{1,0:T(8,128)(2,1)S(1)} %maximum_maximum_fusion), channel_id=1, source_target_pairs={{0,1},{1,0},{2,3},{3,2},{4,5},{5,4},{6,7},{7,6},{8,9},{9,8},{10,11... | collective-permute-start | bytes 172040 | tf_op jit(solution)/shard_map/ppermute | solution.py:501
  15.6 6.4 %collective-permute-start.2 = (bf16[224,128]{1,0:T(8,128)(2,1)S(1)}, bf16[224,128]{1,0:T(8,128)(2,1)S(1)}, u32[]{:S(2)}, u32[]{:S(2)}) collective-permute-start(bf16[224,128]{1,0:T(8,128)(2,1)S(1)} %maximum_maximum_fusion.1), channel_id=1, source_target_pairs={{0,15},{1,2},{2,1},{3,4},{4,3},{5,6},{6,5},{7,8},{8,7},{9,10},{10,... | collective-permute-start | bytes 172040 | tf_op jit(solution)/shard_map/ppermute | solution.py:501
  20.0 1.0 %copy-start.7 = (bf16[128,512]{1,0:T(8,128)(2,1)S(1)}, bf16[128,512]{1,0:T(8,128)(2,1)}, u32[]{:S(2)}) copy-start(bf16[128,512]{1,0:T(8,128)(2,1)} %constant.40.clone.temp_rows) | copy-start | bytes 393220
  20.0 2.0 %copy-start.2 = (bf16[256,256]{1,0:T(8,128)(2,1)S(1)}, bf16[256,256]{1,0:T(8,128)(2,1)}, u32[]{:S(2)}) copy-start(bf16[256,256]{1,0:T(8,128)(2,1)} %constant.38.clone.refs_11_) | copy-start | bytes 393220
  20.0 2.0 %copy-start.3 = (bf16[256,256]{1,0:T(8,128)(2,1)S(1)}, bf16[256,256]{1,0:T(8,128)(2,1)}, u32[]{:S(2)}) copy-start(bf16[256,256]{1,0:T(8,128)(2,1)} %constant.37.clone.refs_10_) | copy-start | bytes 393220
  20.0 2.0 %copy-start.4 = (bf16[256,256]{1,0:T(8,128)(2,1)S(1)}, bf16[256,256]{1,0:T(8,128)(2,1)}, u32[]{:S(2)}) copy-start(bf16[256,256]{1,0:T(8,128)(2,1)} %constant.36.clone.refs_9_) | copy-start | bytes 393220
  20.0 2.0 %copy-start.5 = (bf16[256,256]{1,0:T(8,128)(2,1)S(1)}, bf16[256,256]{1,0:T(8,128)(2,1)}, u32[]{:S(2)}) copy-start(bf16[256,256]{1,0:T(8,128)(2,1)} %constant.35.clone.refs_8_) | copy-start | bytes 393220
  20.0 2.0 %copy-start.6 = (bf16[256,256]{1,0:T(8,128)(2,1)S(1)}, bf16[256,256]{1,0:T(8,128)(2,1)}, u32[]{:S(2)}) copy-start(bf16[256,256]{1,0:T(8,128)(2,1)} %constant.34.clone.refs_7_) | copy-start | bytes 393220
  21.0 1.1 %copy-start = (bf16[1024,256]{1,0:T(8,128)(2,1)S(1)}, bf16[1024,256]{1,0:T(8,128)(2,1)}, u32[]{:S(2)}) copy-start(bf16[1024,256]{1,0:T(8,128)(2,1)} %constant.41.clone.refs_13_) | copy-start | bytes 1572868
  21.1 1.1 %copy-start.1 = (bf16[256,256]{1,0:T(8,128)(2,1)S(1)}, bf16[256,256]{1,0:T(8,128)(2,1)}, u32[]{:S(2)}) copy-start(bf16[256,256]{1,0:T(8,128)(2,1)} %constant.39.clone.refs_12_) | copy-start | bytes 393220
